TPU v7x, 32 devices: a whole 2x2x4 slice. The times are simulated.
32 devices in a mesh: dp: 8 (over y, x, core), tensor: 4 (over z).
Axes of the slice: x: 2, y: 2, z: 4, core: 2. Of those that a mesh axis runs over, the one named last changes fastest.
Arguments:
- inputs: bfloat16 [8, 2048, 768], P('dp', 'tensor'), may hold values from -6 to 6
- encoder_out: bfloat16 [8, 1024, 768], P('dp', 'tensor'), may hold values from -6 to 6
- block_ids: int32 [8, 8], P('dp'), may hold values from 0 to 4, never falling along the last dimension, each value on 1 to 3 neighbouring positions
- out_grad: bfloat16 [8, 2048, 768], P('dp', 'tensor'), may hold values from -6 to 6
- in_weight: float32 [6, 768, 768], P(None, 'dp', 'tensor'), may hold values from -0.21875 to 0.21875
- out_weight: float32 [2, 768, 768], P(None, 'tensor', 'dp'), may hold values from -4.8 to 4.8
- up_weight: float32 [768, 3072], P('dp', 'tensor'), may hold values from -0.21875 to 0.21875
- down_weight: float32 [3072, 768], P('tensor', 'dp'), may hold values from -0.109375 to 0.109375
- vectors: float32 [10, 768], replicated, may hold values from -0.24 to 0.24
- norm_gains: float32 [3, 768], replicated, may hold values from 0.25 to 1.75
- up_bias: float32 [3072], replicated, may hold values from -1.8 to 1.8
Outputs:
- layer_out: bfloat16 [8, 2048, 768], P('dp', 'tensor')
- grad_input: float32 [8, 2048, 768], P('dp', 'tensor')
- grad_encoder: float32 [8, 1024, 768], P('dp', 'tensor')
- grad_in_weight: float32 [6, 768, 768], P(None, 'dp', 'tensor')
- grad_out_weight: float32 [2, 768, 768], P(None, 'tensor', 'dp')
- grad_up_weight: float32 [768, 3072], P('dp', 'tensor')
- grad_down_weight: float32 [3072, 768], P('tensor', 'dp')
- grad_vectors: float32 [10, 768], replicated
- grad_gains: float32 [3, 768], replicated
- grad_up_bias: float32 [3072], replicated
Inputs may be any that keep to these rules, and one draw needn't show every extreme that they name: `block_ids`: along each sequence the index never falls from one block to the next, and every value from 0 to 4 appears.
All inputs are finite; a program needn't handle non-finite values.
Results may differ from a plain program's by a relative error of at most 0.035.
Values may be sent and summed in bfloat16 or wider, within the bound.
No kernel may reach another device: no remote copies, remote signals or barrier semaphores. Data moves between devices by JAX's collectives and lax.ppermute only.
A program may use at most 128 MiB of HBM per device.

v0:
```python
import jax
import jax.numpy as jnp
from jax import lax
from jax.sharding import PartitionSpec as P

D = 768
H = 12
HD = 64
FF = 3072
BLOCK = 256


masked_value = -1e30
norm_epsilon = 1e-05
root_half = 0.7071067811865476
density_factor = 0.3989422804014327


def product(former, latter):
    return jnp.dot(former, latter, preferred_element_type=jnp.float32)


def contract_rows(former, latter):
    return lax.dot_general(
        former, latter, (((0,), (0,)), ((), ())), preferred_element_type=jnp.float32
    )


def times_transposed(former, latter):
    return lax.dot_general(
        former, latter, (((1,), (1,)), ((), ())), preferred_element_type=jnp.float32
    )


def layer_norm(summed, norm_gain, norm_shift):
    centered = summed - jnp.mean(summed, axis=-1, keepdims=True)
    inverse = lax.rsqrt(jnp.mean(centered * centered, axis=-1, keepdims=True) + norm_epsilon)
    return centered * inverse * norm_gain + norm_shift


def layer_norm_back(upstream, summed, norm_gain):
    centered = summed - jnp.mean(summed, axis=-1, keepdims=True)
    inverse = lax.rsqrt(jnp.mean(centered * centered, axis=-1, keepdims=True) + norm_epsilon)
    normed = centered * inverse
    scaled = upstream * norm_gain
    through = inverse * (
        scaled
        - jnp.mean(scaled, axis=-1, keepdims=True)
        - normed * jnp.mean(scaled * normed, axis=-1, keepdims=True)
    )
    return (through, jnp.sum(upstream * normed, axis=0), jnp.sum(upstream, axis=0))


def gelu_slope(before):
    return 0.5 * (1.0 + lax.erf(before * root_half)) + before * density_factor * jnp.exp(
        -0.5 * before * before
    )


def attend(queries, keys_all, values_all, query_ids, key_ids, head_count):
    row_count = queries.shape[0]
    block_rows = min(512, row_count)
    block_count = row_count // block_rows
    head_width = queries.shape[1] // head_count
    heads_k = keys_all.reshape(-1, head_count, head_width)
    heads_v = values_all.reshape(-1, head_count, head_width)

    def one_block(packed):
        query_block, ids_block = packed
        heads_q = query_block.reshape(block_rows, head_count, head_width)
        scores = jnp.einsum("qhd,khd->hqk", heads_q, heads_k, preferred_element_type=jnp.float32)
        allowed = key_ids[None, :] <= ids_block[:, None]
        scores = jnp.where(allowed[None], scores, masked_value)
        row_max = jnp.max(scores, axis=-1, keepdims=True)
        exponent = jnp.exp(scores - row_max)
        row_sum = jnp.sum(exponent, axis=-1, keepdims=True)
        chances = (exponent / row_sum).astype(jnp.bfloat16)
        mixed_heads = jnp.einsum(
            "hqk,khd->qhd", chances, heads_v, preferred_element_type=jnp.float32
        )
        return (
            mixed_heads.reshape(block_rows, -1).astype(jnp.bfloat16),
            (row_max + jnp.log(row_sum))[:, :, 0],
        )

    mixed_heads, logsum = lax.map(
        one_block,
        (queries.reshape(block_count, block_rows, -1), query_ids.reshape(block_count, block_rows)),
    )
    return (mixed_heads.reshape(row_count, -1), logsum)


def attend_back(grad_mixed, queries, keys_all, values_all, logsum, query_ids, key_ids, head_count):
    row_count = queries.shape[0]
    key_count = keys_all.shape[0]
    block_rows = min(512, row_count)
    block_count = row_count // block_rows
    head_width = queries.shape[1] // head_count
    heads_k = keys_all.reshape(key_count, head_count, head_width)
    heads_v = values_all.reshape(key_count, head_count, head_width)

    def one_block(totals, packed):
        key_total, value_total = totals
        query_block, grad_block, logsum_block, ids_block = packed
        heads_q = query_block.reshape(block_rows, head_count, head_width)
        heads_g = grad_block.reshape(block_rows, head_count, head_width)
        scores = jnp.einsum("qhd,khd->hqk", heads_q, heads_k, preferred_element_type=jnp.float32)
        allowed = key_ids[None, :] <= ids_block[:, None]
        chances = jnp.where(allowed[None], jnp.exp(scores - logsum_block[:, :, None]), 0.0)
        grad_chances = jnp.einsum(
            "qhd,khd->hqk", heads_g, heads_v, preferred_element_type=jnp.float32
        )
        centre = jnp.sum(chances * grad_chances, axis=-1, keepdims=True)
        grad_scores = (chances * (grad_chances - centre)).astype(jnp.bfloat16)
        grad_query = jnp.einsum(
            "hqk,khd->qhd", grad_scores, heads_k, preferred_element_type=jnp.float32
        )
        key_total = key_total + jnp.einsum(
            "hqk,qhd->khd", grad_scores, heads_q, preferred_element_type=jnp.float32
        )
        value_total = value_total + jnp.einsum(
            "hqk,qhd->khd",
            chances.astype(jnp.bfloat16),
            heads_g,
            preferred_element_type=jnp.float32,
        )
        return ((key_total, value_total), grad_query.reshape(block_rows, -1).astype(jnp.bfloat16))

    empty_keys = jnp.zeros((key_count, head_count, head_width), jnp.float32)
    packed_all = (
        queries.reshape(block_count, block_rows, -1),
        grad_mixed.reshape(block_count, block_rows, -1),
        logsum,
        query_ids.reshape(block_count, block_rows),
    )
    (key_total, value_total), query_grad = lax.scan(one_block, (empty_keys, empty_keys), packed_all)
    return (
        query_grad.reshape(row_count, -1),
        key_total.reshape(key_count, -1).astype(jnp.bfloat16),
        value_total.reshape(key_count, -1).astype(jnp.bfloat16),
    )


def body(
    inputs,
    encoder_out,
    block_ids,
    out_grad,
    in_weight,
    out_weight,
    up_weight,
    down_weight,
    vectors,
    norm_gains,
    up_bias,
):
    tensor_count = lax.axis_size("tensor")
    tensor_rank = lax.axis_index("tensor")
    local_heads = H // tensor_count
    local_width = D // tensor_count
    local_units = FF // tensor_count
    query_scale = HD ** (-0.5)
    column_start = tensor_rank * local_width
    unit_start = tensor_rank * local_units
    rows_local = inputs[0].astype(jnp.float32)
    local_rows = rows_local.shape[0]
    encoder_local = encoder_out.shape[1]

    def spread_rows(local_part):
        return lax.all_gather(local_part, "tensor", axis=0, tiled=True)

    def spread_grads(local_part):
        return lax.all_gather(local_part, "tensor", axis=0, tiled=True)

    def sum_rows(source, weight):

        def partial_term(offset, length):
            return product(source, weight)

        return lax.psum_scatter(
            partial_term(jnp.int32(0), local_rows * lax.axis_size("tensor")).astype(jnp.bfloat16),
            "tensor",
            scatter_dimension=0,
            tiled=True,
        ).astype(jnp.float32)

    def back_rows(operands):

        def partial_term(offset, length):
            accumulated = jnp.zeros((length, D), jnp.float32)
            for source, weight, factor in operands:
                accumulated = accumulated + factor * times_transposed(source, weight)
            return accumulated

        return lax.psum_scatter(
            partial_term(jnp.int32(0), local_rows * lax.axis_size("tensor")).astype(jnp.bfloat16),
            "tensor",
            scatter_dimension=0,
            tiled=True,
        ).astype(jnp.float32)

    def embed_slice(part):
        return lax.dynamic_update_slice_in_dim(jnp.zeros((D,), jnp.float32), part, column_start, 0)

    in_local, out_local, up_local, down_local = (
        lax.all_gather(in_weight.astype(jnp.bfloat16), "dp", axis=1, tiled=True),
        lax.all_gather(out_weight.astype(jnp.bfloat16), "dp", axis=2, tiled=True),
        lax.all_gather(up_weight.astype(jnp.bfloat16), "dp", axis=0, tiled=True),
        lax.all_gather(down_weight.astype(jnp.bfloat16), "dp", axis=1, tiled=True),
    )
    head_bias = lax.dynamic_slice_in_dim(vectors[0:4], column_start, local_width, 1)
    row_ids = jnp.repeat(block_ids[0], BLOCK)
    zero_rows = jnp.zeros_like(row_ids)
    encoder_full = lax.all_gather(encoder_out[0], "tensor", axis=0, tiled=True)
    zero_keys = jnp.zeros((encoder_full.shape[0],), jnp.int32)
    hidden_self = spread_rows(inputs[0])
    query_self = ((product(hidden_self, in_local[0]) + head_bias[0]) * query_scale).astype(
        jnp.bfloat16
    )
    key_self = product(hidden_self, in_local[1]).astype(jnp.bfloat16)
    value_self = (product(hidden_self, in_local[2]) + head_bias[1]).astype(jnp.bfloat16)
    mixed_self, logsum_self = attend(
        query_self, key_self, value_self, row_ids, row_ids, local_heads
    )
    summed_one = rows_local + (sum_rows(mixed_self, out_local[0]) + vectors[4])
    normed_one = layer_norm(summed_one, norm_gains[0], vectors[7])
    hidden_cross = spread_rows(normed_one.astype(jnp.bfloat16))
    query_cross = ((product(hidden_cross, in_local[3]) + head_bias[2]) * query_scale).astype(
        jnp.bfloat16
    )
    key_cross = product(encoder_full, in_local[4]).astype(jnp.bfloat16)
    value_cross = (product(encoder_full, in_local[5]) + head_bias[3]).astype(jnp.bfloat16)
    mixed_cross, logsum_cross = attend(
        query_cross, key_cross, value_cross, zero_rows, zero_keys, local_heads
    )
    summed_two = normed_one + (sum_rows(mixed_cross, out_local[1]) + vectors[5])
    normed_two = layer_norm(summed_two, norm_gains[1], vectors[8])
    hidden_ffn = spread_rows(normed_two.astype(jnp.bfloat16))
    before = product(hidden_ffn, up_local) + lax.dynamic_slice_in_dim(
        up_bias, unit_start, local_units, 0
    )
    active = jax.nn.gelu(before, approximate=False).astype(jnp.bfloat16)
    summed_three = normed_two + (sum_rows(active, down_local) + vectors[6])
    layer_out = layer_norm(summed_three, norm_gains[2], vectors[9]).astype(jnp.bfloat16)
    in_local, out_local, up_local, down_local = (
        lax.all_gather(in_weight.astype(jnp.bfloat16), "dp", axis=1, tiled=True),
        lax.all_gather(out_weight.astype(jnp.bfloat16), "dp", axis=2, tiled=True),
        lax.all_gather(up_weight.astype(jnp.bfloat16), "dp", axis=0, tiled=True),
        lax.all_gather(down_weight.astype(jnp.bfloat16), "dp", axis=1, tiled=True),
    )
    upstream = out_grad[0].astype(jnp.float32)
    grad_three, gain_three, shift_three = layer_norm_back(upstream, summed_three, norm_gains[2])
    branch_three = grad_three.astype(jnp.bfloat16)
    bias_down = jnp.sum(branch_three.astype(jnp.float32), axis=0)
    wide_three = spread_grads(branch_three)
    grad_active = times_transposed(wide_three, down_local)
    down_grad = contract_rows(active, wide_three)
    grad_before = (grad_active * gelu_slope(before)).astype(jnp.bfloat16)
    unit_part = jnp.sum(grad_before.astype(jnp.float32), axis=0)
    unit_bias = lax.dynamic_update_slice_in_dim(
        jnp.zeros((FF,), jnp.float32), unit_part, unit_start, 0
    )
    up_grad = contract_rows(hidden_ffn, grad_before)
    grad_two_in = grad_three + back_rows(((grad_before, up_local, 1.0),))
    grad_two, gain_two, shift_two = layer_norm_back(grad_two_in, summed_two, norm_gains[1])
    branch_two = grad_two.astype(jnp.bfloat16)
    bias_cross_out = jnp.sum(branch_two.astype(jnp.float32), axis=0)
    wide_two = spread_grads(branch_two)
    grad_mixed_cross = times_transposed(wide_two, out_local[1]).astype(jnp.bfloat16)
    out_grad_cross = contract_rows(mixed_cross, wide_two)
    query_grad_cross, key_grad_cross, value_grad_cross = attend_back(
        grad_mixed_cross,
        query_cross,
        key_cross,
        value_cross,
        logsum_cross,
        zero_rows,
        zero_keys,
        local_heads,
    )
    weight_query_cross = query_scale * contract_rows(hidden_cross, query_grad_cross)
    weight_key_cross = contract_rows(encoder_full, key_grad_cross)
    weight_value_cross = contract_rows(encoder_full, value_grad_cross)
    bias_query_cross = query_scale * jnp.sum(query_grad_cross.astype(jnp.float32), axis=0)
    bias_value_cross = jnp.sum(value_grad_cross.astype(jnp.float32), axis=0)
    grad_one_in = grad_two + back_rows(((query_grad_cross, in_local[3], query_scale),))
    operands = ((key_grad_cross, in_local[4]), (value_grad_cross, in_local[5]))

    def partial_term(offset, length):
        accumulated = jnp.zeros((length, D), jnp.float32)
        for source, weight in operands:
            accumulated = accumulated + times_transposed(source, weight)
        return accumulated

    encoder_grad = lax.psum_scatter(
        partial_term(jnp.int32(0), encoder_local * lax.axis_size("tensor")).astype(jnp.bfloat16),
        "tensor",
        scatter_dimension=0,
        tiled=True,
    ).astype(jnp.float32)
    grad_one, gain_one, shift_one = layer_norm_back(grad_one_in, summed_one, norm_gains[0])
    branch_one = grad_one.astype(jnp.bfloat16)
    bias_self_out = jnp.sum(branch_one.astype(jnp.float32), axis=0)
    wide_one = spread_grads(branch_one)
    grad_mixed_self = times_transposed(wide_one, out_local[0]).astype(jnp.bfloat16)
    out_grad_self = contract_rows(mixed_self, wide_one)
    query_grad_self, key_grad_self, value_grad_self = attend_back(
        grad_mixed_self,
        query_self,
        key_self,
        value_self,
        logsum_self,
        row_ids,
        row_ids,
        local_heads,
    )
    weight_query_self = query_scale * contract_rows(hidden_self, query_grad_self)
    weight_key_self = contract_rows(hidden_self, key_grad_self)
    weight_value_self = contract_rows(hidden_self, value_grad_self)
    bias_query_self = query_scale * jnp.sum(query_grad_self.astype(jnp.float32), axis=0)
    bias_value_self = jnp.sum(value_grad_self.astype(jnp.float32), axis=0)
    input_grad = grad_one + back_rows(
        (
            (query_grad_self, in_local[0], query_scale),
            (key_grad_self, in_local[1], 1.0),
            (value_grad_self, in_local[2], 1.0),
        )
    )
    in_grad_stack = jnp.stack(
        [
            weight_query_self,
            weight_key_self,
            weight_value_self,
            weight_query_cross,
            weight_key_cross,
            weight_value_cross,
        ]
    )
    out_grad_stack = jnp.stack([out_grad_self, out_grad_cross])
    in_grad_shard, out_grad_shard, up_grad_shard, down_grad_shard = (
        lax.psum_scatter(in_grad_stack, "dp", scatter_dimension=1, tiled=True),
        lax.psum_scatter(out_grad_stack, "dp", scatter_dimension=2, tiled=True),
        lax.psum_scatter(up_grad, "dp", scatter_dimension=0, tiled=True),
        lax.psum_scatter(down_grad, "dp", scatter_dimension=1, tiled=True),
    )
    vector_grad = jnp.stack(
        [
            embed_slice(bias_query_self),
            embed_slice(bias_value_self),
            embed_slice(bias_query_cross),
            embed_slice(bias_value_cross),
            bias_self_out,
            bias_cross_out,
            bias_down,
            shift_one,
            shift_two,
            shift_three,
        ]
    )
    gain_grad = jnp.stack([gain_one, gain_two, gain_three])
    vector_total, gain_total, unit_total = lax.psum(
        (vector_grad, gain_grad, unit_bias), ("dp", "tensor")
    )
    return (
        layer_out[None],
        input_grad[None],
        encoder_grad[None],
        in_grad_shard,
        out_grad_shard,
        up_grad_shard,
        down_grad_shard,
        vector_total,
        gain_total,
        unit_total,
    )


def solution(mesh):
    return jax.shard_map(
        body,
        mesh=mesh,
        in_specs=(
            P("dp", "tensor", None),
            P("dp", "tensor", None),
            P("dp", None),
            P("dp", "tensor", None),
            P(None, "dp", "tensor"),
            P(None, "tensor", "dp"),
            P("dp", "tensor"),
            P("tensor", "dp"),
            P(),
            P(),
            P(),
        ),
        out_specs=(
            P("dp", "tensor", None),
            P("dp", "tensor", None),
            P("dp", "tensor", None),
            P(None, "dp", "tensor"),
            P(None, "tensor", "dp"),
            P("dp", "tensor"),
            P("tensor", "dp"),
            P(),
            P(),
            P(),
        ),
        check_vma=False,
    )
```

profile of v0, /device:TPU:0, one launch (start us, length us, event | category | flops | bytes accessed | tf_op | source)
XLA Modules:
  0.0 1423.4 jit_solution(8328995921679387437)
XLA Ops:
  13.0 13.0 all_gather.39
  29.2 13.7 all-gather.13.cloned.1.call-done
  42.9 65.0 %all-gather.29.cloned.1.call-done = bf16[1,2048,768]{2,1,0:T(8,128)(2,1)} async-done(((bf16[1,512,768]{2,1,0:T(8,128)(2,1)}), bf16[1,2048,768]{2,1,0:T(8,128)(2,1)}) %all-gather.29.cloned.1.call-update) | async-done | bytes 3145744 | tf_op jit(solution)/shard_map/all_gather | solution.py:170
  116.7 90.6 %while.56 = (s32[]{:T(128)}, bf16[4,512,192]{1,2,0:T(8,128)(2,1)S(1)}, f32[4,3,512]{2,1,0:T(4,128)S(1)}, s32[4,512]{1,0:T(4,128)S(1)}, bf16[4,512,192]{1,2,0:T(8...) while((s32[]{:T(128)}, ...), condition=%wide.region_3.4_spmd.clone, body=%wide.region_0.3_spmd.clone.sunk | while | flops 834763264 | bytes 44789908 | solution.py:86
  118.4 6.7 select_reduce_fusion.2
  125.1 7.8 fusion.271
  132.9 6.4 fusion.272
  141.0 6.7 select_reduce_fusion.2
  147.8 7.8 fusion.271
  155.5 6.4 fusion.272
  163.7 6.7 select_reduce_fusion.2
  170.4 7.8 fusion.271
  178.2 6.4 fusion.272
  186.3 6.7 select_reduce_fusion.2
  193.1 7.8 fusion.271
  200.8 6.4 fusion.272
  212.8 57.7 %reduce-scatter.16.cloned.1.call-done = bf16[512,768]{1,0:T(8,128)(2,1)} async-done(((bf16[2048,768]{1,0:T(8,128)(2,1)}), bf16[512,768]{1,0:T(8,128)(2,1)}) %reduce-scatter.16.cloned.1.call-update) | async-done | bytes 786448 | tf_op jit(solution)/shard_map/reduce_scatter | solution.py:180
  276.7 32.1 %all-gather.31.cloned.1.call-done = bf16[1,1024,768]{2,1,0:T(8,128)(2,1)} async-done(((bf16[1,256,768]{2,1,0:T(8,128)(2,1)}), bf16[1,1024,768]{2,1,0:T(8,128)(2,1)}) %all-gather.31.cloned.1.call-update) | async-done | bytes 1572880 | tf_op jit(solution)/shard_map/all_gather | solution.py:214
  313.2 60.0 %all-gather.15.cloned.1.call-done = bf16[2048,768]{1,0:T(8,128)(2,1)} async-done(((bf16[512,768]{1,0:T(8,128)(2,1)}), bf16[2048,768]{1,0:T(8,128)(2,1)}) %all-gather.15.cloned.1.call-update) | async-done | bytes 3145744 | tf_op jit(solution)/shard_map/all_gather | solution.py:170
  377.4 20.2 %while.55 = (s32[]{:T(128)}, bf16[4,512,192]{1,2,0:T(8,128)(2,1)}, f32[4,3,512]{2,1,0:T(4,128)S(1)}, bf16[4,512,192]{1,2,0:T(8,128)(2,1)S(1)}, bf16[1024,3,64]{0...) while((s32[]{:T(128)}, bf16[4,512,192]{1,2,0:T(8,128)(2,1)}, ...), condition=%wide.region_10.11_spmd, body=%wide.region_7.10_spmd.sunk | while | flops 412187136 | bytes 20895840 | solution.py:86
  399.6 3.9 convolution_convert_fusion.4
  405.3 57.5 %reduce-scatter.18.cloned.1.call-done = bf16[512,768]{1,0:T(8,128)(2,1)} async-done(((bf16[2048,768]{1,0:T(8,128)(2,1)}), bf16[512,768]{1,0:T(8,128)(2,1)}) %reduce-scatter.18.cloned.1.call-update) | async-done | bytes 786448 | tf_op jit(solution)/shard_map/reduce_scatter | solution.py:180
  468.9 20.2 %all-gather.19.cloned.1.call-done = bf16[768,768]{1,0:T(8,128)(2,1)} async-done(((bf16[96,768]{1,0:T(8,128)(2,1)}), bf16[768,768]{1,0:T(8,128)(2,1)}) %all-gather.19.cloned.1.call-update) | async-done | bytes 1179664 | tf_op jit(solution)/shard_map/all_gather | solution.py:208
  489.1 65.6 %all-gather.17.cloned.1.call-done = bf16[2048,768]{1,0:T(8,128)(2,1)} async-done(((bf16[512,768]{1,0:T(8,128)(2,1)}), bf16[2048,768]{1,0:T(8,128)(2,1)}) %all-gather.17.cloned.1.call-update) | async-done | bytes 3145744 | tf_op jit(solution)/shard_map/all_gather | solution.py:170
  554.7 18.4 %fusion.38 = (bf16[2048,768]{1,0:T(8,128)(2,1)}, f32[2048,768]{1,0:T(8,128)}) fusion(f32[768]{0:T(1024)S(1)} %dynamic_slice.42, bf16[2048,768]{1,0:T(8,128)(2,1)} %all-gather.17.cloned.1.call-done, bf16[768,768]{1,0:T(8,128)(2,1)} %all-gather.19.cloned.1.call-done), kind=kOutput, calls=%fused_computation.63 | convolution fusion | flops 2519728128 | bytes 13765632 | tf_op jit(solution)/shard_map/dot_general | solution.py:20
  573.1 6.6 all-gather.21.cloned.1.call-done
  579.8 6.5 convolution_convert_fusion.3
  586.4 60.5 %reduce-scatter.20.cloned.1.call-done = bf16[512,768]{1,0:T(8,128)(2,1)} async-done(((bf16[2048,768]{1,0:T(8,128)(2,1)}), bf16[512,768]{1,0:T(8,128)(2,1)}) %reduce-scatter.20.cloned.1.call-update) | async-done | bytes 786448 | tf_op jit(solution)/shard_map/reduce_scatter | solution.py:180
  652.9 63.5 %all-gather.23.cloned.1.call-done = bf16[2048,768]{1,0:T(8,128)(2,1)} async-done(((bf16[512,768]{1,0:T(8,128)(2,1)}), bf16[2048,768]{1,0:T(8,128)(2,1)}) %all-gather.23.cloned.1.call-update) | async-done | bytes 3145744 | tf_op jit(solution)/shard_map/all_gather | solution.py:173
  716.3 7.6 convert_reduce_fusion
  725.6 4.0 convolution_convert_fusion.2
  729.9 59.0 %reduce-scatter.22.cloned.1.call-done = bf16[512,768]{1,0:T(8,128)(2,1)} async-done(((bf16[2048,768]{1,0:T(8,128)(2,1)}), bf16[512,768]{1,0:T(8,128)(2,1)}) %reduce-scatter.22.cloned.1.call-update) | async-done | bytes 786448 | tf_op jit(solution)/shard_map/reduce_scatter | solution.py:195
  794.1 63.4 %all-gather.25.cloned.1.call-done = bf16[2048,768]{1,0:T(8,128)(2,1)} async-done(((bf16[512,768]{1,0:T(8,128)(2,1)}), bf16[2048,768]{1,0:T(8,128)(2,1)}) %all-gather.25.cloned.1.call-update) | async-done | bytes 3145744 | tf_op jit(solution)/shard_map/all_gather | solution.py:173
  861.6 37.2 %while.57 = (s32[]{:T(128)}, f32[1024,3,64]{0,2,1:T(8,128)S(1)}, f32[1024,3,64]{0,2,1:T(8,128)S(1)}, bf16[4,512,192]{1,2,0:T(8,128)(2,1)S(1)}, bf16[4,512,192]{1...) while((s32[]{:T(128)}, f32[1024,3,64]{0,2,1:T(8,128)S(1)}, ...), condition=%wide.region_24.25_spmd.clone, body=%wide.region_22.24_spmd.clone.sunk | while | flops 1021671936 | bytes 53717128 | solution.py:136
  904.6 59.2 %reduce-scatter.24.cloned.1.call-done = bf16[512,768]{1,0:T(8,128)(2,1)} async-done(((bf16[2048,768]{1,0:T(8,128)(2,1)}), bf16[512,768]{1,0:T(8,128)(2,1)}) %reduce-scatter.24.cloned.1.call-update) | async-done | bytes 786448 | tf_op jit(solution)/shard_map/reduce_scatter | solution.py:195
  979.3 54.1 %all-gather.27.cloned.1.call-done = bf16[2048,768]{1,0:T(8,128)(2,1)} async-done(((bf16[512,768]{1,0:T(8,128)(2,1)}), bf16[2048,768]{1,0:T(8,128)(2,1)}) %all-gather.27.cloned.1.call-update) | async-done | bytes 3145744 | tf_op jit(solution)/shard_map/all_gather | solution.py:173
  1038.4 122.5 %while.58 = (s32[]{:T(128)}, f32[2048,3,64]{0,2,1:T(8,128)}, f32[2048,3,64]{0,2,1:T(8,128)}, bf16[4,512,192]{1,2,0:T(8,128)(2,1)}, bf16[4,512,192]{1,2,0:T(8,128...) while((s32[]{:T(128)}, f32[2048,3,64]{0,2,1:T(8,128)}, ...), condition=%wide.region_30.31_spmd.clone, body=%wide.region_28.30_spmd.clone.sunk | while | flops 2053732864 | bytes 141967648 | solution.py:136
  1047.4 5.3 multiply_reduce_fusion.14
  1052.8 5.9 multiply_convert_fusion.6
  1058.7 5.1 convolution_convert_fusion.11
  1072.0 5.1 fusion.298
  1077.2 5.3 multiply_reduce_fusion.14
  1082.5 5.9 multiply_convert_fusion.6
  1088.4 5.1 convolution_convert_fusion.11
  1093.6 3.9 fusion.297
  1103.2 5.1 fusion.298
  1108.4 5.3 multiply_reduce_fusion.14
  1113.7 5.9 multiply_convert_fusion.6
  1119.6 5.1 convolution_convert_fusion.11
  1124.7 3.9 fusion.297
  1134.4 5.1 fusion.298
  1139.6 5.3 multiply_reduce_fusion.14
  1144.9 5.9 multiply_convert_fusion.6
  1150.8 5.1 convolution_convert_fusion.11
  1155.9 3.9 fusion.297
  1187.0 6.2 copy.65
  1193.2 6.6 reshape.380
  1205.1 3.8 add_convert_fusion
  1210.8 6.0 fusion.165
  1216.9 7.3 fusion.166
  1228.9 40.6 %all-reduce = (f32[10,768]{1,0:T(8,128)}, f32[3,768]{1,0:T(4,128)}, f32[3072]{0:T(1024)}) all-reduce(f32[10,768]{1,0:T(8,128)S(1)} %stack.92, f32[3,768]{1,0:T(4,128)S(1)} %pad_maximum_fusion.1, f32[3072]{0:T(1024)S(1)} %dynamic_update_slice.43), channel_id=1, replica_groups=mesh['dp'=8,'tensor'=4] {'dp','tensor'}, use_global_device_ids=true, to_apply=%region_47.48 | all-reduce | flops 13056 | bytes 104448 | tf_op jit(solution)/shard_map/psum | solution.py:361
  1273.7 50.3 %reduce-scatter.26.cloned.1.call-done = bf16[512,768]{1,0:T(8,128)(2,1)} async-done(((bf16[2048,768]{1,0:T(8,128)(2,1)}), bf16[512,768]{1,0:T(8,128)(2,1)}) %reduce-scatter.26.cloned.1.call-update) | async-done | bytes 786448 | tf_op jit(solution)/shard_map/reduce_scatter | solution.py:195
  1326.5 43.6 %reduce-scatter.30.cloned.1.call-done = f32[96,768]{1,0:T(8,128)} async-done(((f32[768,768]{1,0:T(8,128)}), f32[96,768]{1,0:T(8,128)}) %reduce-scatter.30.cloned.1.call-update) | async-done | bytes 294928 | tf_op jit(solution)/shard_map/reduce_scatter | solution.py:343
  1370.1 46.3 %reduce-scatter.32.cloned.1.call-done = f32[768,96]{0,1:T(8,128)} async-done(((f32[768,768]{0,1:T(8,128)}), f32[768,96]{0,1:T(8,128)}) %reduce-scatter.32.cloned.1.call-update) | async-done | bytes 294928 | tf_op jit(solution)/shard_map/reduce_scatter | solution.py:344
  (475 shorter events, 228.0 us)
Async XLA Ops:
  7.2 35.7 %all-gather.13.cloned.1.call-start = ((), (), s32[]{:S(2)}) async-start(), calls=%async_computation.11 | async-start | bytes 2654208 | tf_op jit(solution)/shard_map/all_gather | solution.py:206
  9.1 19.5 %slice-start = ((f32[10,768]{1,0:T(8,128)}), f32[4,768]{1,0:T(4,128)S(1)}, s32[]{:S(2)}) async-start(f32[10,768]{1,0:T(8,128)} %param.27), calls=%async_computation.32 | async-start | bytes 24576 | tf_op jit(solution)/shard_map/slice | solution.py:211
  9.1 98.9 %all-gather.29.cloned.1.call-start = ((), (), s32[]{:S(2)}) async-start(), calls=%async_computation.28 | async-start | bytes 3932160 | tf_op jit(solution)/shard_map/all_gather | solution.py:170
  9.8 260.7 %reduce-scatter.16.cloned.1.call-start = ((), (), s32[]{:S(2)}) async-start(), calls=%async_computation.12 | async-start | bytes 3932160 | tf_op jit(solution)/shard_map/reduce_scatter | solution.py:180
  28.6 178.9 %copy-start.43 = (bf16[1,192,768]{2,1,0:T(8,128)(2,1)}, bf16[1,192,768]{2,1,0:T(8,128)(2,1)S(1)}, u32[]{:S(2)}) copy-start(bf16[1,192,768]{2,1,0:T(8,128)(2,1)S(1)} %copy.70) | copy-start | bytes 884740
  211.2 59.2 %copy-start.5 = (bf16[1,512,768]{2,1,0:T(8,128)(2,1)S(1)}, bf16[1,512,768]{2,1,0:T(8,128)(2,1)}, u32[]{:S(2)}) copy-start(bf16[1,512,768]{2,1,0:T(8,128)(2,1)} %param.19) | copy-start | bytes 2359300
  211.3 97.6 %all-gather.31.cloned.1.call-start = ((), (), s32[]{:S(2)}) async-start(), calls=%async_computation.29 | async-start | bytes 1966080 | tf_op jit(solution)/shard_map/all_gather | solution.py:214
  211.8 161.3 %all-gather.15.cloned.1.call-start = ((), (), s32[]{:S(2)}) async-start(), calls=%async_computation.13 | async-start | bytes 3932160 | tf_op jit(solution)/shard_map/all_gather | solution.py:170
  212.8 62.3 %copy-start.62 = (f32[768]{0:T(1024)}, f32[768]{0:T(1024)S(1)}, u32[]{:S(2)}) copy-start(f32[768]{0:T(1024)S(1)} %get-tuple-element.482) | copy-start | bytes 9220
  212.8 250.0 %copy-start.47 = (f32[768]{0:T(1024)}, f32[768]{0:T(1024)S(1)}, u32[]{:S(2)}) copy-start(f32[768]{0:T(1024)S(1)} %get-tuple-element.483) | copy-start | bytes 9220
  212.8 250.0 %copy-start.51 = (f32[768]{0:T(1024)}, f32[768]{0:T(1024)S(1)}, u32[]{:S(2)}) copy-start(f32[768]{0:T(1024)S(1)} %get-tuple-element.600) | copy-start | bytes 9220
  270.5 4.6 copy-start.38
  272.1 190.7 %copy-start.54 = (f32[512]{0:T(512)}, f32[512]{0:T(512)S(1)}, u32[]{:S(2)}) copy-start(f32[512]{0:T(512)S(1)} %broadcast_multiply_fusion.8) | copy-start | bytes 6148
  273.7 37.3 %copy-start.56 = (f32[512]{0:T(512)}, f32[512]{0:T(512)S(1)}, u32[]{:S(2)}) copy-start(f32[512]{0:T(512)S(1)} %add_rsqrt_fusion.2) | copy-start | bytes 6148
  273.7 37.3 %copy-start.76 = (f32[1,192]{1,0:T(1,128)S(1)}, f32[1,192]{1,0:T(1,128)}, u32[]{:S(2)}) copy-start(f32[1,192]{1,0:T(1,128)} %get-tuple-element.591) | copy-start | bytes 2308
  275.0 98.2 %copy-start.79 = (f32[1,192]{1,0:T(1,128)S(1)}, f32[1,192]{1,0:T(1,128)}, u32[]{:S(2)}) copy-start(f32[1,192]{1,0:T(1,128)} %get-tuple-element.592) | copy-start | bytes 2308
  275.1 187.7 %reduce-scatter.18.cloned.1.call-start = ((), (), s32[]{:S(2)}) async-start(), calls=%async_computation.14 | async-start | bytes 3932160 | tf_op jit(solution)/shard_map/reduce_scatter | solution.py:180
  397.5 6.0 copy-start.13
  397.5 6.0 copy-start.50
  403.6 85.5 %all-gather.19.cloned.1.call-start = ((), (), s32[]{:S(2)}) async-start(), calls=%async_computation.16 | async-start | bytes 1327104 | tf_op jit(solution)/shard_map/all_gather | solution.py:208
  405.2 149.5 %all-gather.17.cloned.1.call-start = ((), (), s32[]{:S(2)}) async-start(), calls=%async_computation.15 | async-start | bytes 3932160 | tf_op jit(solution)/shard_map/all_gather | solution.py:170
  466.9 112.9 %all-gather.21.cloned.1.call-start = ((), (), s32[]{:S(2)}) async-start(), calls=%async_computation.17 | async-start | bytes 1327104 | tf_op jit(solution)/shard_map/all_gather | solution.py:209
  467.7 179.2 %reduce-scatter.20.cloned.1.call-start = ((), (), s32[]{:S(2)}) async-start(), calls=%async_computation.18 | async-start | bytes 3932160 | tf_op jit(solution)/shard_map/reduce_scatter | solution.py:180
  468.9 104.2 %copy-start.78 = (f32[768]{0:T(1024)}, f32[768]{0:T(1024)S(1)}, u32[]{:S(2)}) copy-start(f32[768]{0:T(1024)S(1)} %dynamic_slice.42) | copy-start | bytes 9220
  586.3 60.6 %copy-start.61 = (f32[768]{0:T(1024)S(1)}, f32[768]{0:T(1024)}, u32[]{:S(2)}) copy-start(f32[768]{0:T(1024)} %get-tuple-element.480) | copy-start | bytes 9220
  586.3 60.6 %copy-start.65 = (f32[768]{0:T(1024)S(1)}, f32[768]{0:T(1024)}, u32[]{:S(2)}) copy-start(f32[768]{0:T(1024)} %get-tuple-element.484) | copy-start | bytes 9220
  586.3 62.7 %copy-start.24 = (bf16[1,512,768]{2,1,0:T(8,128)(2,1)S(1)}, bf16[1,512,768]{2,1,0:T(8,128)(2,1)}, u32[]{:S(2)}) copy-start(bf16[1,512,768]{2,1,0:T(8,128)(2,1)} %param.22) | copy-start | bytes 2359300
  586.3 62.7 %copy-start.60 = (f32[768]{0:T(1024)S(1)}, f32[768]{0:T(1024)}, u32[]{:S(2)}) copy-start(f32[768]{0:T(1024)} %get-tuple-element.601) | copy-start | bytes 9220
  586.4 130.0 %all-gather.23.cloned.1.call-start = ((), (), s32[]{:S(2)}) async-start(), calls=%async_computation.19 | async-start | bytes 3932160 | tf_op jit(solution)/shard_map/all_gather | solution.py:173
  652.8 136.0 %reduce-scatter.22.cloned.1.call-start = ((), (), s32[]{:S(2)}) async-start(), calls=%async_computation.20 | async-start | bytes 3932160 | tf_op jit(solution)/shard_map/reduce_scatter | solution.py:195
  716.3 9.3 copy-start.81
  729.6 127.9 %all-gather.25.cloned.1.call-start = ((), (), s32[]{:S(2)}) async-start(), calls=%async_computation.21 | async-start | bytes 3932160 | tf_op jit(solution)/shard_map/all_gather | solution.py:173
  794.0 169.7 %reduce-scatter.24.cloned.1.call-start = ((), (), s32[]{:S(2)}) async-start(), calls=%async_computation.22 | async-start | bytes 3932160 | tf_op jit(solution)/shard_map/reduce_scatter | solution.py:195
  794.1 67.5 %copy-start.14 = (bf16[1024,3,64]{0,2,1:T(8,128)(2,1)S(1)}, bf16[1024,3,64]{0,2,1:T(8,128)(2,1)}, u32[]{:S(2)}) copy-start(bf16[1024,3,64]{0,2,1:T(8,128)(2,1)} %copy-done.13) | copy-start | bytes 1179652
  900.7 63.1 %copy-start.6 = (bf16[1,512,768]{2,1,0:T(8,128)(2,1)S(1)}, bf16[1,512,768]{2,1,0:T(8,128)(2,1)}, u32[]{:S(2)}) copy-start(bf16[1,512,768]{2,1,0:T(8,128)(2,1)} %param.19) | copy-start | bytes 2359300
  900.7 63.1 %copy-start.11 = (bf16[512,768]{1,0:T(8,128)(2,1)S(1)}, bf16[512,768]{1,0:T(8,128)(2,1)}, u32[]{:S(2)}) copy-start(bf16[512,768]{1,0:T(8,128)(2,1)} %reduce-scatter.16.cloned.1.call-done) | copy-start | bytes 2359300
  900.7 63.1 %copy-start.48 = (f32[768]{0:T(1024)S(1)}, f32[768]{0:T(1024)}, u32[]{:S(2)}) copy-start(f32[768]{0:T(1024)} %copy-done.47) | copy-start | bytes 9220
  900.7 63.1 %copy-start.52 = (f32[768]{0:T(1024)S(1)}, f32[768]{0:T(1024)}, u32[]{:S(2)}) copy-start(f32[768]{0:T(1024)} %copy-done.51) | copy-start | bytes 9220
  900.7 63.1 %copy-start.55 = (f32[512]{0:T(512)S(1)}, f32[512]{0:T(512)}, u32[]{:S(2)}) copy-start(f32[512]{0:T(512)} %copy-done.54) | copy-start | bytes 6148
  900.7 63.1 %copy-start.57 = (f32[512]{0:T(512)S(1)}, f32[512]{0:T(512)}, u32[]{:S(2)}) copy-start(f32[512]{0:T(512)} %copy-done.56) | copy-start | bytes 6148
  904.6 128.9 %all-gather.27.cloned.1.call-start = ((), (), s32[]{:S(2)}) async-start(), calls=%async_computation.23 | async-start | bytes 3932160 | tf_op jit(solution)/shard_map/all_gather | solution.py:173
  969.9 256.1 %reduce-scatter.28.cloned.1.call-start = ((), (), s32[]{:S(2)}) async-start(), calls=%async_computation.25 | async-start | bytes 1966080 | tf_op jit(solution)/shard_map/reduce_scatter | solution.py:295
  970.1 5.4 copy-start.34
  970.8 4.7 copy-start.32
  975.5 58.0 %copy-start.44 = (bf16[1,192,768]{2,1,0:T(8,128)(2,1)S(1)}, bf16[1,192,768]{2,1,0:T(8,128)(2,1)}, u32[]{:S(2)}) copy-start(bf16[1,192,768]{2,1,0:T(8,128)(2,1)} %copy-done.43) | copy-start | bytes 884740
  975.5 294.0 %reduce-scatter.36.cloned.1.call-start = ((), (), s32[]{:S(2)}) async-start(), calls=%async_computation.31 | async-start | bytes 1327104
  979.3 59.1 %copy-start.3 = (bf16[2048,3,64]{0,2,1:T(8,128)(2,1)S(1)}, bf16[2048,3,64]{0,2,1:T(8,128)(2,1)}, u32[]{:S(2)}) copy-start(bf16[2048,3,64]{0,2,1:T(8,128)(2,1)} %copy-done.2) | copy-start | bytes 2359300
  979.3 59.1 %copy-start.59 = (s32[1,8]{1,0:T(1,128)S(1)}, s32[1,8]{1,0:T(1,128)}, u32[]{:S(2)}) copy-start(s32[1,8]{1,0:T(1,128)} %param.21) | copy-start | bytes 100
  1058.7 5.1 copy-start
  1088.4 5.1 copy-start
  1093.6 4.6 copy-start.4
  1119.6 5.1 copy-start
  1124.7 4.6 copy-start.4
  1150.8 5.1 copy-start
  1155.9 4.6 copy-start.4
  1160.9 5.4 copy-start.42
  1168.5 5.7 copy-start.9
  1174.2 97.3 %reduce-scatter.34.cloned.1.call-start = ((), (), s32[]{:S(2)}) async-start(), calls=%async_computation.30 | async-start | bytes 3981312
  1174.2 4.5 copy-start.19
  1199.7 124.3 %reduce-scatter.26.cloned.1.call-start = ((), (), s32[]{:S(2)}) async-start(), calls=%async_computation.24 | async-start | bytes 3932160 | tf_op jit(solution)/shard_map/reduce_scatter | solution.py:195
  1208.9 161.2 %reduce-scatter.30.cloned.1.call-start = ((), (), s32[]{:S(2)}) async-start(), calls=%async_computation.26 | async-start | bytes 2654208 | tf_op jit(solution)/shard_map/reduce_scatter | solution.py:343
  1216.8 7.5 copy-start.26
  1216.8 199.6 %reduce-scatter.32.cloned.1.call-start = ((), (), s32[]{:S(2)}) async-start(), calls=%async_computation.27 | async-start | bytes 2654208 | tf_op jit(solution)/shard_map/reduce_scatter | solution.py:344
  1225.6 98.4 %copy-start.30 = (f32[512,768]{1,0:T(8,128)S(1)}, f32[512,768]{1,0:T(8,128)}, u32[]{:S(2)}) copy-start(f32[512,768]{1,0:T(8,128)} %get-tuple-element.567) | copy-start | bytes 4718596
  (50 other events, 108.6 us)
Sparse Core Ops, SparseCore 0:
  10.5 32.4 all-gather.12
  44.5 63.4 all-gather.28
  211.4 59.0 reduce-scatter.15
  271.9 36.9 all-gather.30
  310.8 62.2 all-gather.14
  403.7 59.0 reduce-scatter.17
  465.2 23.8 all-gather.18
  491.2 63.4 all-gather.16
  557.2 22.5 all-gather.20
  586.5 60.3 reduce-scatter.19
  652.9 63.3 all-gather.22
  729.8 59.0 reduce-scatter.21
  794.2 63.3 all-gather.24
  904.7 59.0 reduce-scatter.23
  970.1 63.3 all-gather.26
  1035.6 34.0 reduce-scatter.27
  1174.3 35.3 reduce-scatter.35
  1213.0 48.3 reduce-scatter.33
  1263.7 60.3 reduce-scatter.25
  1327.8 42.2 reduce-scatter.29
  1374.0 42.3 reduce-scatter.31
where the time goes:
time: 1430 us; the launch traced here: 1420 us
  waiting for transfers between devices  880 us (62%)
  matrix products  282 us (20%)
  other arithmetic  112 us (8%)
  local copies, waits for them, and re-layouts  77.8 us (5%)
  blocking collectives  53.6 us (4%)
  between operations  15.6 us (1%)
    all_gather x3, waiting for transfers between devices, spread_rows(): return lax.all_gather(local_part, 'tensor', axis=0, tiled=True)  191 us
    all_gather x3, waiting for transfers between devices, spread_grads(): return lax.all_gather(local_part, 'tensor', axis=0, tiled=True)  181 us
    reduce_scatter x3, waiting for transfers between devices, sum_rows(): lax.psum_scatter(partial_term(jnp.int32(0), local_rows * lax.axis_size('t...  176 us
    reduce_scatter x3, waiting for transfers between devices, back_rows(): lax.psum_scatter(partial_term(jnp.int32(0), local_rows * lax.axis_size('t...  168 us
    dot_general x10, matrix products, product(): return jnp.dot(former, latter, preferred_element_type=jnp.float32)  46.7 us
    reduce_scatter x1, waiting for transfers between devices, body(): lax.psum_scatter(down_grad, 'dp', scatter_dimension=1, tiled=True)  46.3 us
    reduce_scatter x1, waiting for transfers between devices, body(): lax.psum_scatter(up_grad, 'dp', scatter_dimension=0, tiled=True)  43.6 us
    dot_general x16, matrix products, one_block(): jnp.einsum('qhd,khd->hqk', heads_q, heads_k, preferred_element_type=jnp.f...  42.7 us
  transfers between devices with their start and end apart: 21, of which 18 were waited for; matrix products, arithmetic and copies ran while one was open for 17% of the time, Pallas kernels for 0%

commit v1 on v0

v1 whole, which is shorter than its diff:
```python
import functools
import jax, jax.numpy as jnp
from jax import lax
from jax.experimental import pallas as pl
from jax.experimental.pallas import tpu as pltpu
HD=64
KB=256
def dot_nn(a,b): return jnp.dot(a,b,preferred_element_type=jnp.float32)
def dot_nt(a,b): return lax.dot_general(a,b,(((1,),(1,)),((),())),preferred_element_type=jnp.float32)

def head_masked(block, h):
    rows = lax.broadcasted_iota(jnp.int32, block.shape, 0)
    return jnp.where((rows >= h*HD) & (rows < (h+1)*HD), block, jnp.zeros_like(block))

def attend_kernel(counts_ref, q_ref, k_ref, v_ref, o_ref, lse_ref, vt_ref, *, heads):
    i = pl.program_id(0)
    nk = k_ref.shape[0]//KB
    bq = q_ref.shape[1]
    @pl.when(i == 0)
    def _():
        for j in range(nk):
            vt_ref[:, j*KB:(j+1)*KB] = v_ref[j*KB:(j+1)*KB, :].T
    q = q_ref[...]
    qm = [head_masked(q, h) for h in range(heads)]
    def step(j, carry):
        start = pl.multiple_of(j*KB, KB)
        kj = k_ref[pl.ds(start, KB), :]
        new = []
        for h in range(heads):
            m, l, acc = carry[h]
            s = dot_nn(kj, qm[h])
            m_new = jnp.maximum(m, jnp.max(s, axis=0, keepdims=True))
            p = jnp.exp(s - m_new)
            alpha = jnp.exp(m - m_new)
            l = l*alpha + jnp.sum(p, axis=0, keepdims=True)
            vt = vt_ref[h*HD:(h+1)*HD, pl.ds(start, KB)]
            acc = acc*alpha + dot_nn(vt, p.astype(jnp.bfloat16))
            new.append((m_new, l, acc))
        return tuple(new)
    init = tuple((jnp.full((1,bq),-1e30,jnp.float32), jnp.zeros((1,bq),jnp.float32), jnp.zeros((HD,bq),jnp.float32)) for _ in range(heads))
    fin = lax.fori_loop(0, counts_ref[i], step, init)
    for h in range(heads):
        m, l, acc = fin[h]
        o_ref[h*HD:(h+1)*HD, :] = (acc/l).astype(jnp.bfloat16)
        lse_ref[h:h+1, :] = m + jnp.log(l)

def attend(counts, q_t, k, v, bq=256):
    width, rows = q_t.shape
    nk = k.shape[0]
    heads = width//HD
    return pl.pallas_call(
        functools.partial(attend_kernel, heads=heads),
        grid_spec=pltpu.PrefetchScalarGridSpec(
            num_scalar_prefetch=1, grid=(rows//bq,),
            in_specs=[pl.BlockSpec((width,bq), lambda i,c:(0,i)),
                      pl.BlockSpec((nk,width), lambda i,c:(0,0)),
                      pl.BlockSpec((nk,width), lambda i,c:(0,0))],
            out_specs=[pl.BlockSpec((width,bq), lambda i,c:(0,i)),
                       pl.BlockSpec((8,bq), lambda i,c:(0,i))],
            scratch_shapes=[pltpu.VMEM((width,nk), jnp.bfloat16)]),
        out_shape=(jax.ShapeDtypeStruct((width,rows),jnp.bfloat16), jax.ShapeDtypeStruct((8,rows),jnp.float32)),
        compiler_params=pltpu.CompilerParams(dimension_semantics=("arbitrary",), vmem_limit_bytes=40<<20),
        name="attend",
    )(counts, q_t, k, v)

def attend_back_kernel(counts_ref, q_ref, g_ref, o_ref, lse_ref, k_ref, v_ref, dq_ref, dkv_ref, kt_ref, dka_ref, dva_ref, *, heads):
    i = pl.program_id(0)
    nk = k_ref.shape[0]//KB
    bq = q_ref.shape[1]
    @pl.when(i == 0)
    def _():
        for j in range(nk):
            kt_ref[:, j*KB:(j+1)*KB] = k_ref[j*KB:(j+1)*KB, :].T
        dka_ref[...] = jnp.zeros_like(dka_ref)
        dva_ref[...] = jnp.zeros_like(dva_ref)
    q = q_ref[...]
    g = g_ref[...]
    prod = g.astype(jnp.float32)*o_ref[...].astype(jnp.float32)
    qm = [head_masked(q, h) for h in range(heads)]
    gm = [head_masked(g, h) for h in range(heads)]
    delta = [jnp.sum(prod[h*HD:(h+1)*HD], axis=0, keepdims=True) for h in range(heads)]
    lse = [lse_ref[h:h+1, :] for h in range(heads)]
    def step(j, carry):
        start = pl.multiple_of(j*KB, KB)
        kj = k_ref[pl.ds(start, KB), :]
        vj = v_ref[pl.ds(start, KB), :]
        new = []
        for h in range(heads):
            lo, hi = h*HD, (h+1)*HD
            p = jnp.exp(dot_nn(kj, qm[h]) - lse[h])
            dp = dot_nn(vj, gm[h])
            ds = (p*(dp - delta[h])).astype(jnp.bfloat16)
            dva_ref[lo:hi, pl.ds(start, KB)] += dot_nt(g[lo:hi], p.astype(jnp.bfloat16))
            dka_ref[lo:hi, pl.ds(start, KB)] += dot_nt(q[lo:hi], ds)
            new.append(carry[h] + dot_nn(kt_ref[lo:hi, pl.ds(start, KB)], ds))
        return tuple(new)
    fin = lax.fori_loop(0, counts_ref[i], step, tuple(jnp.zeros((HD,bq),jnp.float32) for _ in range(heads)))
    for h in range(heads):
        dq_ref[h*HD:(h+1)*HD, :] = (fin[h] * HD**-0.5).astype(jnp.bfloat16)
    @pl.when(i == pl.num_programs(0)-1)
    def _():
        dkv_ref[:heads*HD, :] = dka_ref[...].astype(jnp.bfloat16)
        dkv_ref[heads*HD:, :] = dva_ref[...].astype(jnp.bfloat16)

def attend_back(counts, q_t, g_t, o_t, lse, k, v, bq=256):
    width, rows = q_t.shape
    nk = k.shape[0]
    heads = width//HD
    per = pl.BlockSpec((width,bq), lambda i,c:(0,i))
    whole = pl.BlockSpec((nk,width), lambda i,c:(0,0))
    wide = pl.BlockSpec((2*width,nk), lambda i,c:(0,0))
    return pl.pallas_call(
        functools.partial(attend_back_kernel, heads=heads),
        grid_spec=pltpu.PrefetchScalarGridSpec(
            num_scalar_prefetch=1, grid=(rows//bq,),
            in_specs=[per,per,per,pl.BlockSpec((8,bq), lambda i,c:(0,i)),whole,whole],
            out_specs=[per,wide],
            scratch_shapes=[pltpu.VMEM((width,nk), jnp.bfloat16),pltpu.VMEM((width,nk), jnp.float32),pltpu.VMEM((width,nk), jnp.float32)]),
        out_shape=(jax.ShapeDtypeStruct((width,rows),jnp.bfloat16),)+(jax.ShapeDtypeStruct((2*width,nk),jnp.bfloat16),),
        compiler_params=pltpu.CompilerParams(dimension_semantics=("arbitrary",), vmem_limit_bytes=48<<20),
        name="attend_back",
    )(counts, q_t, g_t, o_t, lse, k, v)


from jax.sharding import Mesh, PartitionSpec as P

D = 768
H = 12
FF = 3072
BLOCK = 256
norm_epsilon = 1e-05
root_half = 0.7071067811865476
density_factor = 0.3989422804014327
DP = ("outer", "mid", "core")
EVERY = ("outer", "mid", "core", "tensor")


def dot_tn(former, latter):
    return lax.dot_general(former, latter, (((0,), (0,)), ((), ())), preferred_element_type=jnp.float32)


def dot_tt(former, latter):
    return lax.dot_general(former, latter, (((0,), (1,)), ((), ())), preferred_element_type=jnp.float32)


def normed_of(summed):
    centered = summed - jnp.mean(summed, axis=-1, keepdims=True)
    inverse = lax.rsqrt(jnp.mean(centered * centered, axis=-1, keepdims=True) + norm_epsilon)
    return centered * inverse, inverse


def layer_norm(summed, norm_gain, norm_shift):
    return normed_of(summed)[0] * norm_gain + norm_shift


def layer_norm_back(upstream, summed, norm_gain):
    normed, inverse = normed_of(summed)
    scaled = upstream * norm_gain
    through = inverse * (
        scaled
        - jnp.mean(scaled, axis=-1, keepdims=True)
        - normed * jnp.mean(scaled * normed, axis=-1, keepdims=True)
    )
    return (through, jnp.sum(upstream * normed, axis=0), jnp.sum(upstream, axis=0))


def units_kernel(x_ref, up_ref, down_ref, bias_ref, active_ref, slope_ref, out_ref, acc_ref):
    i = pl.program_id(0)
    before = dot_nn(x_ref[...], up_ref[0]) + bias_ref[...]
    chance = 0.5 * (1.0 + lax.erf(before * root_half))
    active = (before * chance).astype(jnp.bfloat16)
    active_ref[...] = active
    slope_ref[...] = (chance + before * density_factor * jnp.exp(-0.5 * before * before)).astype(jnp.bfloat16)
    part = dot_nt(active, down_ref[0])

    @pl.when(i == 0)
    def _():
        acc_ref[...] = part

    @pl.when(i > 0)
    def _():
        acc_ref[...] += part

    @pl.when(i == pl.num_programs(0) - 1)
    def _():
        out_ref[...] = acc_ref[...]


def units(x, both, bias):
    rows, width = x.shape
    count = both.shape[0]
    local = both.shape[2] // 2
    cols = pl.BlockSpec((rows, local), lambda i: (0, i))
    return pl.pallas_call(
        units_kernel,
        grid=(count,),
        in_specs=[pl.BlockSpec((rows, width), lambda i: (0, 0)),
                  pl.BlockSpec((1, width, local), lambda i: (i, 0, 0)),
                  pl.BlockSpec((1, width, local), lambda i: (i, 0, 1)),
                  pl.BlockSpec((1, local), lambda i: (0, i))],
        out_specs=[cols, cols, pl.BlockSpec((rows, width), lambda i: (0, 0))],
        scratch_shapes=[pltpu.VMEM((rows, width), jnp.float32)],
        out_shape=(jax.ShapeDtypeStruct((rows, count * local), jnp.bfloat16),) * 2
        + (jax.ShapeDtypeStruct((rows, width), jnp.float32),),
        compiler_params=pltpu.CompilerParams(dimension_semantics=("arbitrary",), vmem_limit_bytes=40 << 20),
        name="units",
    )(x, both, both, bias)


def units_back_kernel(g_ref, up_ref, down_ref, slope_ref, grad_ref, sums_ref, out_ref, acc_ref):
    i = pl.program_id(0)
    grad = (dot_nn(g_ref[...], down_ref[0]) * slope_ref[...].astype(jnp.float32)).astype(jnp.bfloat16)
    grad_ref[...] = grad
    sums_ref[...] = jnp.sum(grad.astype(jnp.float32), axis=0, keepdims=True)
    part = dot_nt(grad, up_ref[0])

    @pl.when(i == 0)
    def _():
        acc_ref[...] = part

    @pl.when(i > 0)
    def _():
        acc_ref[...] += part

    @pl.when(i == pl.num_programs(0) - 1)
    def _():
        out_ref[...] = acc_ref[...]


def units_back(g, both, slope):
    rows, width = g.shape
    count = both.shape[0]
    local = both.shape[2] // 2
    cols = pl.BlockSpec((rows, local), lambda i: (0, i))
    return pl.pallas_call(
        units_back_kernel,
        grid=(count,),
        in_specs=[pl.BlockSpec((rows, width), lambda i: (0, 0)),
                  pl.BlockSpec((1, width, local), lambda i: (i, 0, 0)),
                  pl.BlockSpec((1, width, local), lambda i: (i, 0, 1)),
                  cols],
        out_specs=[cols, pl.BlockSpec((1, local), lambda i: (0, i)), pl.BlockSpec((rows, width), lambda i: (0, 0))],
        scratch_shapes=[pltpu.VMEM((rows, width), jnp.float32)],
        out_shape=(jax.ShapeDtypeStruct((rows, count * local), jnp.bfloat16),
                   jax.ShapeDtypeStruct((1, count * local), jnp.float32),
                   jax.ShapeDtypeStruct((rows, width), jnp.float32)),
        compiler_params=pltpu.CompilerParams(dimension_semantics=("arbitrary",), vmem_limit_bytes=40 << 20),
        name="units_back",
    )(g, both, both, slope)


def swapped(x, axis):
    return lax.ppermute(x, axis, [(0, 1), (1, 0)])


def gather_axis(x, axis):
    if lax.axis_size(axis) != 2:
        return lax.all_gather(x, axis, axis=0)
    other = swapped(x, axis)
    first = lax.axis_index(axis) == 0
    return jnp.stack([jnp.where(first, x, other), jnp.where(first, other, x)])


def gather_over(x, axes):
    for axis in axes:
        x = gather_axis(x, axis)
    return x


def shifted(piece, step):
    count = lax.axis_size("tensor")
    return lax.ppermute(piece, "tensor", [(i, (i + step) % count) for i in range(count)])


def exchange(take, put, start):
    count = lax.axis_size("tensor")
    rank = lax.axis_index("tensor")
    got = [(shifted(take((rank + s) % count), s), (rank - s) % count) for s in range(1, count)]
    out = put(start, take(rank), rank)
    for piece, source in got:
        out = put(out, piece, source)
    return out


def tokens_to_heads(whole):
    count = lax.axis_size("tensor")
    width = whole.shape[0] // count
    own = whole.shape[1]
    return exchange(
        lambda d: lax.dynamic_slice_in_dim(whole, d * width, width, 0),
        lambda out, piece, s: lax.dynamic_update_slice_in_dim(out, piece, s * own, 1),
        jnp.zeros((width, count * own), whole.dtype),
    )


def heads_to_tokens(mine):
    count = lax.axis_size("tensor")
    width = mine.shape[0]
    own = mine.shape[1] // count
    return exchange(
        lambda d: lax.dynamic_slice_in_dim(mine, d * own, own, 1),
        lambda out, piece, s: lax.dynamic_update_slice_in_dim(out, piece, s * width, 0),
        jnp.zeros((count * width, own), mine.dtype),
    )


def gather_tokens(mine):
    count = lax.axis_size("tensor")
    rank = lax.axis_index("tensor")
    own = mine.shape[0]
    out = jnp.zeros((count * own,) + mine.shape[1:], mine.dtype)
    got = [(shifted(mine, s), (rank - s) % count) for s in range(1, count)]
    out = lax.dynamic_update_slice_in_dim(out, mine, rank * own, 0)
    for piece, source in got:
        out = lax.dynamic_update_slice_in_dim(out, piece, source * own, 0)
    return out


def reduce_columns(partial):
    count = lax.axis_size("tensor")
    rank = lax.axis_index("tensor")
    width = partial.shape[1] // count

    def take(d):
        return lax.dynamic_slice_in_dim(partial, d * width, width, 1)

    total = take(rank).astype(jnp.float32)
    for s in range(1, count):
        total = total + shifted(take((rank + s) % count), s).astype(jnp.float32)
    return total


def reduce_rows(partial):
    return lax.psum_scatter(partial, DP, scatter_dimension=0, tiled=True)


def body(
    inputs,
    encoder_out,
    block_ids,
    out_grad,
    in_weight,
    out_weight,
    up_weight,
    down_weight,
    vectors,
    norm_gains,
    up_bias,
):
    low = jnp.bfloat16
    tensor_count = lax.axis_size("tensor")
    tensor_rank = lax.axis_index("tensor")
    width = D // tensor_count
    scale = HD ** (-0.5)
    start = tensor_rank * width
    rows = inputs[0]
    ids = block_ids[0]

    in_low = in_weight.astype(low)
    shards = in_low.shape[1]
    hidden_self = lax.all_gather(rows, "tensor", axis=0, tiled=True)
    head_pack = jnp.concatenate([in_low[0], in_low[1], in_low[2], in_low[4], in_low[5]], axis=1)
    head_pack = gather_over(head_pack, ("core", "mid", "outer")).reshape(D, 5 * width)
    w_self = head_pack[:, : 3 * width]
    w_cross = head_pack[:, 3 * width :]
    out_turned = jnp.swapaxes(out_weight.astype(low), 1, 2)
    mid_pack = jnp.concatenate([in_low[3], out_turned[0], out_turned[1]], axis=1)
    mid_pack = gather_over(gather_tokens(mid_pack).reshape(tensor_count, shards, 3 * width), ("core", "mid", "outer"))
    mid_pack = mid_pack.reshape(D // shards, tensor_count, shards, 3 * width)
    mid_pack = jnp.swapaxes(mid_pack, 0, 1).reshape(tensor_count, D, 3, width)
    turned = jnp.transpose(mid_pack, (2, 0, 3, 1)).reshape(3, D, D)
    wq_cross_t, wo_self, wo_cross = turned[0], turned[1], turned[2]
    unit_pack = jnp.concatenate([up_weight.astype(low), down_weight.astype(low).T], axis=1)
    unit_pack = lax.all_gather(unit_pack, ("tensor",) + DP, axis=0, tiled=True).reshape(tensor_count, D, -1)
    encoder_full = gather_tokens(encoder_out[0])

    head_bias = lax.dynamic_slice_in_dim(vectors[0:4], start, width, 1)
    counts_self = jnp.sum((ids[None, :] <= ids[:, None]).astype(jnp.int32), axis=1)
    counts_cross = jnp.full(ids.shape, encoder_full.shape[0] // KB, jnp.int32)

    q_self = ((dot_tt(w_self[:, :width], hidden_self) + head_bias[0][:, None]) * scale).astype(low)
    k_self = dot_nn(hidden_self, w_self[:, width : 2 * width]).astype(low)
    v_self = (dot_nn(hidden_self, w_self[:, 2 * width :]) + head_bias[1]).astype(low)
    mine_self, lse_self = attend(counts_self, q_self, k_self, v_self)
    k_cross = dot_nn(encoder_full, w_cross[:, :width]).astype(low)
    v_cross = (dot_nn(encoder_full, w_cross[:, width:]) + head_bias[3]).astype(low)
    mixed_self = heads_to_tokens(mine_self)
    summed_one = rows.astype(jnp.float32) + (dot_tn(mixed_self, wo_self) + vectors[4])
    normed_one = layer_norm(summed_one, norm_gains[0], vectors[7])
    hidden_cross = normed_one.astype(low)
    q_cross = tokens_to_heads(((dot_nt(wq_cross_t, hidden_cross) + vectors[2][:, None]) * scale).astype(low))
    mine_cross, lse_cross = attend(counts_cross, q_cross, k_cross, v_cross)
    mixed_cross = heads_to_tokens(mine_cross)
    summed_two = normed_one + (dot_tn(mixed_cross, wo_cross) + vectors[5])
    normed_two = layer_norm(summed_two, norm_gains[1], vectors[8])
    hidden_units = normed_two.astype(low)
    active, slope, unit_out = units(hidden_units, unit_pack, up_bias[None])
    summed_three = normed_two + (unit_out + vectors[6])
    layer_out = layer_norm(summed_three, norm_gains[2], vectors[9]).astype(low)

    grad_three, gain_three, shift_three = layer_norm_back(out_grad[0].astype(jnp.float32), summed_three, norm_gains[2])
    branch_three = grad_three.astype(low)
    bias_down = jnp.sum(branch_three.astype(jnp.float32), axis=0)
    grad_before, unit_bias, unit_back = units_back(branch_three, unit_pack, slope)
    down_grad = reduce_rows(dot_tn(branch_three, active).astype(low))
    up_grad = reduce_rows(dot_tn(hidden_units, grad_before).astype(low))
    grad_two, gain_two, shift_two = layer_norm_back(grad_three + unit_back, summed_two, norm_gains[1])
    branch_two = grad_two.astype(low)
    bias_cross_out = jnp.sum(branch_two.astype(jnp.float32), axis=0)
    grad_mixed_cross = tokens_to_heads(dot_nt(wo_cross, branch_two).astype(low))
    out_grad_cross = reduce_rows(dot_tt(branch_two, mixed_cross).astype(low))
    dq_mine, dkv_cross = attend_back(
        counts_cross, q_cross, grad_mixed_cross, mine_cross, lse_cross, k_cross, v_cross)
    dq_cross = heads_to_tokens(dq_mine)
    kv_grad = reduce_rows(dot_tt(encoder_full, dkv_cross).astype(low))
    encoder_grad = lax.psum_scatter(
        dot_tt(dkv_cross, w_cross).astype(low), "tensor", scatter_dimension=0, tiled=True).astype(jnp.float32)
    bias_query_cross = jnp.sum(dq_cross.astype(jnp.float32), axis=1)
    bias_value_cross = jnp.sum(dkv_cross[width:].astype(jnp.float32), axis=1)
    query_grad_cross = reduce_rows(dot_tt(hidden_cross, dq_cross).astype(low))
    grad_one_in = grad_two + dot_tn(dq_cross, wq_cross_t)
    grad_one, gain_one, shift_one = layer_norm_back(grad_one_in, summed_one, norm_gains[0])
    branch_one = grad_one.astype(low)
    bias_self_out = jnp.sum(branch_one.astype(jnp.float32), axis=0)
    grad_mixed_self = tokens_to_heads(dot_nt(wo_self, branch_one).astype(low))
    out_grad_self = reduce_rows(dot_tt(branch_one, mixed_self).astype(low))
    dq_self, dkv_self = attend_back(
        counts_self, q_self, grad_mixed_self, mine_self, lse_self, k_self, v_self)
    dqkv = jnp.concatenate([dq_self, dkv_self], axis=0)
    input_part = dot_tt(dqkv, w_self).astype(low)
    input_grad = grad_one + lax.psum_scatter(
        input_part, "tensor", scatter_dimension=0, tiled=True).astype(jnp.float32)
    self_grad = reduce_rows(dot_tt(hidden_self, dqkv).astype(low)).astype(jnp.float32)
    bias_query_self = jnp.sum(dq_self.astype(jnp.float32), axis=1)
    bias_value_self = jnp.sum(dkv_self[width:].astype(jnp.float32), axis=1)

    kv_grad = kv_grad.astype(jnp.float32)
    mid_grads = [reduce_columns(g) for g in (query_grad_cross, out_grad_self, out_grad_cross)]
    up_shard = reduce_columns(up_grad)
    down_shard = reduce_columns(down_grad).T
    in_shard = jnp.stack([
        self_grad[:, :width], self_grad[:, width : 2 * width], self_grad[:, 2 * width :],
        mid_grads[0], kv_grad[:, :width], kv_grad[:, width:]])
    out_shard = jnp.stack([mid_grads[1].T, mid_grads[2].T])

    def embed(part):
        return lax.dynamic_update_slice_in_dim(jnp.zeros((D,), jnp.float32), part, start, 0)

    vector_grad = jnp.stack([
        embed(bias_query_self), embed(bias_value_self), bias_query_cross, embed(bias_value_cross),
        bias_self_out, bias_cross_out, bias_down, shift_one, shift_two, shift_three])
    gain_grad = jnp.stack([gain_one, gain_two, gain_three])
    vector_total, gain_total, unit_total = lax.psum((vector_grad, gain_grad, unit_bias[0]), EVERY)
    return (
        layer_out[None],
        input_grad[None],
        encoder_grad[None],
        in_shard,
        out_shard,
        up_shard,
        down_shard,
        vector_total,
        gain_total,
        unit_total,
    )


def solution(mesh):
    devices = mesh.devices
    wide = Mesh(devices.reshape(devices.shape[0] // 4, 2, 2, devices.shape[1]), EVERY)
    return jax.shard_map(
        body,
        mesh=wide,
        in_specs=(
            P(DP, "tensor", None),
            P(DP, "tensor", None),
            P(DP, None),
            P(DP, "tensor", None),
            P(None, DP, "tensor"),
            P(None, "tensor", DP),
            P(DP, "tensor"),
            P("tensor", DP),
            P(),
            P(),
            P(),
        ),
        out_specs=(
            P(DP, "tensor", None),
            P(DP, "tensor", None),
            P(DP, "tensor", None),
            P(None, DP, "tensor"),
            P(None, "tensor", DP),
            P(DP, "tensor"),
            P("tensor", DP),
            P(),
            P(),
            P(),
        ),
        check_vma=False,
    )
```

time: 1430 us -> 846 us (0.59)
  waiting for transfers between devices: 880 us -> 349 us
  matrix products: 282 us -> 52.7 us
  Pallas kernels: 0 us -> 164 us
  starting transfers between devices: 1.83 us -> 115 us
  other arithmetic: 112 us -> 36.8 us
  local copies, waits for them, and re-layouts: 77.8 us -> 58.2 us
    all_gather x10 -> x2, waiting for transfers between devices: 444 us -> 0.01 us  [the longest x1 0.01 us: body(): lax.all_gather(unit_pack, ('tensor',) + DP, axis=0, tiled=True)]
    reduce_scatter x9 -> x6, waiting for transfers between devices: 434 us -> 196 us  [the longest x4 110 us: reduce_rows(): return lax.psum_scatter(partial, DP, scatter_dimension=0, tiled=True)]
    dot_general x86 -> x20, matrix products: 282 us -> 52.7 us  [the longest x8 25.2 us: dot_tt(): lax.dot_general(former, latter, (((0,), (1,)), ((), ())), preferred_eleme...]
    pallas_call x0 -> x6, Pallas kernels: none -> 164 us  [the longest x2 72.4 us: attend(): pl.pallas_call(functools.partial(attend_kernel, heads=heads), grid_spec=p...]
    ppermute x0 -> x45, waiting for transfers between devices: none -> 125 us  [the longest x39 92.1 us: shifted(): lax.ppermute(piece, 'tensor', [(i, (i + step) % count) for i in range(cou...]
    ppermute x0 -> x45, starting transfers between devices: none -> 115 us  [the longest x39 109 us: shifted(): lax.ppermute(piece, 'tensor', [(i, (i + step) % count) for i in range(cou...]
    reduce_sum x18 -> x9, other arithmetic: 47.2 us -> 4.59 us  [the longest x1 1.32 us: body(): bias_value_self = jnp.sum(dkv_self[width:].astype(jnp.float32), axis=1)]
    convert_element_type x15 -> x5, other arithmetic: 38 us -> 2.24 us  [the longest x1 1.19 us: body(): hidden_units = normed_two.astype(low)]
  transfers between devices with their start and end apart: 21 -> 56, of which waited for: 18 -> 30; matrix products, arithmetic and copies ran while one was open for 17% -> 15% of each run, Pallas kernels for 0% -> 14%
where the time goes in v1:
time: 846 us; the launch traced here: 834 us
  waiting for transfers between devices  349 us (41%)
  Pallas kernels  164 us (19%)
  starting transfers between devices  115 us (14%)
  local copies, waits for them, and re-layouts  58.2 us (7%)
  matrix products  52.7 us (6%)
  blocking collectives  42.2 us (5%)
  other arithmetic  36.8 us (4%)
  between operations  16 us (2%)
    reduce_scatter x4, waiting for transfers between devices, reduce_rows(): return lax.psum_scatter(partial, DP, scatter_dimension=0, tiled=True)  110 us
    ppermute x39, starting transfers between devices, shifted(): lax.ppermute(piece, 'tensor', [(i, (i + step) % count) for i in range(cou...  109 us
    ppermute x39, waiting for transfers between devices, shifted(): lax.ppermute(piece, 'tensor', [(i, (i + step) % count) for i in range(cou...  92.1 us
    pallas_call x2, Pallas kernels, attend(): pl.pallas_call(functools.partial(attend_kernel, heads=heads), grid_spec=p...  72.4 us
    pallas_call x2, Pallas kernels, attend_back(): pl.pallas_call(functools.partial(attend_back_kernel, heads=heads), grid_s...  72.4 us
    reduce_scatter x1, waiting for transfers between devices, body(): lax.psum_scatter(input_part, 'tensor', scatter_dimension=0, tiled=True)  60 us
    psum x1, blocking collectives, body(): lax.psum((vector_grad, gain_grad, unit_bias[0]), EVERY)  42.2 us
    ppermute x6, waiting for transfers between devices, swapped(): return lax.ppermute(x, axis, [(0, 1), (1, 0)])  33.4 us
  transfers between devices with their start and end apart: 56, of which 30 were waited for; matrix products, arithmetic and copies ran while one was open for 15% of the time, Pallas kernels for 14%

profile of v1, /device:TPU:0, one launch (start us, length us, event | category | flops | bytes accessed | tf_op | source)
XLA Modules:
  0.0 833.8 jit_solution(17918427756130705744)
XLA Ops:
  11.1 3.1 collective-permute-start.6
  14.2 2.6 collective-permute-start.7
  18.2 2.4 collective-permute-done.6
  20.5 7.1 collective-permute-done.7
  31.4 9.9 %collective-permute-start.15 = (bf16[256,768]{1,0:T(8,128)(2,1)}, bf16[256,768]{1,0:T(8,128)(2,1)}, u32[]{:S(2)}, u32[]{:S(2)}) collective-permute-start(bf16[256,768]{1,0:T(8,128)(2,1)} %bitcast.35), channel_id=1, source_target_pairs={{0,1},{1,2},{2,3},{3,0},{4,5},{5,6},{6,7},{7,4},{8,9},{9,10},{10,1... | collective-permute-start | bytes 1179656 | tf_op jit(solution)/shard_map/ppermute | solution.py:272
  41.3 4.4 collective-permute-start.16
  48.2 6.4 collective-permute-done.10
  59.3 2.9 collective-permute-done.1
  68.8 23.8 %collective-permute-done.16 = bf16[256,768]{1,0:T(8,128)(2,1)} collective-permute-done((bf16[256,768]{1,0:T(8,128)(2,1)}, bf16[256,768]{1,0:T(8,128)(2,1)}, u32[]{:S(2)}, u32[]{:S(2)}) %collective-permute-start.16) | collective-permute-done | bytes 393248 | tf_op jit(solution)/shard_map/ppermute | solution.py:272
  96.1 21.9 %collective-permute-done.2 = bf16[2,2,96,960]{3,2,1,0:T(8,128)(2,1)} collective-permute-done((bf16[2,2,96,960]{3,2,1,0:T(8,128)(2,1)S(1)}, bf16[2,2,96,960]{3,2,1,0:T(8,128)(2,1)}, u32[]{:S(2)}, u32[]{:S(2)}) %collective-permute-start.2) | collective-permute-done | bytes 737312 | tf_op jit(solution)/shard_map/ppermute | solution.py:253
  121.9 2.2 select_bitcast_fusion.1
  124.1 2.6 pad_maximum_fusion
  126.7 8.3 %copy.64 = bf16[8,4,96,576]{2,0,3,1:T(8,128)(2,1)} copy(bf16[8,4,96,576]{3,2,1,0:T(8,128)(2,1)} %bitcast.204) | data formatting | bytes 7077888 | tf_op jit(solution)/shard_map/reshape | solution.py:369
  135.0 8.2 reshape.115
  143.3 3.5 fusion.20
  147.5 3.4 fusion.23.q_ref
  152.0 40.1 %attend.2 = (bf16[192,2048]{1,0:T(8,128)(2,1)S(1)}, f32[8,2048]{1,0:T(8,128)S(1)}) custom-call(s32[8]{0:T(128)S(1)} %convert_reduce_fusion.8.counts_ref, bf16[192,2048]{1,0:T(8,128)(2,1)S(1)} %fusion.23.q_ref, bf16[2048,192]{1,0:T(8,128)(2,1)S(1)} %bitcast.195, bf16[2048,192]{1,0:T(8,128)(2,1)S(1)} %fusion.26.v_ref), custom_call_target="tpu_custom_call" | custom-call | tf_op jit(solution)/shard_map/attend/pallas_call | solution.py:51
  192.3 11.0 %collective-permute-start.3 = (bf16[192,512]{1,0:T(8,128)(2,1)S(1)}, bf16[192,512]{1,0:T(8,128)(2,1)S(1)}, u32[]{:S(2)}, u32[]{:S(2)}) collective-permute-start(bf16[192,512]{1,0:T(8,128)(2,1)S(1)} %get-tuple-element.157), channel_id=1, source_target_pairs={{0,1},{1,2},{2,3},{3,0},{4,5},{5,6},{6,7},{7,4},{8,9},{9,10},{10,1... | collective-permute-start | bytes 589832 | tf_op jit(solution)/shard_map/ppermute | solution.py:272
  203.2 5.5 collective-permute-start.4
  209.1 11.6 %collective-permute-start.5 = (bf16[192,512]{1,0:T(8,128)(2,1)S(1)}, bf16[192,512]{1,0:T(8,128)(2,1)S(1)}, u32[]{:S(2)}, u32[]{:S(2)}) collective-permute-start(bf16[192,512]{1,0:T(8,128)(2,1)S(1)} %get-tuple-element.155), channel_id=1, source_target_pairs={{0,3},{1,0},{2,1},{3,2},{4,7},{5,4},{6,5},{7,6},{8,11},{9,8},{10,9... | collective-permute-start | bytes 589832 | tf_op jit(solution)/shard_map/ppermute | solution.py:272
  220.7 5.6 collective-permute-done.5
  229.3 2.7 collective-permute-start.13
  233.8 3.0 collective-permute-done.12
  236.8 4.4 collective-permute-done.13
  241.3 32.3 %attend.3 = (bf16[192,2048]{1,0:T(8,128)(2,1)S(1)}, f32[8,2048]{1,0:T(8,128)S(1)}) custom-call(s32[8]{0:T(128)S(1)} %broadcast_11_counts_ref.2.counts_ref, bf16[192,2048]{1,0:T(8,128)(2,1)S(1)} %constant_dynamic-update-slice_fusion.16.q_ref, bf16[1024,192]{1,0:T(8,128)(2,1)S(1)} %convolution_convert_fusion.10.k_ref, bf16[1024,192]{1,0:T(8,128)(2,1)S(1)} %fusion.46.v_ref), custom_call_target="tpu_custom_call" | custom-call | tf_op jit(solution)/shard_map/attend/pallas_call | solution.py:51
  273.8 2.7 collective-permute-start.18
  279.0 4.6 collective-permute-done.18
  283.6 5.2 collective-permute-done.19
  293.6 10.1 %units.1 = (bf16[512,3072]{1,0:T(8,128)(2,1)S(1)}, bf16[512,3072]{1,0:T(8,128)(2,1)S(1)}, f32[512,768]{1,0:T(8,128)S(1)}) custom-call(bf16[512,768]{1,0:T(8,128)(2,1)S(1)} %copy-done, bf16[4,768,1536]{2,1,0:T(8,128)(2,1)} %bitcast.199, bf16[4,768,1536]{2,1,0:T(8,128)(2,1)} %bitcast.200, f32[1,3072]{1,0:T(1,128)S(1)} %bitcast.197), custom_call_target="tpu_custom_call" | custom-call | tf_op jit(solution)/shard_map/units/pallas_call | solution.py:194
  308.9 9.0 %units_back.1 = (bf16[512,3072]{1,0:T(8,128)(2,1)S(1)}, f32[1,3072]{1,0:T(1,128)S(1)}, f32[512,768]{1,0:T(8,128)S(1)}) custom-call(bf16[512,768]{1,0:T(8,128)(2,1)S(1)} %get-tuple-element.113.g_ref, bf16[4,768,1536]{2,1,0:T(8,128)(2,1)} %bitcast.201, bf16[4,768,1536]{2,1,0:T(8,128)(2,1)} %bitcast.202, bf16[512,3072]{1,0:T(8,128)(2,1)S(1)} %get-tuple-element.27.slope_ref), custom_call_target="tpu_custom_call" | custom-call | tf_op jit(solution)/shard_map/units_back/pallas_call | solution.py:235
  318.0 2.8 multiply_reduce_fusion
  323.0 4.7 collective-permute-start.21
  330.1 2.9 collective-permute-done.21
  333.0 7.1 collective-permute-done.22
  340.6 31.4 %attend_back.2 = (bf16[192,2048]{1,0:T(8,128)(2,1)S(1)}, bf16[384,1024]{1,0:T(8,128)(2,1)S(1)}) custom-call(s32[8]{0:T(128)S(1)} %copy-done.19, bf16[192,2048]{1,0:T(8,128)(2,1)S(1)} %constant_dynamic-update-slice_fusion.16.q_ref, bf16[192,2048]{1,0:T(8,128)(2,1)S(1)} %constant_dynamic-update-slice_fusion.6.g_ref, bf16[192,2048]{1,0:T(8,128)(2,1)S(1)} %copy-done.11, ...), custom_call_target="tpu_custom_call" | custom-call | tf_op jit(solution)/shard_map/attend_back/pallas_call | solution.py:112
  373.0 4.5 collective-permute-start.24
  377.5 3.4 collective-permute-start.25
  383.3 3.1 collective-permute-done.24
  386.4 7.2 collective-permute-done.25
  394.0 4.5 multiply_reduce_fusion.1
  402.6 4.4 collective-permute-start.27
  408.9 2.4 collective-permute-start.29
  413.3 6.3 collective-permute-done.28
  421.1 41.0 %attend_back.3 = (bf16[192,2048]{1,0:T(8,128)(2,1)S(1)}, bf16[384,2048]{1,0:T(8,128)(2,1)}) custom-call(s32[8]{0:T(128)S(1)} %convert_reduce_fusion.8.counts_ref, bf16[192,2048]{1,0:T(8,128)(2,1)S(1)} %copy-done.7, bf16[192,2048]{1,0:T(8,128)(2,1)} %constant_dynamic-update-slice_fusion.g_ref, bf16[192,2048]{1,0:T(8,128)(2,1)S(1)} %copy-done.5, ...), custom_call_target="tpu_custom_call" | custom-call | tf_op jit(solution)/shard_map/attend_back/pallas_call | solution.py:112
  466.5 2.9 fusion.43
  469.4 2.4 copy.74
  473.9 3.5 convolution_convert_fusion.6
  477.5 3.5 convolution_convert_fusion.3
  481.1 6.3 convolution_convert_fusion
  487.7 6.3 convolution_convert_fusion.2
  495.2 6.3 convolution_convert_fusion.1
  507.3 5.0 collective-permute-start.36
  512.2 3.4 collective-permute-start.37
  516.3 42.2 %all-reduce = (f32[10,768]{1,0:T(8,128)}, f32[3,768]{1,0:T(4,128)}, f32[3072]{0:T(1024)}) all-reduce(f32[10,768]{1,0:T(8,128)S(1)} %stack.170, f32[3,768]{1,0:T(4,128)S(1)} %pad_maximum_fusion.9, f32[3072]{0:T(1024)S(1)} %bitcast.198), channel_id=1, replica_groups=mesh['outer'=2,'mid'=2,'core'=2,'tensor'=4] {'outer','mid','core','tensor'}, use_global_device_ids=true, to_apply=%region_32.33 | all-reduce | flops 13056 | bytes 104448 | tf_op jit(solution)/shard_map/psum | solution.py:453
  566.7 25.8 %reduce-scatter.30.cloned.1.call-done = bf16[96,768]{1,0:T(8,128)(2,1)} async-done(((bf16[768,768]{1,0:T(8,128)(2,1)}), bf16[96,768]{1,0:T(8,128)(2,1)}) %reduce-scatter.30.cloned.1.call-update) | async-done | bytes 147472
  595.4 2.5 collective-permute-start.31
  603.4 26.9 %reduce-scatter.18.cloned.1.call-done = bf16[256,768]{1,0:T(8,128)(2,1)} async-done(((bf16[1024,768]{1,0:T(8,128)(2,1)}), bf16[256,768]{1,0:T(8,128)(2,1)}) %reduce-scatter.18.cloned.1.call-update) | async-done | bytes 393232 | tf_op jit(solution)/shard_map/reduce_scatter | solution.py:416
  632.2 54.2 %reduce-scatter.26.cloned.1.call-done = bf16[96,3072]{1,0:T(8,128)(2,1)} async-done(((bf16[768,3072]{1,0:T(8,128)(2,1)}), bf16[96,3072]{1,0:T(8,128)(2,1)}) %reduce-scatter.26.cloned.1.call-update) | async-done | bytes 589840 | tf_op jit(solution)/shard_map/reduce_scatter | solution.py:334
  689.0 2.4 collective-permute-start.43
  692.9 60.0 %reduce-scatter.16.cloned.1.call-done = bf16[512,768]{1,0:T(8,128)(2,1)} async-done(((bf16[2048,768]{1,0:T(8,128)(2,1)}), bf16[512,768]{1,0:T(8,128)(2,1)}) %reduce-scatter.16.cloned.1.call-update) | async-done | bytes 786448 | tf_op jit(solution)/shard_map/reduce_scatter | solution.py:431
  752.9 2.4 add_bitcast_fusion
  755.3 55.3 %reduce-scatter.24.cloned.1.call-done = bf16[96,3072]{1,0:T(8,128)(2,1)} async-done(((bf16[768,3072]{1,0:T(8,128)(2,1)}), bf16[96,3072]{1,0:T(8,128)(2,1)}) %reduce-scatter.24.cloned.1.call-update) | async-done | bytes 589840 | tf_op jit(solution)/shard_map/reduce_scatter | solution.py:334
  813.3 2.4 collective-permute-start.40
  820.4 5.0 collective-permute-done.40
  (416 shorter events, 112.9 us)
Async XLA Ops:
  7.2 136.1 %all-gather.6.cloned.1.call-start = ((), (), s32[]{:S(2)}) async-start(), calls=%async_computation.16 | async-start | bytes 3932160 | tf_op jit(solution)/shard_map/all_gather | solution.py:361
  7.9 284.5 %all-gather.4.cloned.1.call-start = ((), (), s32[]{:S(2)}) async-start(), calls=%async_computation.9 | async-start | bytes 9732096 | tf_op jit(solution)/shard_map/all_gather | solution.py:374
  10.7 495.5 %reduce-scatter.22.cloned.1.call-start = ((), (), s32[]{:S(2)}) async-start(), calls=%async_computation.13 | async-start | bytes 1327104 | tf_op jit(solution)/shard_map/reduce_scatter | solution.py:334
  11.1 9.4 %collective-permute-start.6 = (bf16[96,576]{1,0:T(8,128)(2,1)S(1)}, bf16[96,576]{1,0:T(8,128)(2,1)S(1)}, u32[]{:S(2)}, u32[]{:S(2)}) collective-permute-start(bf16[96,576]{1,0:T(8,128)(2,1)S(1)} %get-tuple-element.122), channel_id=1, source_target_pairs={{0,1},{1,2},{2,3},{3,0},{4,5},{5,6},{6,7},{7,4},{8,9},{9,10},{10,1... | collective-permute-start | bytes 331784 | tf_op jit(solution)/shard_map/ppermute | solution.py:272
  14.2 13.4 %collective-permute-start.7 = (bf16[96,576]{1,0:T(8,128)(2,1)S(1)}, bf16[96,576]{1,0:T(8,128)(2,1)S(1)}, u32[]{:S(2)}, u32[]{:S(2)}) collective-permute-start(bf16[96,576]{1,0:T(8,128)(2,1)S(1)} %get-tuple-element.122), channel_id=1, source_target_pairs={{0,2},{1,3},{2,0},{3,1},{4,6},{5,7},{6,4},{7,5},{8,10},{9,11},{10,... | collective-permute-start | bytes 331784 | tf_op jit(solution)/shard_map/ppermute | solution.py:272
  16.8 10.8 %collective-permute-start.8 = (bf16[96,576]{1,0:T(8,128)(2,1)S(1)}, bf16[96,576]{1,0:T(8,128)(2,1)S(1)}, u32[]{:S(2)}, u32[]{:S(2)}) collective-permute-start(bf16[96,576]{1,0:T(8,128)(2,1)S(1)} %get-tuple-element.122), channel_id=1, source_target_pairs={{0,3},{1,0},{2,1},{3,2},{4,7},{5,4},{6,5},{7,6},{8,11},{9,8},{10,9... | collective-permute-start | bytes 331784 | tf_op jit(solution)/shard_map/ppermute | solution.py:272
  27.7 1.9 collective-permute-start.9
  29.9 24.8 %collective-permute-start.10 = (bf16[2,4,96,576]{3,2,1,0:T(8,128)(2,1)S(1)}, bf16[2,4,96,576]{3,2,1,0:T(8,128)(2,1)}, u32[]{:S(2)}, u32[]{:S(2)}) collective-permute-start(bf16[2,4,96,576]{3,2,1,0:T(8,128)(2,1)S(1)} %pad_maximum_fusion.3), channel_id=1, source_target_pairs={{0,8},{8,0},{1,9},{9,1},{2,10},{10,2},{3,11},{11,3},{4,12},{12,4},... | collective-permute-start | bytes 2654216 | tf_op jit(solution)/shard_map/ppermute | solution.py:253
  31.4 35.6 %collective-permute-start.15 = (bf16[256,768]{1,0:T(8,128)(2,1)}, bf16[256,768]{1,0:T(8,128)(2,1)}, u32[]{:S(2)}, u32[]{:S(2)}) collective-permute-start(bf16[256,768]{1,0:T(8,128)(2,1)} %bitcast.35), channel_id=1, source_target_pairs={{0,1},{1,2},{2,3},{3,0},{4,5},{5,6},{6,7},{7,4},{8,9},{9,10},{10,1... | collective-permute-start | bytes 1179656 | tf_op jit(solution)/shard_map/ppermute | solution.py:272
  41.3 51.3 %collective-permute-start.16 = (bf16[256,768]{1,0:T(8,128)(2,1)}, bf16[256,768]{1,0:T(8,128)(2,1)}, u32[]{:S(2)}, u32[]{:S(2)}) collective-permute-start(bf16[256,768]{1,0:T(8,128)(2,1)} %bitcast.35), channel_id=1, source_target_pairs={{0,2},{1,3},{2,0},{3,1},{4,6},{5,7},{6,4},{7,5},{8,10},{9,11},{10,... | collective-permute-start | bytes 1179656 | tf_op jit(solution)/shard_map/ppermute | solution.py:272
  45.7 48.7 %collective-permute-start.17 = (bf16[256,768]{1,0:T(8,128)(2,1)}, bf16[256,768]{1,0:T(8,128)(2,1)}, u32[]{:S(2)}, u32[]{:S(2)}) collective-permute-start(bf16[256,768]{1,0:T(8,128)(2,1)} %bitcast.35), channel_id=1, source_target_pairs={{0,3},{1,0},{2,1},{3,2},{4,7},{5,4},{6,5},{7,6},{8,11},{9,8},{10,9... | collective-permute-start | bytes 1179656 | tf_op jit(solution)/shard_map/ppermute | solution.py:272
  45.8 1.5 collective-permute-start
  47.4 14.8 %collective-permute-start.1 = (bf16[2,96,960]{2,1,0:T(8,128)(2,1)S(1)}, bf16[2,96,960]{2,1,0:T(8,128)(2,1)S(1)}, u32[]{:S(2)}, u32[]{:S(2)}) collective-permute-start(bf16[2,96,960]{2,1,0:T(8,128)(2,1)S(1)} %pad_maximum_fusion.5), channel_id=1, source_target_pairs={{0,8},{8,0},{1,9},{9,1},{2,10},{10,2},{3,11},{11,3},{4,12},{12,4},... | collective-permute-start | bytes 1105928 | tf_op jit(solution)/shard_map/ppermute | solution.py:253
  57.7 64.2 %collective-permute-start.11 = (bf16[2,2,4,96,576]{4,3,2,1,0:T(8,128)(2,1)}, bf16[2,2,4,96,576]{4,3,2,1,0:T(8,128)(2,1)}, u32[]{:S(2)}, u32[]{:S(2)}) collective-permute-start(bf16[2,2,4,96,576]{4,3,2,1,0:T(8,128)(2,1)} %pad_maximum_fusion.1), channel_id=1, source_target_pairs={{0,16},{16,0},{1,17},{17,1},{2,18},{18,2},{3,19},{19,3},{4,20},{20... | collective-permute-start | bytes 5308424 | tf_op jit(solution)/shard_map/ppermute | solution.py:253
  62.3 55.8 %collective-permute-start.2 = (bf16[2,2,96,960]{3,2,1,0:T(8,128)(2,1)S(1)}, bf16[2,2,96,960]{3,2,1,0:T(8,128)(2,1)}, u32[]{:S(2)}, u32[]{:S(2)}) collective-permute-start(bf16[2,2,96,960]{3,2,1,0:T(8,128)(2,1)S(1)} %pad_maximum_fusion.4), channel_id=1, source_target_pairs={{0,16},{16,0},{1,17},{17,1},{2,18},{18,2},{3,19},{19,3},{4,20},{20... | collective-permute-start | bytes 2211848 | tf_op jit(solution)/shard_map/ppermute | solution.py:253
  67.0 160.6 %copy-start.82 = (f32[768]{0:T(1024)}, f32[768]{0:T(1024)S(1)}, u32[]{:S(2)}) copy-start(f32[768]{0:T(1024)S(1)} %get-tuple-element.103) | copy-start | bytes 9220
  152.0 56.8 %copy-start.24 = (bf16[4,768,3,192]{1,3,2,0:T(8,128)(2,1)S(1)}, bf16[4,768,3,192]{1,3,2,0:T(8,128)(2,1)}, u32[]{:S(2)}) copy-start(bf16[4,768,3,192]{1,3,2,0:T(8,128)(2,1)} %reshape.115) | copy-start | bytes 10616836
  192.3 28.4 %collective-permute-start.3 = (bf16[192,512]{1,0:T(8,128)(2,1)S(1)}, bf16[192,512]{1,0:T(8,128)(2,1)S(1)}, u32[]{:S(2)}, u32[]{:S(2)}) collective-permute-start(bf16[192,512]{1,0:T(8,128)(2,1)S(1)} %get-tuple-element.157), channel_id=1, source_target_pairs={{0,1},{1,2},{2,3},{3,0},{4,5},{5,6},{6,7},{7,4},{8,9},{9,10},{10,1... | collective-permute-start | bytes 589832 | tf_op jit(solution)/shard_map/ppermute | solution.py:272
  203.2 17.4 %collective-permute-start.4 = (bf16[192,512]{1,0:T(8,128)(2,1)S(1)}, bf16[192,512]{1,0:T(8,128)(2,1)S(1)}, u32[]{:S(2)}, u32[]{:S(2)}) collective-permute-start(bf16[192,512]{1,0:T(8,128)(2,1)S(1)} %get-tuple-element.156), channel_id=1, source_target_pairs={{0,2},{1,3},{2,0},{3,1},{4,6},{5,7},{6,4},{7,5},{8,10},{9,11},{10,... | collective-permute-start | bytes 589832 | tf_op jit(solution)/shard_map/ppermute | solution.py:272
  209.0 79.8 %copy-start.49 = (bf16[1,4,192,768]{3,2,0,1:T(8,128)(2,1)}, bf16[1,4,192,768]{3,2,0,1:T(8,128)(2,1)S(1)}, u32[]{:S(2)}) copy-start(bf16[1,4,192,768]{3,2,0,1:T(8,128)(2,1)S(1)} %get-tuple-element.125) | copy-start | bytes 3538948
  209.1 17.2 %collective-permute-start.5 = (bf16[192,512]{1,0:T(8,128)(2,1)S(1)}, bf16[192,512]{1,0:T(8,128)(2,1)S(1)}, u32[]{:S(2)}, u32[]{:S(2)}) collective-permute-start(bf16[192,512]{1,0:T(8,128)(2,1)S(1)} %get-tuple-element.155), channel_id=1, source_target_pairs={{0,3},{1,0},{2,1},{3,2},{4,7},{5,4},{6,5},{7,6},{8,11},{9,8},{10,9... | collective-permute-start | bytes 589832 | tf_op jit(solution)/shard_map/ppermute | solution.py:272
  227.3 61.6 %copy-start.29 = (f32[512,768]{1,0:T(8,128)}, f32[512,768]{1,0:T(8,128)S(1)}, u32[]{:S(2)}) copy-start(f32[512,768]{1,0:T(8,128)S(1)} %get-tuple-element.191) | copy-start | bytes 4718596
  227.3 61.6 %copy-start.64 = (f32[512]{0:T(512)}, f32[512]{0:T(512)S(1)}, u32[]{:S(2)}) copy-start(f32[512]{0:T(512)S(1)} %broadcast_multiply_fusion.8) | copy-start | bytes 6148
  227.6 61.3 %copy-start.78 = (f32[512]{0:T(512)}, f32[512]{0:T(512)S(1)}, u32[]{:S(2)}) copy-start(f32[512]{0:T(512)S(1)} %add_rsqrt_fusion.2) | copy-start | bytes 6148
  229.1 7.7 collective-permute-start.12
  229.3 12.0 %collective-permute-start.13 = (bf16[192,512]{1,0:T(8,128)(2,1)S(1)}, bf16[192,512]{1,0:T(8,128)(2,1)S(1)}, u32[]{:S(2)}, u32[]{:S(2)}) collective-permute-start(bf16[192,512]{1,0:T(8,128)(2,1)S(1)} %get-tuple-element.152), channel_id=1, source_target_pairs={{0,2},{1,3},{2,0},{3,1},{4,6},{5,7},{6,4},{7,5},{8,10},{9,11},{10,... | collective-permute-start | bytes 589832 | tf_op jit(solution)/shard_map/ppermute | solution.py:272
  232.6 41.1 %copy-start.12 = (bf16[1024,192]{1,0:T(8,128)(2,1)}, bf16[1024,192]{1,0:T(8,128)(2,1)S(1)}, u32[]{:S(2)}) copy-start(bf16[1024,192]{1,0:T(8,128)(2,1)S(1)} %convolution_convert_fusion.10.k_ref) | copy-start | bytes 1179652
  232.7 8.6 %collective-permute-start.14 = (bf16[192,512]{1,0:T(8,128)(2,1)S(1)}, bf16[192,512]{1,0:T(8,128)(2,1)S(1)}, u32[]{:S(2)}, u32[]{:S(2)}) collective-permute-start(bf16[192,512]{1,0:T(8,128)(2,1)S(1)} %get-tuple-element.151), channel_id=1, source_target_pairs={{0,3},{1,0},{2,1},{3,2},{4,7},{5,4},{6,5},{7,6},{8,11},{9,8},{10,9... | collective-permute-start | bytes 589832 | tf_op jit(solution)/shard_map/ppermute | solution.py:272
  273.8 9.7 %collective-permute-start.18 = (bf16[192,512]{1,0:T(8,128)(2,1)S(1)}, bf16[192,512]{1,0:T(8,128)(2,1)S(1)}, u32[]{:S(2)}, u32[]{:S(2)}) collective-permute-start(bf16[192,512]{1,0:T(8,128)(2,1)S(1)} %get-tuple-element.149), channel_id=1, source_target_pairs={{0,1},{1,2},{2,3},{3,0},{4,5},{5,6},{6,7},{7,4},{8,9},{9,10},{10,1... | collective-permute-start | bytes 589832 | tf_op jit(solution)/shard_map/ppermute | solution.py:272
  276.5 12.3 %collective-permute-start.19 = (bf16[192,512]{1,0:T(8,128)(2,1)S(1)}, bf16[192,512]{1,0:T(8,128)(2,1)S(1)}, u32[]{:S(2)}, u32[]{:S(2)}) collective-permute-start(bf16[192,512]{1,0:T(8,128)(2,1)S(1)} %get-tuple-element.148), channel_id=1, source_target_pairs={{0,2},{1,3},{2,0},{3,1},{4,6},{5,7},{6,4},{7,5},{8,10},{9,11},{10,... | collective-permute-start | bytes 589832 | tf_op jit(solution)/shard_map/ppermute | solution.py:272
  278.2 10.7 %collective-permute-start.20 = (bf16[192,512]{1,0:T(8,128)(2,1)S(1)}, bf16[192,512]{1,0:T(8,128)(2,1)S(1)}, u32[]{:S(2)}, u32[]{:S(2)}) collective-permute-start(bf16[192,512]{1,0:T(8,128)(2,1)S(1)} %get-tuple-element.147), channel_id=1, source_target_pairs={{0,3},{1,0},{2,1},{3,2},{4,7},{5,4},{6,5},{7,6},{8,11},{9,8},{10,9... | collective-permute-start | bytes 589832 | tf_op jit(solution)/shard_map/ppermute | solution.py:272
  321.8 59.1 %copy-start.28 = (f32[512,768]{1,0:T(8,128)}, f32[512,768]{1,0:T(8,128)S(1)}, u32[]{:S(2)}) copy-start(f32[512,768]{1,0:T(8,128)S(1)} %get-tuple-element.115) | copy-start | bytes 4718596
  323.0 10.0 %collective-permute-start.21 = (bf16[192,512]{1,0:T(8,128)(2,1)S(1)}, bf16[192,512]{1,0:T(8,128)(2,1)S(1)}, u32[]{:S(2)}, u32[]{:S(2)}) collective-permute-start(bf16[192,512]{1,0:T(8,128)(2,1)S(1)} %get-tuple-element.145), channel_id=1, source_target_pairs={{0,1},{1,2},{2,3},{3,0},{4,5},{5,6},{6,7},{7,4},{8,9},{9,10},{10,1... | collective-permute-start | bytes 589832 | tf_op jit(solution)/shard_map/ppermute | solution.py:272
  327.7 12.4 %collective-permute-start.22 = (bf16[192,512]{1,0:T(8,128)(2,1)S(1)}, bf16[192,512]{1,0:T(8,128)(2,1)S(1)}, u32[]{:S(2)}, u32[]{:S(2)}) collective-permute-start(bf16[192,512]{1,0:T(8,128)(2,1)S(1)} %get-tuple-element.144), channel_id=1, source_target_pairs={{0,2},{1,3},{2,0},{3,1},{4,6},{5,7},{6,4},{7,5},{8,10},{9,11},{10,... | collective-permute-start | bytes 589832 | tf_op jit(solution)/shard_map/ppermute | solution.py:272
  328.4 12.1 %collective-permute-start.23 = (bf16[192,512]{1,0:T(8,128)(2,1)S(1)}, bf16[192,512]{1,0:T(8,128)(2,1)S(1)}, u32[]{:S(2)}, u32[]{:S(2)}) collective-permute-start(bf16[192,512]{1,0:T(8,128)(2,1)S(1)} %get-tuple-element.143), channel_id=1, source_target_pairs={{0,3},{1,0},{2,1},{3,2},{4,7},{5,4},{6,5},{7,6},{8,11},{9,8},{10,9... | collective-permute-start | bytes 589832 | tf_op jit(solution)/shard_map/ppermute | solution.py:272
  373.0 13.4 %collective-permute-start.24 = (bf16[192,512]{1,0:T(8,128)(2,1)}, bf16[192,512]{1,0:T(8,128)(2,1)S(1)}, u32[]{:S(2)}, u32[]{:S(2)}) collective-permute-start(bf16[192,512]{1,0:T(8,128)(2,1)} %get-tuple-element.141), channel_id=1, source_target_pairs={{0,1},{1,2},{2,3},{3,0},{4,5},{5,6},{6,7},{7,4},{8,9},{9,10},{10,1... | collective-permute-start | bytes 589832 | tf_op jit(solution)/shard_map/ppermute | solution.py:272
  377.5 16.1 %collective-permute-start.25 = (bf16[192,512]{1,0:T(8,128)(2,1)}, bf16[192,512]{1,0:T(8,128)(2,1)S(1)}, u32[]{:S(2)}, u32[]{:S(2)}) collective-permute-start(bf16[192,512]{1,0:T(8,128)(2,1)} %get-tuple-element.140), channel_id=1, source_target_pairs={{0,2},{1,3},{2,0},{3,1},{4,6},{5,7},{6,4},{7,5},{8,10},{9,11},{10,... | collective-permute-start | bytes 589832 | tf_op jit(solution)/shard_map/ppermute | solution.py:272
  382.8 175.7 %reduce-scatter.32.cloned.1.call-start = ((), (), s32[]{:S(2)}) async-start(), calls=%async_computation.19 | async-start | bytes 663552
  382.8 11.1 %collective-permute-start.26 = (bf16[192,512]{1,0:T(8,128)(2,1)S(1)}, bf16[192,512]{1,0:T(8,128)(2,1)S(1)}, u32[]{:S(2)}, u32[]{:S(2)}) collective-permute-start(bf16[192,512]{1,0:T(8,128)(2,1)S(1)} %get-tuple-element.139), channel_id=1, source_target_pairs={{0,3},{1,0},{2,1},{3,2},{4,7},{5,4},{6,5},{7,6},{8,11},{9,8},{10,9... | collective-permute-start | bytes 589832 | tf_op jit(solution)/shard_map/ppermute | solution.py:272
  402.6 10.0 %collective-permute-start.27 = (bf16[192,512]{1,0:T(8,128)(2,1)}, bf16[192,512]{1,0:T(8,128)(2,1)S(1)}, u32[]{:S(2)}, u32[]{:S(2)}) collective-permute-start(bf16[192,512]{1,0:T(8,128)(2,1)} %get-tuple-element.137), channel_id=1, source_target_pairs={{0,1},{1,2},{2,3},{3,0},{4,5},{5,6},{6,7},{7,4},{8,9},{9,10},{10,1... | collective-permute-start | bytes 589832 | tf_op jit(solution)/shard_map/ppermute | solution.py:272
  407.0 12.6 %collective-permute-start.28 = (bf16[192,512]{1,0:T(8,128)(2,1)}, bf16[192,512]{1,0:T(8,128)(2,1)S(1)}, u32[]{:S(2)}, u32[]{:S(2)}) collective-permute-start(bf16[192,512]{1,0:T(8,128)(2,1)} %get-tuple-element.136), channel_id=1, source_target_pairs={{0,2},{1,3},{2,0},{3,1},{4,6},{5,7},{6,4},{7,5},{8,10},{9,11},{10,... | collective-permute-start | bytes 589832 | tf_op jit(solution)/shard_map/ppermute | solution.py:272
  408.9 151.7 %reduce-scatter.28.cloned.1.call-start = ((), (), s32[]{:S(2)}) async-start(), calls=%async_computation.17 | async-start | bytes 1105920
  408.9 11.4 %collective-permute-start.29 = (bf16[192,512]{1,0:T(8,128)(2,1)S(1)}, bf16[192,512]{1,0:T(8,128)(2,1)S(1)}, u32[]{:S(2)}, u32[]{:S(2)}) collective-permute-start(bf16[192,512]{1,0:T(8,128)(2,1)S(1)} %get-tuple-element.135), channel_id=1, source_target_pairs={{0,3},{1,0},{2,1},{3,2},{4,7},{5,4},{6,5},{7,6},{8,11},{9,8},{10,9... | collective-permute-start | bytes 589832 | tf_op jit(solution)/shard_map/ppermute | solution.py:272
  471.9 89.9 %reduce-scatter.20.cloned.1.call-start = ((), (), s32[]{:S(2)}) async-start(), calls=%async_computation.12 | async-start | bytes 1327104 | tf_op jit(solution)/shard_map/reduce_scatter | solution.py:334
  473.8 118.7 %reduce-scatter.30.cloned.1.call-start = ((), (), s32[]{:S(2)}) async-start(), calls=%async_computation.18 | async-start | bytes 1327104
  477.5 152.8 %reduce-scatter.18.cloned.1.call-start = ((), (), s32[]{:S(2)}) async-start(), calls=%async_computation.11 | async-start | bytes 1966080 | tf_op jit(solution)/shard_map/reduce_scatter | solution.py:416
  481.1 205.4 %reduce-scatter.26.cloned.1.call-start = ((), (), s32[]{:S(2)}) async-start(), calls=%async_computation.15 | async-start | bytes 5308416 | tf_op jit(solution)/shard_map/reduce_scatter | solution.py:334
  487.5 265.4 %reduce-scatter.16.cloned.1.call-start = ((), (), s32[]{:S(2)}) async-start(), calls=%async_computation.10 | async-start | bytes 3932160 | tf_op jit(solution)/shard_map/reduce_scatter | solution.py:431
  494.1 316.6 %reduce-scatter.24.cloned.1.call-start = ((), (), s32[]{:S(2)}) async-start(), calls=%async_computation.14 | async-start | bytes 5308416 | tf_op jit(solution)/shard_map/reduce_scatter | solution.py:334
  507.3 52.3 %collective-permute-start.36 = (bf16[96,192]{1,0:T(8,128)(2,1)S(1)}, bf16[96,192]{1,0:T(8,128)(2,1)S(1)}, u32[]{:S(2)}, u32[]{:S(2)}) collective-permute-start(bf16[96,192]{1,0:T(8,128)(2,1)S(1)} %get-tuple-element.178), channel_id=1, source_target_pairs={{0,1},{1,2},{2,3},{3,0},{4,5},{5,6},{6,7},{7,4},{8,9},{9,10},{10,1... | collective-permute-start | bytes 110600 | tf_op jit(solution)/shard_map/ppermute | solution.py:272
  512.2 47.3 %collective-permute-start.37 = (bf16[96,192]{1,0:T(8,128)(2,1)S(1)}, bf16[96,192]{1,0:T(8,128)(2,1)S(1)}, u32[]{:S(2)}, u32[]{:S(2)}) collective-permute-start(bf16[96,192]{1,0:T(8,128)(2,1)S(1)} %get-tuple-element.180), channel_id=1, source_target_pairs={{0,2},{1,3},{2,0},{3,1},{4,6},{5,7},{6,4},{7,5},{8,10},{9,11},{10,... | collective-permute-start | bytes 110600 | tf_op jit(solution)/shard_map/ppermute | solution.py:272
  515.6 43.9 %collective-permute-start.38 = (bf16[96,192]{1,0:T(8,128)(2,1)S(1)}, bf16[96,192]{1,0:T(8,128)(2,1)S(1)}, u32[]{:S(2)}, u32[]{:S(2)}) collective-permute-start(bf16[96,192]{1,0:T(8,128)(2,1)S(1)} %get-tuple-element.179), channel_id=1, source_target_pairs={{0,3},{1,0},{2,1},{3,2},{4,7},{5,4},{6,5},{7,6},{8,11},{9,8},{10,9... | collective-permute-start | bytes 110600 | tf_op jit(solution)/shard_map/ppermute | solution.py:272
  562.8 35.3 %collective-permute-start.33 = (bf16[96,192]{1,0:T(8,128)(2,1)S(1)}, bf16[96,192]{1,0:T(8,128)(2,1)S(1)}, u32[]{:S(2)}, u32[]{:S(2)}) collective-permute-start(bf16[96,192]{1,0:T(8,128)(2,1)S(1)} %get-tuple-element.175), channel_id=1, source_target_pairs={{0,1},{1,2},{2,3},{3,0},{4,5},{5,6},{6,7},{7,4},{8,9},{9,10},{10,1... | collective-permute-start | bytes 110600 | tf_op jit(solution)/shard_map/ppermute | solution.py:272
  562.9 36.7 %collective-permute-start.34 = (bf16[96,192]{1,0:T(8,128)(2,1)S(1)}, bf16[96,192]{1,0:T(8,128)(2,1)S(1)}, u32[]{:S(2)}, u32[]{:S(2)}) collective-permute-start(bf16[96,192]{1,0:T(8,128)(2,1)S(1)} %get-tuple-element.177), channel_id=1, source_target_pairs={{0,2},{1,3},{2,0},{3,1},{4,6},{5,7},{6,4},{7,5},{8,10},{9,11},{10,... | collective-permute-start | bytes 110600 | tf_op jit(solution)/shard_map/ppermute | solution.py:272
  564.9 34.7 %collective-permute-start.35 = (bf16[96,192]{1,0:T(8,128)(2,1)S(1)}, bf16[96,192]{1,0:T(8,128)(2,1)S(1)}, u32[]{:S(2)}, u32[]{:S(2)}) collective-permute-start(bf16[96,192]{1,0:T(8,128)(2,1)S(1)} %get-tuple-element.176), channel_id=1, source_target_pairs={{0,3},{1,0},{2,1},{3,2},{4,7},{5,4},{6,5},{7,6},{8,11},{9,8},{10,9... | collective-permute-start | bytes 110600 | tf_op jit(solution)/shard_map/ppermute | solution.py:272
  593.7 7.7 collective-permute-start.30
  595.4 6.3 collective-permute-start.31
  598.1 4.2 collective-permute-start.32
  687.5 128.2 %collective-permute-start.42 = (bf16[96,768]{1,0:T(8,128)(2,1)S(1)}, bf16[96,768]{1,0:T(8,128)(2,1)S(1)}, u32[]{:S(2)}, u32[]{:S(2)}) collective-permute-start(bf16[96,768]{1,0:T(8,128)(2,1)S(1)} %get-tuple-element.161), channel_id=1, source_target_pairs={{0,1},{1,2},{2,3},{3,0},{4,5},{5,6},{6,7},{7,4},{8,9},{9,10},{10,1... | collective-permute-start | bytes 442376 | tf_op jit(solution)/shard_map/ppermute | solution.py:272
  689.0 128.1 %collective-permute-start.43 = (bf16[96,768]{1,0:T(8,128)(2,1)S(1)}, bf16[96,768]{1,0:T(8,128)(2,1)S(1)}, u32[]{:S(2)}, u32[]{:S(2)}) collective-permute-start(bf16[96,768]{1,0:T(8,128)(2,1)S(1)} %get-tuple-element.163), channel_id=1, source_target_pairs={{0,2},{1,3},{2,0},{3,1},{4,6},{5,7},{6,4},{7,5},{8,10},{9,11},{10,... | collective-permute-start | bytes 442376 | tf_op jit(solution)/shard_map/ppermute | solution.py:272
  691.4 125.7 %collective-permute-start.44 = (bf16[96,768]{1,0:T(8,128)(2,1)S(1)}, bf16[96,768]{1,0:T(8,128)(2,1)S(1)}, u32[]{:S(2)}, u32[]{:S(2)}) collective-permute-start(bf16[96,768]{1,0:T(8,128)(2,1)S(1)} %get-tuple-element.162), channel_id=1, source_target_pairs={{0,3},{1,0},{2,1},{3,2},{4,7},{5,4},{6,5},{7,6},{8,11},{9,8},{10,9... | collective-permute-start | bytes 442376 | tf_op jit(solution)/shard_map/ppermute | solution.py:272
  811.8 8.7 %collective-permute-start.39 = (bf16[96,768]{1,0:T(8,128)(2,1)S(1)}, bf16[96,768]{1,0:T(8,128)(2,1)S(1)}, u32[]{:S(2)}, u32[]{:S(2)}) collective-permute-start(bf16[96,768]{1,0:T(8,128)(2,1)S(1)} %get-tuple-element.164), channel_id=1, source_target_pairs={{0,1},{1,2},{2,3},{3,0},{4,5},{5,6},{6,7},{7,4},{8,9},{9,10},{10,1... | collective-permute-start | bytes 442376 | tf_op jit(solution)/shard_map/ppermute | solution.py:272
  813.3 12.1 %collective-permute-start.40 = (bf16[96,768]{1,0:T(8,128)(2,1)S(1)}, bf16[96,768]{1,0:T(8,128)(2,1)S(1)}, u32[]{:S(2)}, u32[]{:S(2)}) collective-permute-start(bf16[96,768]{1,0:T(8,128)(2,1)S(1)} %get-tuple-element.166), channel_id=1, source_target_pairs={{0,2},{1,3},{2,0},{3,1},{4,6},{5,7},{6,4},{7,5},{8,10},{9,11},{10,... | collective-permute-start | bytes 442376 | tf_op jit(solution)/shard_map/ppermute | solution.py:272
  815.7 9.7 %collective-permute-start.41 = (bf16[96,768]{1,0:T(8,128)(2,1)S(1)}, bf16[96,768]{1,0:T(8,128)(2,1)S(1)}, u32[]{:S(2)}, u32[]{:S(2)}) collective-permute-start(bf16[96,768]{1,0:T(8,128)(2,1)S(1)} %get-tuple-element.165), channel_id=1, source_target_pairs={{0,3},{1,0},{2,1},{3,2},{4,7},{5,4},{6,5},{7,6},{8,11},{9,8},{10,9... | collective-permute-start | bytes 442376 | tf_op jit(solution)/shard_map/ppermute | solution.py:272
  (85 other events, 481.4 us)
Sparse Core Ops, SparseCore 0:
  9.6 102.5 all-gather.5
  115.7 81.5 all-gather.3
  382.9 34.7 reduce-scatter.21
  421.2 34.3 reduce-scatter.31
  471.9 40.7 reduce-scatter.27
  515.8 36.6 reduce-scatter.19
  555.8 36.7 reduce-scatter.29
  594.8 35.4 reduce-scatter.17
  633.8 52.6 reduce-scatter.25
  688.6 64.3 reduce-scatter.15
  756.4 54.2 reduce-scatter.23

commit v2 on v1

--- a/solution.py
+++ b/solution.py
@@ -8,11 +8,23 @@
 def dot_nn(a,b): return jnp.dot(a,b,preferred_element_type=jnp.float32)
 def dot_nt(a,b): return lax.dot_general(a,b,(((1,),(1,)),((),())),preferred_element_type=jnp.float32)
 
+def over_chunks(count, blocks, step, carry):
+    done = 0
+    while True:
+        def chunk(j, carry, blocks=blocks, done=done):
+            return step(pl.multiple_of((done + j * blocks) * KB, KB), blocks * KB, carry)
+        trips = (count - done) // blocks
+        carry = lax.fori_loop(0, trips, chunk, carry)
+        if blocks == 1:
+            return carry
+        done = done + trips * blocks
+        blocks //= 2
+
 def head_masked(block, h):
     rows = lax.broadcasted_iota(jnp.int32, block.shape, 0)
     return jnp.where((rows >= h*HD) & (rows < (h+1)*HD), block, jnp.zeros_like(block))
 
-def attend_kernel(counts_ref, q_ref, k_ref, v_ref, o_ref, lse_ref, vt_ref, *, heads):
+def attend_kernel(counts_ref, q_ref, k_ref, v_ref, o_ref, lse_ref, vt_ref, *, heads, blocks):
     i = pl.program_id(0)
     nk = k_ref.shape[0]//KB
     bq = q_ref.shape[1]
@@ -22,9 +34,8 @@
             vt_ref[:, j*KB:(j+1)*KB] = v_ref[j*KB:(j+1)*KB, :].T
     q = q_ref[...]
     qm = [head_masked(q, h) for h in range(heads)]
-    def step(j, carry):
-        start = pl.multiple_of(j*KB, KB)
-        kj = k_ref[pl.ds(start, KB), :]
+    def step(start, keys, carry):
+        kj = k_ref[pl.ds(start, keys), :]
         new = []
         for h in range(heads):
             m, l, acc = carry[h]
@@ -33,23 +44,23 @@
             p = jnp.exp(s - m_new)
             alpha = jnp.exp(m - m_new)
             l = l*alpha + jnp.sum(p, axis=0, keepdims=True)
-            vt = vt_ref[h*HD:(h+1)*HD, pl.ds(start, KB)]
+            vt = vt_ref[h*HD:(h+1)*HD, pl.ds(start, keys)]
             acc = acc*alpha + dot_nn(vt, p.astype(jnp.bfloat16))
             new.append((m_new, l, acc))
         return tuple(new)
     init = tuple((jnp.full((1,bq),-1e30,jnp.float32), jnp.zeros((1,bq),jnp.float32), jnp.zeros((HD,bq),jnp.float32)) for _ in range(heads))
-    fin = lax.fori_loop(0, counts_ref[i], step, init)
+    fin = over_chunks(counts_ref[i], blocks, step, init)
     for h in range(heads):
         m, l, acc = fin[h]
         o_ref[h*HD:(h+1)*HD, :] = (acc/l).astype(jnp.bfloat16)
         lse_ref[h:h+1, :] = m + jnp.log(l)
 
-def attend(counts, q_t, k, v, bq=256):
+def attend(counts, q_t, k, v, bq=256, blocks=4):
     width, rows = q_t.shape
     nk = k.shape[0]
     heads = width//HD
     return pl.pallas_call(
-        functools.partial(attend_kernel, heads=heads),
+        functools.partial(attend_kernel, heads=heads, blocks=blocks),
         grid_spec=pltpu.PrefetchScalarGridSpec(
             num_scalar_prefetch=1, grid=(rows//bq,),
             in_specs=[pl.BlockSpec((width,bq), lambda i,c:(0,i)),
@@ -60,10 +71,11 @@
             scratch_shapes=[pltpu.VMEM((width,nk), jnp.bfloat16)]),
         out_shape=(jax.ShapeDtypeStruct((width,rows),jnp.bfloat16), jax.ShapeDtypeStruct((8,rows),jnp.float32)),
         compiler_params=pltpu.CompilerParams(dimension_semantics=("arbitrary",), vmem_limit_bytes=40<<20),
+        cost_estimate=pl.CostEstimate(flops=4*rows*nk*width*4, transcendentals=rows*nk*heads, bytes_accessed=8*rows*width),
         name="attend",
     )(counts, q_t, k, v)
 
-def attend_back_kernel(counts_ref, q_ref, g_ref, o_ref, lse_ref, k_ref, v_ref, dq_ref, dkv_ref, kt_ref, dka_ref, dva_ref, *, heads):
+def attend_back_kernel(counts_ref, q_ref, g_ref, o_ref, lse_ref, k_ref, v_ref, dq_ref, dkv_ref, kt_ref, dka_ref, dva_ref, *, heads, blocks):
     i = pl.program_id(0)
     nk = k_ref.shape[0]//KB
     bq = q_ref.shape[1]
@@ -80,21 +92,20 @@
     gm = [head_masked(g, h) for h in range(heads)]
     delta = [jnp.sum(prod[h*HD:(h+1)*HD], axis=0, keepdims=True) for h in range(heads)]
     lse = [lse_ref[h:h+1, :] for h in range(heads)]
-    def step(j, carry):
-        start = pl.multiple_of(j*KB, KB)
-        kj = k_ref[pl.ds(start, KB), :]
-        vj = v_ref[pl.ds(start, KB), :]
+    def step(start, keys, carry):
+        kj = k_ref[pl.ds(start, keys), :]
+        vj = v_ref[pl.ds(start, keys), :]
         new = []
         for h in range(heads):
             lo, hi = h*HD, (h+1)*HD
             p = jnp.exp(dot_nn(kj, qm[h]) - lse[h])
             dp = dot_nn(vj, gm[h])
             ds = (p*(dp - delta[h])).astype(jnp.bfloat16)
-            dva_ref[lo:hi, pl.ds(start, KB)] += dot_nt(g[lo:hi], p.astype(jnp.bfloat16))
-            dka_ref[lo:hi, pl.ds(start, KB)] += dot_nt(q[lo:hi], ds)
-            new.append(carry[h] + dot_nn(kt_ref[lo:hi, pl.ds(start, KB)], ds))
+            dva_ref[lo:hi, pl.ds(start, keys)] += dot_nt(g[lo:hi], p.astype(jnp.bfloat16))
+            dka_ref[lo:hi, pl.ds(start, keys)] += dot_nt(q[lo:hi], ds)
+            new.append(carry[h] + dot_nn(kt_ref[lo:hi, pl.ds(start, keys)], ds))
         return tuple(new)
-    fin = lax.fori_loop(0, counts_ref[i], step, tuple(jnp.zeros((HD,bq),jnp.float32) for _ in range(heads)))
+    fin = over_chunks(counts_ref[i], blocks, step, tuple(jnp.zeros((HD,bq),jnp.float32) for _ in range(heads)))
     for h in range(heads):
         dq_ref[h*HD:(h+1)*HD, :] = (fin[h] * HD**-0.5).astype(jnp.bfloat16)
     @pl.when(i == pl.num_programs(0)-1)
@@ -102,7 +113,7 @@
         dkv_ref[:heads*HD, :] = dka_ref[...].astype(jnp.bfloat16)
         dkv_ref[heads*HD:, :] = dva_ref[...].astype(jnp.bfloat16)
 
-def attend_back(counts, q_t, g_t, o_t, lse, k, v, bq=256):
+def attend_back(counts, q_t, g_t, o_t, lse, k, v, bq=256, blocks=4):
     width, rows = q_t.shape
     nk = k.shape[0]
     heads = width//HD
@@ -110,7 +121,7 @@
     whole = pl.BlockSpec((nk,width), lambda i,c:(0,0))
     wide = pl.BlockSpec((2*width,nk), lambda i,c:(0,0))
     return pl.pallas_call(
-        functools.partial(attend_back_kernel, heads=heads),
+        functools.partial(attend_back_kernel, heads=heads, blocks=blocks),
         grid_spec=pltpu.PrefetchScalarGridSpec(
             num_scalar_prefetch=1, grid=(rows//bq,),
             in_specs=[per,per,per,pl.BlockSpec((8,bq), lambda i,c:(0,i)),whole,whole],
@@ -118,6 +129,7 @@
             scratch_shapes=[pltpu.VMEM((width,nk), jnp.bfloat16),pltpu.VMEM((width,nk), jnp.float32),pltpu.VMEM((width,nk), jnp.float32)]),
         out_shape=(jax.ShapeDtypeStruct((width,rows),jnp.bfloat16),)+(jax.ShapeDtypeStruct((2*width,nk),jnp.bfloat16),),
         compiler_params=pltpu.CompilerParams(dimension_semantics=("arbitrary",), vmem_limit_bytes=48<<20),
+        cost_estimate=pl.CostEstimate(flops=10*rows*nk*width*4, transcendentals=rows*nk*heads, bytes_accessed=16*rows*width),
         name="attend_back",
     )(counts, q_t, g_t, o_t, lse, k, v)
 
@@ -257,8 +269,8 @@
     if lax.axis_size(axis) != 2:
         return lax.all_gather(x, axis, axis=0)
     other = swapped(x, axis)
-    first = lax.axis_index(axis) == 0
-    return jnp.stack([jnp.where(first, x, other), jnp.where(first, other, x)])
+    place = lax.broadcasted_iota(jnp.int32, (2,) + (1,) * x.ndim, 0)
+    return jnp.where(place == lax.axis_index(axis), x[None], other[None])
 
 
 def gather_over(x, axes):
@@ -328,6 +340,65 @@
     for s in range(1, count):
         total = total + shifted(take((rank + s) % count), s).astype(jnp.float32)
     return total
+
+
+def tied(*values):
+    return lax.optimization_barrier(values)
+
+
+def parted(x, axis, dim):
+    rank = lax.axis_index(axis)
+    return (lax.dynamic_index_in_dim(x, rank, dim, keepdims=False),
+            lax.dynamic_index_in_dim(x, 1 - rank, dim, keepdims=False))
+
+
+class Flow:
+    def __init__(self, former, latter, axes):
+        self.axes = axes
+        self.pairs = all(lax.axis_size(a) == 2 for a in DP)
+        if not self.pairs:
+            self.moving = reduce_rows(dot_tn(former, latter).astype(jnp.bfloat16))
+            return
+        rows = former.shape[1] // lax.axis_size(DP)
+        mine, theirs = parted(former.reshape(-1, lax.axis_size(DP) // 2, 2, rows), "core", 2)
+        self.kept = dot_tn(mine.reshape(former.shape[0], -1), latter).astype(jnp.bfloat16)
+        self.sent = dot_tn(theirs.reshape(former.shape[0], -1), latter).astype(jnp.bfloat16)
+
+    @classmethod
+    def of(cls, partial, axes):
+        self = cls.__new__(cls)
+        self.axes = axes
+        self.pairs = all(lax.axis_size(a) == 2 for a in DP)
+        if not self.pairs:
+            self.moving = reduce_rows(partial)
+            return self
+        count = lax.axis_size(DP)
+        rows, cols = partial.shape[0] // count, partial.shape[1]
+        mine, theirs = parted(partial.reshape(count // 2, 2, rows, cols), "core", 1)
+        self.kept, self.sent = mine.reshape(-1, cols), theirs.reshape(-1, cols)
+        return self
+
+    def across_core(self):
+        if self.pairs:
+            self.moving = swapped(self.sent, "core")
+
+    def across(self, stage):
+        if not self.pairs:
+            return
+        if stage == 0:
+            whole = (2, 2, -1) + self.kept.shape[1:]
+            kept, got = self.kept.reshape(whole), self.moving.reshape(whole)
+            dim = DP.index(self.axes[0])
+        else:
+            kept, got, dim = self.kept, self.moving, 0
+        pieces = zip(parted(kept, self.axes[stage], dim), parted(got, self.axes[stage], dim))
+        keep, send = [(a.astype(jnp.float32) + b.astype(jnp.float32)).astype(jnp.bfloat16) for a, b in pieces]
+        self.kept, self.moving = keep, swapped(send, self.axes[stage])
+
+    def total(self):
+        if not self.pairs:
+            return self.moving
+        return (self.kept.astype(jnp.float32) + self.moving.astype(jnp.float32)).astype(jnp.bfloat16)
 
 
 def reduce_rows(partial):
@@ -365,18 +436,18 @@
     w_cross = head_pack[:, 3 * width :]
     out_turned = jnp.swapaxes(out_weight.astype(low), 1, 2)
     mid_pack = jnp.concatenate([in_low[3], out_turned[0], out_turned[1]], axis=1)
+    encoder, mid_pack, hidden_self = tied(encoder_out[0], mid_pack, hidden_self)
     mid_pack = gather_over(gather_tokens(mid_pack).reshape(tensor_count, shards, 3 * width), ("core", "mid", "outer"))
-    mid_pack = mid_pack.reshape(D // shards, tensor_count, shards, 3 * width)
-    mid_pack = jnp.swapaxes(mid_pack, 0, 1).reshape(tensor_count, D, 3, width)
-    turned = jnp.transpose(mid_pack, (2, 0, 3, 1)).reshape(3, D, D)
-    wq_cross_t, wo_self, wo_cross = turned[0], turned[1], turned[2]
+    mid_pack = mid_pack.reshape(D // shards, tensor_count, shards, 3, width)
+    wq_cross, wo_self, wo_cross = (
+        jnp.swapaxes(mid_pack[:, :, :, n], 1, 2).reshape(D, D) for n in range(3))
     unit_pack = jnp.concatenate([up_weight.astype(low), down_weight.astype(low).T], axis=1)
     unit_pack = lax.all_gather(unit_pack, ("tensor",) + DP, axis=0, tiled=True).reshape(tensor_count, D, -1)
-    encoder_full = gather_tokens(encoder_out[0])
+    encoder_full = gather_tokens(encoder)
 
     head_bias = lax.dynamic_slice_in_dim(vectors[0:4], start, width, 1)
     counts_self = jnp.sum((ids[None, :] <= ids[:, None]).astype(jnp.int32), axis=1)
-    counts_cross = jnp.full(ids.shape, encoder_full.shape[0] // KB, jnp.int32)
+    counts_cross = jnp.full((ids.shape[0] // 2,), encoder_full.shape[0] // KB, jnp.int32)
 
     q_self = ((dot_tt(w_self[:, :width], hidden_self) + head_bias[0][:, None]) * scale).astype(low)
     k_self = dot_nn(hidden_self, w_self[:, width : 2 * width]).astype(low)
@@ -385,13 +456,13 @@
     k_cross = dot_nn(encoder_full, w_cross[:, :width]).astype(low)
     v_cross = (dot_nn(encoder_full, w_cross[:, width:]) + head_bias[3]).astype(low)
     mixed_self = heads_to_tokens(mine_self)
-    summed_one = rows.astype(jnp.float32) + (dot_tn(mixed_self, wo_self) + vectors[4])
+    summed_one = rows.astype(jnp.float32) + (dot_tt(mixed_self, wo_self) + vectors[4])
     normed_one = layer_norm(summed_one, norm_gains[0], vectors[7])
     hidden_cross = normed_one.astype(low)
-    q_cross = tokens_to_heads(((dot_nt(wq_cross_t, hidden_cross) + vectors[2][:, None]) * scale).astype(low))
-    mine_cross, lse_cross = attend(counts_cross, q_cross, k_cross, v_cross)
+    q_cross = tokens_to_heads(((dot_tt(wq_cross, hidden_cross) + vectors[2][:, None]) * scale).astype(low))
+    mine_cross, lse_cross = attend(counts_cross, q_cross, k_cross, v_cross, bq=512)
     mixed_cross = heads_to_tokens(mine_cross)
-    summed_two = normed_one + (dot_tn(mixed_cross, wo_cross) + vectors[5])
+    summed_two = normed_one + (dot_tt(mixed_cross, wo_cross) + vectors[5])
     normed_two = layer_norm(summed_two, norm_gains[1], vectors[8])
     hidden_units = normed_two.astype(low)
     active, slope, unit_out = units(hidden_units, unit_pack, up_bias[None])
@@ -402,46 +473,69 @@
     branch_three = grad_three.astype(low)
     bias_down = jnp.sum(branch_three.astype(jnp.float32), axis=0)
     grad_before, unit_bias, unit_back = units_back(branch_three, unit_pack, slope)
-    down_grad = reduce_rows(dot_tn(branch_three, active).astype(low))
-    up_grad = reduce_rows(dot_tn(hidden_units, grad_before).astype(low))
     grad_two, gain_two, shift_two = layer_norm_back(grad_three + unit_back, summed_two, norm_gains[1])
     branch_two = grad_two.astype(low)
     bias_cross_out = jnp.sum(branch_two.astype(jnp.float32), axis=0)
-    grad_mixed_cross = tokens_to_heads(dot_nt(wo_cross, branch_two).astype(low))
-    out_grad_cross = reduce_rows(dot_tt(branch_two, mixed_cross).astype(low))
+    down = Flow(branch_three, active, ("mid", "outer"))
+    up = Flow(hidden_units, grad_before, ("outer", "mid"))
+    grad_mixed_cross = tokens_to_heads(dot_tt(wo_cross, branch_two).astype(low))
+    out_grad_cross = dot_tt(branch_two, mixed_cross).astype(low)
+    if down.pairs:
+        grad_mixed_cross, out_grad_cross, down.kept, down.sent, up.kept, up.sent = tied(
+            grad_mixed_cross, out_grad_cross, down.kept, down.sent, up.kept, up.sent)
+    down.across_core()
+    up.across_core()
     dq_mine, dkv_cross = attend_back(
-        counts_cross, q_cross, grad_mixed_cross, mine_cross, lse_cross, k_cross, v_cross)
+        counts_cross, q_cross, grad_mixed_cross, mine_cross, lse_cross, k_cross, v_cross, bq=512)
+    dq_mine, dkv_cross, down.moving, up.moving = tied(dq_mine, dkv_cross, down.moving, up.moving)
+    encoder_part = lax.psum_scatter(
+        dot_tt(dkv_cross, w_cross).astype(low), "tensor", scatter_dimension=0, tiled=True)
+    kv_grad = dot_tt(encoder_full, dkv_cross).astype(low)
     dq_cross = heads_to_tokens(dq_mine)
-    kv_grad = reduce_rows(dot_tt(encoder_full, dkv_cross).astype(low))
-    encoder_grad = lax.psum_scatter(
-        dot_tt(dkv_cross, w_cross).astype(low), "tensor", scatter_dimension=0, tiled=True).astype(jnp.float32)
     bias_query_cross = jnp.sum(dq_cross.astype(jnp.float32), axis=1)
     bias_value_cross = jnp.sum(dkv_cross[width:].astype(jnp.float32), axis=1)
-    query_grad_cross = reduce_rows(dot_tt(hidden_cross, dq_cross).astype(low))
-    grad_one_in = grad_two + dot_tn(dq_cross, wq_cross_t)
+    down.across(0)
+    up.across(0)
+    query_grad_cross = dot_tt(hidden_cross, dq_cross).astype(low)
+    cross_grads = reduce_rows(jnp.concatenate([query_grad_cross, out_grad_cross, kv_grad], axis=1))
+    grad_one_in = grad_two + dot_tt(dq_cross, wq_cross)
     grad_one, gain_one, shift_one = layer_norm_back(grad_one_in, summed_one, norm_gains[0])
     branch_one = grad_one.astype(low)
     bias_self_out = jnp.sum(branch_one.astype(jnp.float32), axis=0)
-    grad_mixed_self = tokens_to_heads(dot_nt(wo_self, branch_one).astype(low))
-    out_grad_self = reduce_rows(dot_tt(branch_one, mixed_self).astype(low))
+    grad_mixed_self = tokens_to_heads(dot_tt(wo_self, branch_one).astype(low))
+    out_grad_self = dot_tt(branch_one, mixed_self).astype(low)
+    grad_mixed_self, down.moving, up.moving, out_grad_self, encoder_part = tied(
+        grad_mixed_self, down.moving, up.moving, out_grad_self, encoder_part)
+    down.across(1)
+    up.across(1)
     dq_self, dkv_self = attend_back(
         counts_self, q_self, grad_mixed_self, mine_self, lse_self, k_self, v_self)
+    dq_self, dkv_self, down.moving, up.moving, cross_grads = tied(
+        dq_self, dkv_self, down.moving, up.moving, cross_grads)
     dqkv = jnp.concatenate([dq_self, dkv_self], axis=0)
     input_part = dot_tt(dqkv, w_self).astype(low)
+    input_part, dqkv = tied(input_part, dqkv)
     input_grad = grad_one + lax.psum_scatter(
         input_part, "tensor", scatter_dimension=0, tiled=True).astype(jnp.float32)
-    self_grad = reduce_rows(dot_tt(hidden_self, dqkv).astype(low)).astype(jnp.float32)
+    self_flow = Flow.of(
+        jnp.concatenate([out_grad_self, dot_tt(hidden_self, dqkv).astype(low)], axis=1), ("mid", "outer"))
+    self_flow.across_core()
+    self_flow.across(0)
+    self_flow.across(1)
+    self_grads = self_flow.total()
     bias_query_self = jnp.sum(dq_self.astype(jnp.float32), axis=1)
     bias_value_self = jnp.sum(dkv_self[width:].astype(jnp.float32), axis=1)
 
-    kv_grad = kv_grad.astype(jnp.float32)
-    mid_grads = [reduce_columns(g) for g in (query_grad_cross, out_grad_self, out_grad_cross)]
-    up_shard = reduce_columns(up_grad)
-    down_shard = reduce_columns(down_grad).T
+    encoder_grad = encoder_part.astype(jnp.float32)
+    query_shard = reduce_columns(cross_grads[:, :D])
+    out_shard = jnp.stack([reduce_columns(self_grads[:, :D]).T, reduce_columns(cross_grads[:, D : 2 * D]).T])
+    kv_shard = cross_grads[:, 2 * D :].astype(jnp.float32)
+    self_shard = self_grads[:, D:].astype(jnp.float32)
+    up_shard = reduce_columns(up.total())
+    down_shard = reduce_columns(down.total()).T
     in_shard = jnp.stack([
-        self_grad[:, :width], self_grad[:, width : 2 * width], self_grad[:, 2 * width :],
-        mid_grads[0], kv_grad[:, :width], kv_grad[:, width:]])
-    out_shard = jnp.stack([mid_grads[1].T, mid_grads[2].T])
+        self_shard[:, :width], self_shard[:, width : 2 * width], self_shard[:, 2 * width :],
+        query_shard, kv_shard[:, :width], kv_shard[:, width:]])
 
     def embed(part):
         return lax.dynamic_update_slice_in_dim(jnp.zeros((D,), jnp.float32), part, start, 0)

time: 846 us -> 650 us (0.77)
  waiting for transfers between devices: 349 us -> 202 us
  Pallas kernels: 164 us -> 103 us
  local copies, waits for them, and re-layouts: 58.2 us -> 76.4 us
  starting transfers between devices: 115 us -> 103 us
    reduce_scatter x4 -> x1, waiting for transfers between devices: 110 us -> 13.6 us  [reduce_rows(): return lax.psum_scatter(partial, DP, scatter_dimension=0, tiled=True)]
    pallas_call x4, Pallas kernels: 145 us -> 83.7 us  [the longest x2 45.5 us: attend_back(): pl.pallas_call(functools.partial(attend_back_kernel, heads=heads, blocks=...]
    reduce_scatter x1, waiting for transfers between devices: 60 us -> 0.01 us  [body(): lax.psum_scatter(input_part, 'tensor', scatter_dimension=0, tiled=True)]
    all_gather x1, waiting for transfers between devices: 0.01 us -> 48.7 us  [body(): hidden_self = lax.all_gather(rows, 'tensor', axis=0, tiled=True)]
    ppermute x39, starting transfers between devices: 109 us -> 80.9 us  [shifted(): lax.ppermute(piece, 'tensor', [(i, (i + step) % count) for i in range(cou...]
    reduce_scatter x1, waiting for transfers between devices: 26.9 us -> 0.02 us  [body(): lax.psum_scatter(dot_tt(dkv_cross, w_cross).astype(low), 'tensor', scatte...]
    unnamed x14 -> x5, waiting for transfers between devices: 26.7 us -> 0.75 us
    convert_element_type x2 -> x11, other arithmetic: 0.04 us -> 17.2 us  [the longest x6 13.1 us: across(): (a.astype(jnp.float32) + b.astype(jnp.float32)).astype(jnp.bfloat16)]
  transfers between devices with their start and end apart: 56 -> 59, of which waited for: 30 -> 24; matrix products, arithmetic and copies ran while one was open for 15% -> 19% of each run, Pallas kernels for 14% -> 13%
where the time goes in v2:
time: 650 us; the launch traced here: 641 us
  waiting for transfers between devices  202 us (31%)
  starting transfers between devices  103 us (16%)
  Pallas kernels  103 us (16%)
  local copies, waits for them, and re-layouts  76.4 us (12%)
  matrix products  49.8 us (8%)
  blocking collectives  47.8 us (7%)
  other arithmetic  43.5 us (7%)
  between operations  16.1 us (2%)
    ppermute x39, waiting for transfers between devices, shifted(): lax.ppermute(piece, 'tensor', [(i, (i + step) % count) for i in range(cou...  101 us
    ppermute x39, starting transfers between devices, shifted(): lax.ppermute(piece, 'tensor', [(i, (i + step) % count) for i in range(cou...  80.9 us
    all_gather x1, waiting for transfers between devices, body(): hidden_self = lax.all_gather(rows, 'tensor', axis=0, tiled=True)  48.7 us
    psum x1, blocking collectives, body(): lax.psum((vector_grad, gain_grad, unit_bias[0]), EVERY)  47.8 us
    pallas_call x2, Pallas kernels, attend_back(): pl.pallas_call(functools.partial(attend_back_kernel, heads=heads, blocks=...  45.5 us
    pallas_call x2, Pallas kernels, attend(): pl.pallas_call(functools.partial(attend_kernel, heads=heads, blocks=block...  38.2 us
    ppermute x15, waiting for transfers between devices, swapped(): return lax.ppermute(x, axis, [(0, 1), (1, 0)])  38 us
    dot_general x14, matrix products, dot_tt(): lax.dot_general(former, latter, (((0,), (1,)), ((), ())), preferred_eleme...  34.1 us
  transfers between devices with their start and end apart: 59, of which 24 were waited for; matrix products, arithmetic and copies ran while one was open for 19% of the time, Pallas kernels for 13%

profile of v2, /device:TPU:0, one launch (start us, length us, event | category | flops | bytes accessed | tf_op | source)
XLA Modules:
  0.0 641.0 jit_solution(2020141814126240995)
XLA Ops:
  12.8 2.9 collective-permute-start.1
  15.9 9.3 %collective-permute-done.1 = bf16[2,96,960]{2,1,0:T(8,128)(2,1)S(1)} collective-permute-done((bf16[2,96,960]{2,1,0:T(8,128)(2,1)S(1)}, bf16[2,96,960]{2,1,0:T(8,128)(2,1)S(1)}, u32[]{:S(2)}, u32[]{:S(2)}) %collective-permute-start.1) | collective-permute-done | bytes 368672 | tf_op jit(solution)/shard_map/ppermute | solution.py:265
  27.1 48.7 %all-gather.6.cloned.1.call-done = bf16[1,2048,768]{2,1,0:T(8,128)(2,1)} async-done(((bf16[1,512,768]{2,1,0:T(8,128)(2,1)}), bf16[1,2048,768]{2,1,0:T(8,128)(2,1)}) %all-gather.6.cloned.1.call-update) | async-done | bytes 3145744 | tf_op jit(solution)/shard_map/all_gather | solution.py:432
  77.1 2.7 collective-permute-start.8
  79.9 4.0 collective-permute-done.6
  83.9 4.0 collective-permute-done.7
  95.0 26.8 %collective-permute-done.10 = bf16[2,4,96,576]{3,2,1,0:T(8,128)(2,1)S(1)} collective-permute-done((bf16[2,4,96,576]{3,2,1,0:T(8,128)(2,1)S(1)}, bf16[2,4,96,576]{3,2,1,0:T(8,128)(2,1)S(1)}, u32[]{:S(2)}, u32[]{:S(2)}) %collective-permute-start.10) | collective-permute-done | bytes 884768 | tf_op jit(solution)/shard_map/ppermute | solution.py:265
  124.7 25.1 %attend.2 = (bf16[192,2048]{1,0:T(8,128)(2,1)S(1)}, f32[8,2048]{1,0:T(8,128)S(1)}) custom-call(s32[8]{0:T(128)S(1)} %convert_reduce_fusion.8.counts_ref, bf16[192,2048]{1,0:T(8,128)(2,1)S(1)} %fusion.2.q_ref, bf16[2048,192]{1,0:T(8,128)(2,1)S(1)} %convolution_convert_fusion.5.k_ref, bf16[2048,192]{1,0:T(8,128)(2,1)S(1)} %fusion.v_ref), custom_call_target="tpu_custom_call" | custom-call | flops 12884901888 | bytes 3145728 | tf_op jit(solution)/shard_map/attend/pallas_call | solution.py:62
  150.0 2.8 collective-permute-start.3
  156.7 3.8 collective-permute-done.3
  161.2 41.4 %collective-permute-done.4 = bf16[192,512]{1,0:T(8,128)(2,1)S(1)} collective-permute-done((bf16[192,512]{1,0:T(8,128)(2,1)S(1)}, bf16[192,512]{1,0:T(8,128)(2,1)S(1)}, u32[]{:S(2)}, u32[]{:S(2)}) %collective-permute-start.4) | collective-permute-done | bytes 196640 | tf_op jit(solution)/shard_map/ppermute | solution.py:284
  202.6 5.0 collective-permute-start.17
  207.8 5.1 collective-permute-done.17
  213.6 4.4 copy.124
  218.0 4.2 copy.125
  222.2 2.9 broadcast_in_dim.238
  230.7 3.8 reshape.270
  236.7 3.8 reshape.271
  240.5 2.7 fusion.59
  246.2 2.4 collective-permute-start.12
  248.6 2.5 collective-permute-start.13
  253.7 2.7 collective-permute-done.12
  256.4 5.2 collective-permute-done.13
  262.1 13.0 %attend.3 = (bf16[192,2048]{1,0:T(8,128)(2,1)S(1)}, f32[8,2048]{1,0:T(8,128)S(1)}) custom-call(s32[4]{0:T(128)S(1)} %broadcast_11_counts_ref.2.counts_ref, bf16[192,2048]{1,0:T(8,128)(2,1)S(1)} %constant_dynamic-update-slice_fusion.16.q_ref, bf16[1024,192]{1,0:T(8,128)(2,1)S(1)} %convolution_convert_fusion.14.k_ref, bf16[1024,192]{1,0:T(8,128)(2,1)S(1)} %fusion.14.v_ref), custom_call_target="tpu_custom_call" | custom-call | flops 6442450944 | bytes 3145728 | tf_op jit(solution)/shard_map/attend/pallas_call | solution.py:62
  276.0 4.2 collective-permute-start.18
  281.9 3.6 copy.133
  285.5 3.8 reshape.272
  290.9 2.8 collective-permute-done.19
  293.8 4.1 collective-permute-done.20
  297.9 3.1 fusion.60
  305.7 10.5 %units.1 = (bf16[512,3072]{1,0:T(8,128)(2,1)S(1)}, bf16[512,3072]{1,0:T(8,128)(2,1)S(1)}, f32[512,768]{1,0:T(8,128)S(1)}) custom-call(bf16[512,768]{1,0:T(8,128)(2,1)S(1)} %fusion.13.x_ref, bf16[4,768,1536]{2,1,0:T(8,128)(2,1)} %bitcast.228, bf16[4,768,1536]{2,1,0:T(8,128)(2,1)} %bitcast.229, f32[1,3072]{1,0:T(1,128)S(1)} %bitcast.226), custom_call_target="tpu_custom_call" | custom-call | tf_op jit(solution)/shard_map/units/pallas_call | solution.py:206
  325.6 8.8 %units_back.1 = (bf16[512,3072]{1,0:T(8,128)(2,1)S(1)}, f32[1,3072]{1,0:T(1,128)S(1)}, f32[512,768]{1,0:T(8,128)S(1)}) custom-call(bf16[512,768]{1,0:T(8,128)(2,1)S(1)} %get-tuple-element.173.g_ref, bf16[4,768,1536]{2,1,0:T(8,128)(2,1)} %bitcast.230, bf16[4,768,1536]{2,1,0:T(8,128)(2,1)} %bitcast.231, bf16[512,3072]{1,0:T(8,128)(2,1)S(1)} %copy-done.1), custom_call_target="tpu_custom_call" | custom-call | tf_op jit(solution)/shard_map/units_back/pallas_call | solution.py:247
  334.4 2.9 convolution_convert_fusion
  337.3 2.8 convolution_convert_fusion.1
  340.2 2.8 convolution_convert_fusion.2
  343.0 2.8 convolution_convert_fusion.3
  345.8 2.5 multiply_reduce_fusion
  351.2 2.7 collective-permute-start.22
  356.3 4.0 collective-permute-done.21
  360.3 7.4 %collective-permute-done.22 = bf16[192,512]{1,0:T(8,128)(2,1)S(1)} collective-permute-done((bf16[192,512]{1,0:T(8,128)(2,1)S(1)}, bf16[192,512]{1,0:T(8,128)(2,1)S(1)}, u32[]{:S(2)}, u32[]{:S(2)}) %collective-permute-start.22) | collective-permute-done | bytes 196640 | tf_op jit(solution)/shard_map/ppermute | solution.py:284
  372.7 18.8 %attend_back.2 = (bf16[192,2048]{1,0:T(8,128)(2,1)S(1)}, bf16[384,1024]{1,0:T(8,128)(2,1)S(1)}) custom-call(s32[4]{0:T(128)S(1)} %broadcast_11_counts_ref.2.counts_ref, bf16[192,2048]{1,0:T(8,128)(2,1)S(1)} %constant_dynamic-update-slice_fusion.16.q_ref, bf16[192,2048]{1,0:T(8,128)(2,1)S(1)} %copy-done.3, bf16[192,2048]{1,0:T(8,128)(2,1)S(1)} %get-tuple-element.53.o_ref, ...), custom_call_target="tpu_custom_call" | custom-call | flops 16106127360 | bytes 6291456 | tf_op jit(solution)/shard_map/attend_back/pallas_call | solution.py:123
  393.3 3.5 convolution_convert_fusion.6
  398.9 4.1 collective-permute-start.26
  405.6 4.8 add_convert_fusion
  410.6 4.1 add_convert_fusion.1
  414.7 4.3 collective-permute-start.32
  421.2 3.4 multiply_reduce_fusion.1
  427.7 10.4 %collective-permute-start.29 = (bf16[192,512]{1,0:T(8,128)(2,1)}, bf16[192,512]{1,0:T(8,128)(2,1)}, u32[]{:S(2)}, u32[]{:S(2)}) collective-permute-start(bf16[192,512]{1,0:T(8,128)(2,1)} %get-tuple-element.195), channel_id=1, source_target_pairs={{0,1},{1,2},{2,3},{3,0},{4,5},{5,6},{6,7},{7,4},{8,9},{9,10},{10,1... | collective-permute-start | bytes 589832 | tf_op jit(solution)/shard_map/ppermute | solution.py:284
  438.0 3.3 collective-permute-start.30
  445.1 3.1 convolution_convert_fusion.8
  451.9 6.6 %collective-permute-done.30 = bf16[192,512]{1,0:T(8,128)(2,1)} collective-permute-done((bf16[192,512]{1,0:T(8,128)(2,1)}, bf16[192,512]{1,0:T(8,128)(2,1)}, u32[]{:S(2)}, u32[]{:S(2)}) %collective-permute-start.30) | collective-permute-done | bytes 196640 | tf_op jit(solution)/shard_map/ppermute | solution.py:284
  460.9 4.6 collective-permute-start.35
  467.0 26.8 %attend_back.3 = (bf16[192,2048]{1,0:T(8,128)(2,1)S(1)}, bf16[384,2048]{1,0:T(8,128)(2,1)}) custom-call(s32[8]{0:T(128)S(1)} %convert_reduce_fusion.8.counts_ref, bf16[192,2048]{1,0:T(8,128)(2,1)S(1)} %copy-done.9, bf16[192,2048]{1,0:T(8,128)(2,1)S(1)} %constant_dynamic-update-slice_fusion.g_ref, bf16[192,2048]{1,0:T(8,128)(2,1)S(1)} %get-tuple-element.50.o_ref, ...), custom_call_target="tpu_custom_call" | custom-call | flops 32212254720 | bytes 6291456 | tf_op jit(solution)/shard_map/attend_back/pallas_call | solution.py:123
  494.8 13.6 %reduce-scatter.6.cloned.1.call-done = bf16[96,1920]{1,0:T(8,128)(2,1)} async-done(((bf16[768,1920]{1,0:T(8,128)(2,1)}), bf16[96,1920]{1,0:T(8,128)(2,1)}) %reduce-scatter.6.cloned.1.call-update) | async-done | bytes 368656 | tf_op jit(solution)/shard_map/reduce_scatter | solution.py:405
  514.4 4.1 convolution_convert_fusion.4
  518.6 5.6 convolution_convert_fusion.10
  528.4 2.4 copy.141
  546.1 47.8 %all-reduce = (f32[10,768]{1,0:T(8,128)}, f32[3,768]{1,0:T(4,128)}, f32[3072]{0:T(1024)}) all-reduce(f32[10,768]{1,0:T(8,128)S(1)} %stack.98, f32[3,768]{1,0:T(4,128)S(1)} %pad_maximum_fusion.5, f32[3072]{0:T(1024)S(1)} %bitcast.227), channel_id=1, replica_groups=mesh['outer'=2,'mid'=2,'core'=2,'tensor'=4] {'outer','mid','core','tensor'}, use_global_device_ids=true, to_apply=%region_26.27 | all-reduce | flops 13056 | bytes 104448 | tf_op jit(solution)/shard_map/psum | solution.py:547
  600.0 2.6 collective-permute-start.50
  602.7 5.5 collective-permute-done.52
  611.4 6.0 collective-permute-start.40
  617.9 4.0 collective-permute-start.41
  624.7 3.3 collective-permute-start.44
  631.5 2.4 add_bitcast_fusion
  (418 shorter events, 132.2 us)
Async XLA Ops:
  7.2 68.6 %all-gather.6.cloned.1.call-start = ((), (), s32[]{:S(2)}) async-start(), calls=%async_computation.7 | async-start | bytes 3932160 | tf_op jit(solution)/shard_map/all_gather | solution.py:432
  7.9 297.8 %all-gather.4.cloned.1.call-start = ((), (), s32[]{:S(2)}) async-start(), calls=%async_computation.3 | async-start | bytes 9732096 | tf_op jit(solution)/shard_map/all_gather | solution.py:445
  10.7 448.8 %reduce-scatter.4.cloned.1.call-start = ((), (), s32[]{:S(2)}) async-start(), calls=%async_computation.4 | async-start | bytes 1966080 | tf_op jit(solution)/shard_map/reduce_scatter | solution.py:491
  11.1 1.6 collective-permute-start
  12.8 12.3 %collective-permute-start.1 = (bf16[2,96,960]{2,1,0:T(8,128)(2,1)S(1)}, bf16[2,96,960]{2,1,0:T(8,128)(2,1)S(1)}, u32[]{:S(2)}, u32[]{:S(2)}) collective-permute-start(bf16[2,96,960]{2,1,0:T(8,128)(2,1)S(1)} %broadcast_select_fusion.4), channel_id=1, source_target_pairs={{0,8},{8,0},{1,9},{9,1},{2,10},{10,2},{3,11},{11,3},{4,12},{12,4},... | collective-permute-start | bytes 1105928 | tf_op jit(solution)/shard_map/ppermute | solution.py:265
  15.8 72.5 %slice-start = ((f32[10,768]{1,0:T(8,128)}), f32[4,768]{1,0:T(4,128)S(1)}, s32[]{:S(2)}) async-start(f32[10,768]{1,0:T(8,128)} %param.19), calls=%async_computation.8 | async-start | bytes 24576 | tf_op jit(solution)/shard_map/slice | solution.py:448
  15.8 72.6 %copy-start.80 = (s32[1,8]{1,0:T(1,128)S(1)}, s32[1,8]{1,0:T(1,128)}, u32[]{:S(2)}) copy-start(s32[1,8]{1,0:T(1,128)} %param.13) | copy-start | bytes 100
  15.8 72.8 %copy-start.70 = (f32[10,768]{1,0:T(8,128)S(1)}, f32[10,768]{1,0:T(8,128)}, u32[]{:S(2)}) copy-start(f32[10,768]{1,0:T(8,128)} %param.19) | copy-start | bytes 92164
  25.3 63.4 %collective-permute-start.2 = (bf16[2,2,96,960]{3,2,1,0:T(8,128)(2,1)S(1)}, bf16[2,2,96,960]{3,2,1,0:T(8,128)(2,1)S(1)}, u32[]{:S(2)}, u32[]{:S(2)}) collective-permute-start(bf16[2,2,96,960]{3,2,1,0:T(8,128)(2,1)S(1)} %broadcast_select_fusion.3), channel_id=1, source_target_pairs={{0,16},{16,0},{1,17},{17,1},{2,18},{18,2},{3,19},{19,3},{4,20},{20... | collective-permute-start | bytes 2211848 | tf_op jit(solution)/shard_map/ppermute | solution.py:265
  75.8 8.0 %collective-permute-start.6 = (bf16[96,576]{1,0:T(8,128)(2,1)S(1)}, bf16[96,576]{1,0:T(8,128)(2,1)S(1)}, u32[]{:S(2)}, u32[]{:S(2)}) collective-permute-start(bf16[96,576]{1,0:T(8,128)(2,1)S(1)} %pad_maximum_fusion.4), channel_id=1, source_target_pairs={{0,1},{1,2},{2,3},{3,0},{4,5},{5,6},{6,7},{7,4},{8,9},{9,10},{10,1... | collective-permute-start | bytes 331784 | tf_op jit(solution)/shard_map/ppermute | solution.py:284
  75.8 12.1 %collective-permute-start.7 = (bf16[96,576]{1,0:T(8,128)(2,1)S(1)}, bf16[96,576]{1,0:T(8,128)(2,1)S(1)}, u32[]{:S(2)}, u32[]{:S(2)}) collective-permute-start(bf16[96,576]{1,0:T(8,128)(2,1)S(1)} %pad_maximum_fusion.4), channel_id=1, source_target_pairs={{0,2},{1,3},{2,0},{3,1},{4,6},{5,7},{6,4},{7,5},{8,10},{9,11},{10,... | collective-permute-start | bytes 331784 | tf_op jit(solution)/shard_map/ppermute | solution.py:284
  77.1 10.8 %collective-permute-start.8 = (bf16[96,576]{1,0:T(8,128)(2,1)S(1)}, bf16[96,576]{1,0:T(8,128)(2,1)S(1)}, u32[]{:S(2)}, u32[]{:S(2)}) collective-permute-start(bf16[96,576]{1,0:T(8,128)(2,1)S(1)} %pad_maximum_fusion.4), channel_id=1, source_target_pairs={{0,3},{1,0},{2,1},{3,2},{4,7},{5,4},{6,5},{7,6},{8,11},{9,8},{10,9... | collective-permute-start | bytes 331784 | tf_op jit(solution)/shard_map/ppermute | solution.py:284
  87.9 1.9 collective-permute-start.9
  88.7 209.2 %copy-start.77 = (f32[768]{0:T(1024)}, f32[768]{0:T(1024)S(1)}, u32[]{:S(2)}) copy-start(f32[768]{0:T(1024)S(1)} %get-tuple-element.163) | copy-start | bytes 9220
  88.9 124.0 %copy-start.48 = (bf16[768,960]{1,0:T(8,128)(2,1)}, bf16[768,960]{1,0:T(8,128)(2,1)S(1)}, u32[]{:S(2)}) copy-start(bf16[768,960]{1,0:T(8,128)(2,1)S(1)} %bitcast_select_fusion) | copy-start | bytes 4423684
  90.0 31.7 %collective-permute-start.10 = (bf16[2,4,96,576]{3,2,1,0:T(8,128)(2,1)S(1)}, bf16[2,4,96,576]{3,2,1,0:T(8,128)(2,1)S(1)}, u32[]{:S(2)}, u32[]{:S(2)}) collective-permute-start(bf16[2,4,96,576]{3,2,1,0:T(8,128)(2,1)S(1)} %broadcast_select_fusion.2), channel_id=1, source_target_pairs={{0,8},{8,0},{1,9},{9,1},{2,10},{10,2},{3,11},{11,3},{4,12},{12,4},... | collective-permute-start | bytes 2654216 | tf_op jit(solution)/shard_map/ppermute | solution.py:265
  123.2 94.7 %collective-permute-start.11 = (bf16[2,2,4,96,576]{4,3,2,1,0:T(8,128)(2,1)}, bf16[2,2,4,96,576]{4,3,2,1,0:T(8,128)(2,1)}, u32[]{:S(2)}, u32[]{:S(2)}) collective-permute-start(bf16[2,2,4,96,576]{4,3,2,1,0:T(8,128)(2,1)} %broadcast_select_fusion.1), channel_id=1, source_target_pairs={{0,16},{16,0},{1,17},{17,1},{2,18},{18,2},{3,19},{19,3},{4,20},{20... | collective-permute-start | bytes 5308424 | tf_op jit(solution)/shard_map/ppermute | solution.py:265
  150.0 10.5 %collective-permute-start.3 = (bf16[192,512]{1,0:T(8,128)(2,1)S(1)}, bf16[192,512]{1,0:T(8,128)(2,1)S(1)}, u32[]{:S(2)}, u32[]{:S(2)}) collective-permute-start(bf16[192,512]{1,0:T(8,128)(2,1)S(1)} %get-tuple-element.219), channel_id=1, source_target_pairs={{0,1},{1,2},{2,3},{3,0},{4,5},{5,6},{6,7},{7,4},{8,9},{9,10},{10,1... | collective-permute-start | bytes 589832 | tf_op jit(solution)/shard_map/ppermute | solution.py:284
  152.9 54.7 %collective-permute-start.15 = (bf16[256,768]{1,0:T(8,128)(2,1)S(1)}, bf16[256,768]{1,0:T(8,128)(2,1)S(1)}, u32[]{:S(2)}, u32[]{:S(2)}) collective-permute-start(bf16[256,768]{1,0:T(8,128)(2,1)S(1)} %bitcast.245), channel_id=1, source_target_pairs={{0,1},{1,2},{2,3},{3,0},{4,5},{5,6},{6,7},{7,4},{8,9},{9,10},{10,1... | collective-permute-start | bytes 1179656 | tf_op jit(solution)/shard_map/ppermute | solution.py:284
  153.7 54.0 %collective-permute-start.16 = (bf16[256,768]{1,0:T(8,128)(2,1)S(1)}, bf16[256,768]{1,0:T(8,128)(2,1)S(1)}, u32[]{:S(2)}, u32[]{:S(2)}) collective-permute-start(bf16[256,768]{1,0:T(8,128)(2,1)S(1)} %bitcast.246), channel_id=1, source_target_pairs={{0,2},{1,3},{2,0},{3,1},{4,6},{5,7},{6,4},{7,5},{8,10},{9,11},{10,... | collective-permute-start | bytes 1179656 | tf_op jit(solution)/shard_map/ppermute | solution.py:284
  154.6 48.0 %collective-permute-start.4 = (bf16[192,512]{1,0:T(8,128)(2,1)S(1)}, bf16[192,512]{1,0:T(8,128)(2,1)S(1)}, u32[]{:S(2)}, u32[]{:S(2)}) collective-permute-start(bf16[192,512]{1,0:T(8,128)(2,1)S(1)} %get-tuple-element.218), channel_id=1, source_target_pairs={{0,2},{1,3},{2,0},{3,1},{4,6},{5,7},{6,4},{7,5},{8,10},{9,11},{10,... | collective-permute-start | bytes 589832 | tf_op jit(solution)/shard_map/ppermute | solution.py:284
  160.6 47.0 %collective-permute-start.5 = (bf16[192,512]{1,0:T(8,128)(2,1)S(1)}, bf16[192,512]{1,0:T(8,128)(2,1)S(1)}, u32[]{:S(2)}, u32[]{:S(2)}) collective-permute-start(bf16[192,512]{1,0:T(8,128)(2,1)S(1)} %get-tuple-element.217), channel_id=1, source_target_pairs={{0,3},{1,0},{2,1},{3,2},{4,7},{5,4},{6,5},{7,6},{8,11},{9,8},{10,9... | collective-permute-start | bytes 589832 | tf_op jit(solution)/shard_map/ppermute | solution.py:284
  202.6 10.3 %collective-permute-start.17 = (bf16[256,768]{1,0:T(8,128)(2,1)S(1)}, bf16[256,768]{1,0:T(8,128)(2,1)S(1)}, u32[]{:S(2)}, u32[]{:S(2)}) collective-permute-start(bf16[256,768]{1,0:T(8,128)(2,1)S(1)} %bitcast.248), channel_id=1, source_target_pairs={{0,3},{1,0},{2,1},{3,2},{4,7},{5,4},{6,5},{7,6},{8,11},{9,8},{10,9... | collective-permute-start | bytes 1179656 | tf_op jit(solution)/shard_map/ppermute | solution.py:284
  246.2 10.2 %collective-permute-start.12 = (bf16[192,512]{1,0:T(8,128)(2,1)S(1)}, bf16[192,512]{1,0:T(8,128)(2,1)S(1)}, u32[]{:S(2)}, u32[]{:S(2)}) collective-permute-start(bf16[192,512]{1,0:T(8,128)(2,1)S(1)} %get-tuple-element.215), channel_id=1, source_target_pairs={{0,1},{1,2},{2,3},{3,0},{4,5},{5,6},{6,7},{7,4},{8,9},{9,10},{10,1... | collective-permute-start | bytes 589832 | tf_op jit(solution)/shard_map/ppermute | solution.py:284
  248.6 12.9 %collective-permute-start.13 = (bf16[192,512]{1,0:T(8,128)(2,1)S(1)}, bf16[192,512]{1,0:T(8,128)(2,1)S(1)}, u32[]{:S(2)}, u32[]{:S(2)}) collective-permute-start(bf16[192,512]{1,0:T(8,128)(2,1)S(1)} %get-tuple-element.214), channel_id=1, source_target_pairs={{0,2},{1,3},{2,0},{3,1},{4,6},{5,7},{6,4},{7,5},{8,10},{9,11},{10,... | collective-permute-start | bytes 589832 | tf_op jit(solution)/shard_map/ppermute | solution.py:284
  252.9 9.1 %collective-permute-start.14 = (bf16[192,512]{1,0:T(8,128)(2,1)S(1)}, bf16[192,512]{1,0:T(8,128)(2,1)S(1)}, u32[]{:S(2)}, u32[]{:S(2)}) collective-permute-start(bf16[192,512]{1,0:T(8,128)(2,1)S(1)} %get-tuple-element.213), channel_id=1, source_target_pairs={{0,3},{1,0},{2,1},{3,2},{4,7},{5,4},{6,5},{7,6},{8,11},{9,8},{10,9... | collective-permute-start | bytes 589832 | tf_op jit(solution)/shard_map/ppermute | solution.py:284
  276.0 14.0 %collective-permute-start.18 = (bf16[192,512]{1,0:T(8,128)(2,1)}, bf16[192,512]{1,0:T(8,128)(2,1)}, u32[]{:S(2)}, u32[]{:S(2)}) collective-permute-start(bf16[192,512]{1,0:T(8,128)(2,1)} %get-tuple-element.211), channel_id=1, source_target_pairs={{0,1},{1,2},{2,3},{3,0},{4,5},{5,6},{6,7},{7,4},{8,9},{9,10},{10,1... | collective-permute-start | bytes 589832 | tf_op jit(solution)/shard_map/ppermute | solution.py:284
  280.2 13.5 %collective-permute-start.19 = (bf16[192,512]{1,0:T(8,128)(2,1)}, bf16[192,512]{1,0:T(8,128)(2,1)S(1)}, u32[]{:S(2)}, u32[]{:S(2)}) collective-permute-start(bf16[192,512]{1,0:T(8,128)(2,1)} %get-tuple-element.210), channel_id=1, source_target_pairs={{0,2},{1,3},{2,0},{3,1},{4,6},{5,7},{6,4},{7,5},{8,10},{9,11},{10,... | collective-permute-start | bytes 589832 | tf_op jit(solution)/shard_map/ppermute | solution.py:284
  289.3 8.5 %collective-permute-start.20 = (bf16[192,512]{1,0:T(8,128)(2,1)}, bf16[192,512]{1,0:T(8,128)(2,1)S(1)}, u32[]{:S(2)}, u32[]{:S(2)}) collective-permute-start(bf16[192,512]{1,0:T(8,128)(2,1)} %get-tuple-element.209), channel_id=1, source_target_pairs={{0,3},{1,0},{2,1},{3,2},{4,7},{5,4},{6,5},{7,6},{8,11},{9,8},{10,9... | collective-permute-start | bytes 589832 | tf_op jit(solution)/shard_map/ppermute | solution.py:284
  350.5 9.7 %collective-permute-start.21 = (bf16[192,512]{1,0:T(8,128)(2,1)S(1)}, bf16[192,512]{1,0:T(8,128)(2,1)S(1)}, u32[]{:S(2)}, u32[]{:S(2)}) collective-permute-start(bf16[192,512]{1,0:T(8,128)(2,1)S(1)} %get-tuple-element.207), channel_id=1, source_target_pairs={{0,1},{1,2},{2,3},{3,0},{4,5},{5,6},{6,7},{7,4},{8,9},{9,10},{10,1... | collective-permute-start | bytes 589832 | tf_op jit(solution)/shard_map/ppermute | solution.py:284
  351.2 16.5 %collective-permute-start.22 = (bf16[192,512]{1,0:T(8,128)(2,1)S(1)}, bf16[192,512]{1,0:T(8,128)(2,1)S(1)}, u32[]{:S(2)}, u32[]{:S(2)}) collective-permute-start(bf16[192,512]{1,0:T(8,128)(2,1)S(1)} %get-tuple-element.206), channel_id=1, source_target_pairs={{0,2},{1,3},{2,0},{3,1},{4,6},{5,7},{6,4},{7,5},{8,10},{9,11},{10,... | collective-permute-start | bytes 589832 | tf_op jit(solution)/shard_map/ppermute | solution.py:284
  355.8 12.0 %collective-permute-start.23 = (bf16[192,512]{1,0:T(8,128)(2,1)S(1)}, bf16[192,512]{1,0:T(8,128)(2,1)S(1)}, u32[]{:S(2)}, u32[]{:S(2)}) collective-permute-start(bf16[192,512]{1,0:T(8,128)(2,1)S(1)} %get-tuple-element.205), channel_id=1, source_target_pairs={{0,3},{1,0},{2,1},{3,2},{4,7},{5,4},{6,5},{7,6},{8,11},{9,8},{10,9... | collective-permute-start | bytes 589832 | tf_op jit(solution)/shard_map/ppermute | solution.py:284
  368.7 22.8 %collective-permute-start.24 = (bf16[384,3072]{1,0:T(8,128)(2,1)}, bf16[384,3072]{1,0:T(8,128)(2,1)}, u32[]{:S(2)}, u32[]{:S(2)}) collective-permute-start(bf16[384,3072]{1,0:T(8,128)(2,1)} %convolution_convert_fusion.2), channel_id=1, source_target_pairs={{0,4},{4,0},{1,5},{5,1},{2,6},{6,2},{3,7},{7,3},{8,12},{12,8},{9,1... | collective-permute-start | bytes 7077896 | tf_op jit(solution)/shard_map/ppermute | solution.py:265
  368.7 22.8 %collective-permute-start.25 = (bf16[384,3072]{1,0:T(8,128)(2,1)}, bf16[384,3072]{1,0:T(8,128)(2,1)}, u32[]{:S(2)}, u32[]{:S(2)}) collective-permute-start(bf16[384,3072]{1,0:T(8,128)(2,1)} %convolution_convert_fusion), channel_id=1, source_target_pairs={{0,4},{4,0},{1,5},{5,1},{2,6},{6,2},{3,7},{7,3},{8,12},{12,8},{9,1... | collective-permute-start | bytes 7077896 | tf_op jit(solution)/shard_map/ppermute | solution.py:265
  398.9 20.3 %collective-permute-start.26 = (bf16[192,512]{1,0:T(8,128)(2,1)}, bf16[192,512]{1,0:T(8,128)(2,1)}, u32[]{:S(2)}, u32[]{:S(2)}) collective-permute-start(bf16[192,512]{1,0:T(8,128)(2,1)} %get-tuple-element.199), channel_id=1, source_target_pairs={{0,1},{1,2},{2,3},{3,0},{4,5},{5,6},{6,7},{7,4},{8,9},{9,10},{10,1... | collective-permute-start | bytes 589832 | tf_op jit(solution)/shard_map/ppermute | solution.py:284
  402.9 17.2 %collective-permute-start.27 = (bf16[192,512]{1,0:T(8,128)(2,1)}, bf16[192,512]{1,0:T(8,128)(2,1)}, u32[]{:S(2)}, u32[]{:S(2)}) collective-permute-start(bf16[192,512]{1,0:T(8,128)(2,1)} %get-tuple-element.198), channel_id=1, source_target_pairs={{0,2},{1,3},{2,0},{3,1},{4,6},{5,7},{6,4},{7,5},{8,10},{9,11},{10,... | collective-permute-start | bytes 589832 | tf_op jit(solution)/shard_map/ppermute | solution.py:284
  403.0 18.1 %collective-permute-start.28 = (bf16[192,512]{1,0:T(8,128)(2,1)}, bf16[192,512]{1,0:T(8,128)(2,1)S(1)}, u32[]{:S(2)}, u32[]{:S(2)}) collective-permute-start(bf16[192,512]{1,0:T(8,128)(2,1)} %get-tuple-element.197), channel_id=1, source_target_pairs={{0,3},{1,0},{2,1},{3,2},{4,7},{5,4},{6,5},{7,6},{8,11},{9,8},{10,9... | collective-permute-start | bytes 589832 | tf_op jit(solution)/shard_map/ppermute | solution.py:284
  405.3 103.1 %reduce-scatter.6.cloned.1.call-start = ((), (), s32[]{:S(2)}) async-start(), calls=%async_computation.5 | async-start | bytes 3317760 | tf_op jit(solution)/shard_map/reduce_scatter | solution.py:405
  410.4 49.1 %collective-permute-start.33 = (bf16[2,96,3072]{2,1,0:T(8,128)(2,1)}, bf16[2,96,3072]{2,1,0:T(8,128)(2,1)}, u32[]{:S(2)}, u32[]{:S(2)}) collective-permute-start(bf16[2,96,3072]{2,1,0:T(8,128)(2,1)} %get-tuple-element.182), channel_id=1, source_target_pairs={{0,16},{16,0},{1,17},{17,1},{2,18},{18,2},{3,19},{19,3},{4,20},{20... | collective-permute-start | bytes 3538952 | tf_op jit(solution)/shard_map/ppermute | solution.py:265
  414.7 44.8 %collective-permute-start.32 = (bf16[2,96,3072]{2,1,0:T(8,128)(2,1)}, bf16[2,96,3072]{2,1,0:T(8,128)(2,1)}, u32[]{:S(2)}, u32[]{:S(2)}) collective-permute-start(bf16[2,96,3072]{2,1,0:T(8,128)(2,1)} %get-tuple-element.184), channel_id=1, source_target_pairs={{0,8},{8,0},{1,9},{9,1},{2,10},{10,2},{3,11},{11,3},{4,12},{12,4},... | collective-permute-start | bytes 3538952 | tf_op jit(solution)/shard_map/ppermute | solution.py:265
  427.7 23.3 %collective-permute-start.29 = (bf16[192,512]{1,0:T(8,128)(2,1)}, bf16[192,512]{1,0:T(8,128)(2,1)}, u32[]{:S(2)}, u32[]{:S(2)}) collective-permute-start(bf16[192,512]{1,0:T(8,128)(2,1)} %get-tuple-element.195), channel_id=1, source_target_pairs={{0,1},{1,2},{2,3},{3,0},{4,5},{5,6},{6,7},{7,4},{8,9},{9,10},{10,1... | collective-permute-start | bytes 589832 | tf_op jit(solution)/shard_map/ppermute | solution.py:284
  438.0 20.5 %collective-permute-start.30 = (bf16[192,512]{1,0:T(8,128)(2,1)}, bf16[192,512]{1,0:T(8,128)(2,1)}, u32[]{:S(2)}, u32[]{:S(2)}) collective-permute-start(bf16[192,512]{1,0:T(8,128)(2,1)} %get-tuple-element.194), channel_id=1, source_target_pairs={{0,2},{1,3},{2,0},{3,1},{4,6},{5,7},{6,4},{7,5},{8,10},{9,11},{10,... | collective-permute-start | bytes 589832 | tf_op jit(solution)/shard_map/ppermute | solution.py:284
  441.3 18.1 %collective-permute-start.31 = (bf16[192,512]{1,0:T(8,128)(2,1)}, bf16[192,512]{1,0:T(8,128)(2,1)S(1)}, u32[]{:S(2)}, u32[]{:S(2)}) collective-permute-start(bf16[192,512]{1,0:T(8,128)(2,1)} %get-tuple-element.193), channel_id=1, source_target_pairs={{0,3},{1,0},{2,1},{3,2},{4,7},{5,4},{6,5},{7,6},{8,11},{9,8},{10,9... | collective-permute-start | bytes 589832 | tf_op jit(solution)/shard_map/ppermute | solution.py:284
  449.0 182.6 %reduce-scatter.8.cloned.1.call-start = ((), (), s32[]{:S(2)}) async-start(), calls=%async_computation.6 | async-start | bytes 3932160 | tf_op jit(solution)/shard_map/reduce_scatter | solution.py:518
  460.9 33.8 %collective-permute-start.35 = (bf16[96,3072]{1,0:T(8,128)(2,1)S(1)}, bf16[96,3072]{1,0:T(8,128)(2,1)}, u32[]{:S(2)}, u32[]{:S(2)}) collective-permute-start(bf16[96,3072]{1,0:T(8,128)(2,1)S(1)} %fusion.26), channel_id=1, source_target_pairs={{0,8},{8,0},{1,9},{9,1},{2,10},{10,2},{3,11},{11,3},{4,12},{12,4},... | collective-permute-start | bytes 1769480 | tf_op jit(solution)/shard_map/ppermute | solution.py:265
  466.9 27.8 %collective-permute-start.34 = (bf16[96,3072]{1,0:T(8,128)(2,1)S(1)}, bf16[96,3072]{1,0:T(8,128)(2,1)S(1)}, u32[]{:S(2)}, u32[]{:S(2)}) collective-permute-start(bf16[96,3072]{1,0:T(8,128)(2,1)S(1)} %fusion.25), channel_id=1, source_target_pairs={{0,16},{16,0},{1,17},{17,1},{2,18},{18,2},{3,19},{19,3},{4,20},{20... | collective-permute-start | bytes 1769480 | tf_op jit(solution)/shard_map/ppermute | solution.py:265
  510.6 89.4 %collective-permute-start.51 = (bf16[96,768]{1,0:T(8,128)(2,1)}, bf16[96,768]{1,0:T(8,128)(2,1)}, u32[]{:S(2)}, u32[]{:S(2)}) collective-permute-start(bf16[96,768]{1,0:T(8,128)(2,1)} %get-tuple-element.221), channel_id=1, source_target_pairs={{0,1},{1,2},{2,3},{3,0},{4,5},{5,6},{6,7},{7,4},{8,9},{9,10},{10,1... | collective-permute-start | bytes 442376 | tf_op jit(solution)/shard_map/ppermute | solution.py:284
  530.8 9.9 %collective-permute-start.36 = (bf16[384,1344]{0,1:T(8,128)(2,1)}, bf16[384,1344]{0,1:T(8,128)(2,1)}, u32[]{:S(2)}, u32[]{:S(2)}) collective-permute-start(bf16[384,1344]{0,1:T(8,128)(2,1)} %copy.141), channel_id=1, source_target_pairs={{0,4},{4,0},{1,5},{5,1},{2,6},{6,2},{3,7},{7,3},{8,12},{12,8},{9,1... | collective-permute-start | bytes 3096584 | tf_op jit(solution)/shard_map/ppermute | solution.py:265
  531.6 62.3 %collective-permute-start.45 = (bf16[96,192]{1,0:T(8,128)(2,1)}, bf16[96,192]{1,0:T(8,128)(2,1)S(1)}, u32[]{:S(2)}, u32[]{:S(2)}) collective-permute-start(bf16[96,192]{1,0:T(8,128)(2,1)} %get-tuple-element.238), channel_id=1, source_target_pairs={{0,1},{1,2},{2,3},{3,0},{4,5},{5,6},{6,7},{7,4},{8,9},{9,10},{10,1... | collective-permute-start | bytes 110600 | tf_op jit(solution)/shard_map/ppermute | solution.py:284
  533.2 62.6 %collective-permute-start.46 = (bf16[96,192]{1,0:T(8,128)(2,1)}, bf16[96,192]{1,0:T(8,128)(2,1)S(1)}, u32[]{:S(2)}, u32[]{:S(2)}) collective-permute-start(bf16[96,192]{1,0:T(8,128)(2,1)} %get-tuple-element.240), channel_id=1, source_target_pairs={{0,2},{1,3},{2,0},{3,1},{4,6},{5,7},{6,4},{7,5},{8,10},{9,11},{10,... | collective-permute-start | bytes 110600 | tf_op jit(solution)/shard_map/ppermute | solution.py:284
  534.8 62.9 %collective-permute-start.47 = (bf16[96,192]{1,0:T(8,128)(2,1)}, bf16[96,192]{1,0:T(8,128)(2,1)}, u32[]{:S(2)}, u32[]{:S(2)}) collective-permute-start(bf16[96,192]{1,0:T(8,128)(2,1)} %get-tuple-element.239), channel_id=1, source_target_pairs={{0,3},{1,0},{2,1},{3,2},{4,7},{5,4},{6,5},{7,6},{8,11},{9,8},{10,9... | collective-permute-start | bytes 110600 | tf_op jit(solution)/shard_map/ppermute | solution.py:284
  543.8 55.1 %collective-permute-start.37 = (bf16[2,96,1344]{2,1,0:T(8,128)(2,1)}, bf16[2,96,1344]{2,1,0:T(8,128)(2,1)S(1)}, u32[]{:S(2)}, u32[]{:S(2)}) collective-permute-start(bf16[2,96,1344]{2,1,0:T(8,128)(2,1)} %get-tuple-element.189), channel_id=1, source_target_pairs={{0,8},{8,0},{1,9},{9,1},{2,10},{10,2},{3,11},{11,3},{4,12},{12,4},... | collective-permute-start | bytes 1548296 | tf_op jit(solution)/shard_map/ppermute | solution.py:265
  593.9 14.2 %collective-permute-start.52 = (bf16[96,768]{1,0:T(8,128)(2,1)S(1)}, bf16[96,768]{1,0:T(8,128)(2,1)S(1)}, u32[]{:S(2)}, u32[]{:S(2)}) collective-permute-start(bf16[96,768]{1,0:T(8,128)(2,1)S(1)} %copy-done.68), channel_id=1, source_target_pairs={{0,2},{1,3},{2,0},{3,1},{4,6},{5,7},{6,4},{7,5},{8,10},{9,11},{10,... | collective-permute-start | bytes 442376 | tf_op jit(solution)/shard_map/ppermute | solution.py:284
  595.8 12.3 %collective-permute-start.53 = (bf16[96,768]{1,0:T(8,128)(2,1)S(1)}, bf16[96,768]{1,0:T(8,128)(2,1)S(1)}, u32[]{:S(2)}, u32[]{:S(2)}) collective-permute-start(bf16[96,768]{1,0:T(8,128)(2,1)S(1)} %copy-done.67), channel_id=1, source_target_pairs={{0,3},{1,0},{2,1},{3,2},{4,7},{5,4},{6,5},{7,6},{8,11},{9,8},{10,9... | collective-permute-start | bytes 442376 | tf_op jit(solution)/shard_map/ppermute | solution.py:284
  597.7 13.7 %collective-permute-start.48 = (bf16[96,768]{1,0:T(8,128)(2,1)}, bf16[96,768]{1,0:T(8,128)(2,1)S(1)}, u32[]{:S(2)}, u32[]{:S(2)}) collective-permute-start(bf16[96,768]{1,0:T(8,128)(2,1)} %get-tuple-element.224), channel_id=1, source_target_pairs={{0,1},{1,2},{2,3},{3,0},{4,5},{5,6},{6,7},{7,4},{8,9},{9,10},{10,1... | collective-permute-start | bytes 442376 | tf_op jit(solution)/shard_map/ppermute | solution.py:284
  598.9 19.0 %collective-permute-start.49 = (bf16[96,768]{1,0:T(8,128)(2,1)}, bf16[96,768]{1,0:T(8,128)(2,1)S(1)}, u32[]{:S(2)}, u32[]{:S(2)}) collective-permute-start(bf16[96,768]{1,0:T(8,128)(2,1)} %get-tuple-element.226), channel_id=1, source_target_pairs={{0,2},{1,3},{2,0},{3,1},{4,6},{5,7},{6,4},{7,5},{8,10},{9,11},{10,... | collective-permute-start | bytes 442376 | tf_op jit(solution)/shard_map/ppermute | solution.py:284
  600.0 21.9 %collective-permute-start.50 = (bf16[96,768]{1,0:T(8,128)(2,1)S(1)}, bf16[96,768]{1,0:T(8,128)(2,1)S(1)}, u32[]{:S(2)}, u32[]{:S(2)}) collective-permute-start(bf16[96,768]{1,0:T(8,128)(2,1)S(1)} %copy-done.69), channel_id=1, source_target_pairs={{0,3},{1,0},{2,1},{3,2},{4,7},{5,4},{6,5},{7,6},{8,11},{9,8},{10,9... | collective-permute-start | bytes 442376 | tf_op jit(solution)/shard_map/ppermute | solution.py:284
  608.1 16.5 %collective-permute-start.39 = (bf16[96,192]{1,0:T(8,128)(2,1)S(1)}, bf16[96,192]{1,0:T(8,128)(2,1)S(1)}, u32[]{:S(2)}, u32[]{:S(2)}) collective-permute-start(bf16[96,192]{1,0:T(8,128)(2,1)S(1)} %get-tuple-element.241), channel_id=1, source_target_pairs={{0,1},{1,2},{2,3},{3,0},{4,5},{5,6},{6,7},{7,4},{8,9},{9,10},{10,1... | collective-permute-start | bytes 110600 | tf_op jit(solution)/shard_map/ppermute | solution.py:284
  608.1 15.5 %collective-permute-start.38 = (bf16[96,1344]{1,0:T(8,128)(2,1)S(1)}, bf16[96,1344]{1,0:T(8,128)(2,1)S(1)}, u32[]{:S(2)}, u32[]{:S(2)}) collective-permute-start(bf16[96,1344]{1,0:T(8,128)(2,1)S(1)} %fusion.40), channel_id=1, source_target_pairs={{0,16},{16,0},{1,17},{17,1},{2,18},{18,2},{3,19},{19,3},{4,20},{20... | collective-permute-start | bytes 774152 | tf_op jit(solution)/shard_map/ppermute | solution.py:265
  611.4 16.6 %collective-permute-start.40 = (bf16[96,192]{1,0:T(8,128)(2,1)S(1)}, bf16[96,192]{1,0:T(8,128)(2,1)S(1)}, u32[]{:S(2)}, u32[]{:S(2)}) collective-permute-start(bf16[96,192]{1,0:T(8,128)(2,1)S(1)} %get-tuple-element.243), channel_id=1, source_target_pairs={{0,2},{1,3},{2,0},{3,1},{4,6},{5,7},{6,4},{7,5},{8,10},{9,11},{10,... | collective-permute-start | bytes 110600 | tf_op jit(solution)/shard_map/ppermute | solution.py:284
  617.9 10.1 %collective-permute-start.41 = (bf16[96,192]{1,0:T(8,128)(2,1)S(1)}, bf16[96,192]{1,0:T(8,128)(2,1)S(1)}, u32[]{:S(2)}, u32[]{:S(2)}) collective-permute-start(bf16[96,192]{1,0:T(8,128)(2,1)S(1)} %get-tuple-element.242), channel_id=1, source_target_pairs={{0,3},{1,0},{2,1},{3,2},{4,7},{5,4},{6,5},{7,6},{8,11},{9,8},{10,9... | collective-permute-start | bytes 110600 | tf_op jit(solution)/shard_map/ppermute | solution.py:284
  623.9 5.9 collective-permute-start.42
  623.9 5.9 collective-permute-start.43
  624.7 5.9 collective-permute-start.44
  (77 other events, 728.1 us)
Sparse Core Ops, SparseCore 0:
  9.6 66.1 all-gather.5
  79.3 119.0 all-gather.3
  405.4 46.7 reduce-scatter.3
  455.5 52.8 reduce-scatter.5
  518.7 63.5 reduce-scatter.7

commit v3 on v2

--- a/solution.py
+++ b/solution.py
@@ -261,148 +261,190 @@
     )(g, both, both, slope)
 
 
+COLUMN = ("core", "tensor")
+
+
+def place_of(sequence, quarter):
+    return (quarter // 2) * 4 + 2 * sequence + quarter % 2
+
+
+def relocated(x):
+    return lax.ppermute(x, COLUMN, [(s * 4 + t, place_of(s, t)) for s in range(2) for t in range(4)])
+
+
+def group_swapped(x, delta):
+    return lax.ppermute(x, COLUMN, [(place_of(s, q), place_of(s, q ^ delta)) for s in range(2) for q in range(4)])
+
+
+def quarter_rank():
+    return 2 * lax.axis_index("core") + lax.axis_index("tensor") % 2
+
+
+def half_rank():
+    return lax.axis_index("tensor") // 2
+
+
 def swapped(x, axis):
     return lax.ppermute(x, axis, [(0, 1), (1, 0)])
 
 
-def gather_axis(x, axis):
+def ordered(x, other, rank, dim=0):
+    place = lax.broadcasted_iota(jnp.int32, (1,) * dim + (2,) + (1,) * (x.ndim - dim), dim)
+    return jnp.where(place == rank, jnp.expand_dims(x, dim), jnp.expand_dims(other, dim))
+
+
+def gather_axis(x, axis, dim=0):
     if lax.axis_size(axis) != 2:
-        return lax.all_gather(x, axis, axis=0)
-    other = swapped(x, axis)
-    place = lax.broadcasted_iota(jnp.int32, (2,) + (1,) * x.ndim, 0)
-    return jnp.where(place == lax.axis_index(axis), x[None], other[None])
-
-
-def gather_over(x, axes):
-    for axis in axes:
-        x = gather_axis(x, axis)
-    return x
-
-
-def shifted(piece, step):
-    count = lax.axis_size("tensor")
-    return lax.ppermute(piece, "tensor", [(i, (i + step) % count) for i in range(count)])
-
-
-def exchange(take, put, start):
+        return lax.all_gather(x, axis, axis=dim)
+    return ordered(x, swapped(x, axis), lax.axis_index(axis), dim)
+
+
+def piece_of(x, index, size, dim):
+    return lax.dynamic_slice_in_dim(x, index * size, size, dim)
+
+
+def group_exchange(x, size, dim, out_dim, out_size):
+    rank = quarter_rank()
+    shape = list(x.shape)
+    shape[dim] = size
+    shape[out_dim] = 4 * out_size
+    got = [(group_swapped(piece_of(x, rank ^ d, size, dim), d), rank ^ d) for d in (3, 1, 2)]
+    out = jnp.zeros(tuple(shape), x.dtype)
+    for piece, source in [(piece_of(x, rank, size, dim), rank)] + got[::-1]:
+        out = lax.dynamic_update_slice_in_dim(out, piece, source * out_size, out_dim)
+    return out
+
+
+def tokens_to_heads(whole):
+    return group_exchange(whole, whole.shape[0] // 4, 0, 1, whole.shape[1])
+
+
+def heads_to_tokens(mine):
+    return group_exchange(mine, mine.shape[1] // 4, 1, 0, mine.shape[0])
+
+
+def gather_quarters(mine):
+    pair = ordered(mine, group_swapped(mine, 1), lax.axis_index("tensor") % 2)
+    whole = ordered(pair, group_swapped(pair, 2), lax.axis_index("core"))
+    return whole.reshape((-1,) + mine.shape[1:])
+
+
+def added(a, b):
+    return a.astype(jnp.float32) + b.astype(jnp.float32)
+
+
+def parts_of(x, rank, dim=0):
+    return (lax.dynamic_index_in_dim(x, rank, dim, keepdims=False),
+            lax.dynamic_index_in_dim(x, 1 - rank, dim, keepdims=False))
+
+
+def scatter_quarters(partial):
+    whole = partial.reshape((2, 2, -1) + partial.shape[1:])
+    keep, send = parts_of(whole, lax.axis_index("core"))
+    got = group_swapped(send, 2)
+    low = lax.axis_index("tensor") % 2
+    keep, send = [added(a, b) for a, b in zip(parts_of(keep, low), parts_of(got, low))]
+    return keep + group_swapped(send.astype(jnp.bfloat16), 1).astype(jnp.float32)
+
+
+def gather_shards(x):
     count = lax.axis_size("tensor")
     rank = lax.axis_index("tensor")
-    got = [(shifted(take((rank + s) % count), s), (rank - s) % count) for s in range(1, count)]
-    out = put(start, take(rank), rank)
-    for piece, source in got:
-        out = put(out, piece, source)
+    out = jnp.zeros((count,) + x.shape, x.dtype)
+    got = [(lax.ppermute(x, "tensor", [(i, (i + s) % count) for i in range(count)]), (rank - s) % count)
+           for s in range(1, count)]
+    for piece, source in [(x, rank)] + got:
+        out = lax.dynamic_update_slice_in_dim(out, piece[None], source, 0)
     return out
 
 
-def tokens_to_heads(whole):
-    count = lax.axis_size("tensor")
-    width = whole.shape[0] // count
-    own = whole.shape[1]
-    return exchange(
-        lambda d: lax.dynamic_slice_in_dim(whole, d * width, width, 0),
-        lambda out, piece, s: lax.dynamic_update_slice_in_dim(out, piece, s * own, 1),
-        jnp.zeros((width, count * own), whole.dtype),
-    )
-
-
-def heads_to_tokens(mine):
-    count = lax.axis_size("tensor")
-    width = mine.shape[0]
-    own = mine.shape[1] // count
-    return exchange(
-        lambda d: lax.dynamic_slice_in_dim(mine, d * own, own, 1),
-        lambda out, piece, s: lax.dynamic_update_slice_in_dim(out, piece, s * width, 0),
-        jnp.zeros((count * width, own), mine.dtype),
-    )
-
-
-def gather_tokens(mine):
-    count = lax.axis_size("tensor")
-    rank = lax.axis_index("tensor")
-    own = mine.shape[0]
-    out = jnp.zeros((count * own,) + mine.shape[1:], mine.dtype)
-    got = [(shifted(mine, s), (rank - s) % count) for s in range(1, count)]
-    out = lax.dynamic_update_slice_in_dim(out, mine, rank * own, 0)
-    for piece, source in got:
-        out = lax.dynamic_update_slice_in_dim(out, piece, source * own, 0)
-    return out
-
-
-def reduce_columns(partial):
+def column_sums(partial):
     count = lax.axis_size("tensor")
     rank = lax.axis_index("tensor")
     width = partial.shape[1] // count
-
-    def take(d):
-        return lax.dynamic_slice_in_dim(partial, d * width, width, 1)
-
-    total = take(rank).astype(jnp.float32)
+    total = piece_of(partial, rank, width, 1).astype(jnp.float32)
     for s in range(1, count):
-        total = total + shifted(take((rank + s) % count), s).astype(jnp.float32)
+        piece = piece_of(partial, (rank + s) % count, width, 1)
+        total = total + lax.ppermute(
+            piece, "tensor", [(i, (i + s) % count) for i in range(count)]).astype(jnp.float32)
     return total
+
+
+def interleaved(parts):
+    count = lax.axis_size("tensor")
+    rows = parts[0].shape[0]
+    return jnp.concatenate([p.reshape(rows, count, -1) for p in parts], axis=2).reshape(rows, -1)
+
+
+def summed_everywhere(x):
+    for axis in DP:
+        if lax.axis_size(axis) == 2:
+            x = x + swapped(x, axis)
+        else:
+            x = lax.psum(x, axis)
+    count = lax.axis_size("tensor")
+    for d in (1, 2):
+        x = x + lax.ppermute(x, "tensor", [(i, i ^ d) for i in range(count)])
+    return x
 
 
 def tied(*values):
     return lax.optimization_barrier(values)
 
 
-def parted(x, axis, dim):
-    rank = lax.axis_index(axis)
-    return (lax.dynamic_index_in_dim(x, rank, dim, keepdims=False),
-            lax.dynamic_index_in_dim(x, 1 - rank, dim, keepdims=False))
-
-
-class Flow:
-    def __init__(self, former, latter, axes):
-        self.axes = axes
-        self.pairs = all(lax.axis_size(a) == 2 for a in DP)
-        if not self.pairs:
-            self.moving = reduce_rows(dot_tn(former, latter).astype(jnp.bfloat16))
-            return
-        rows = former.shape[1] // lax.axis_size(DP)
-        mine, theirs = parted(former.reshape(-1, lax.axis_size(DP) // 2, 2, rows), "core", 2)
-        self.kept = dot_tn(mine.reshape(former.shape[0], -1), latter).astype(jnp.bfloat16)
-        self.sent = dot_tn(theirs.reshape(former.shape[0], -1), latter).astype(jnp.bfloat16)
-
-    @classmethod
-    def of(cls, partial, axes):
-        self = cls.__new__(cls)
-        self.axes = axes
-        self.pairs = all(lax.axis_size(a) == 2 for a in DP)
-        if not self.pairs:
-            self.moving = reduce_rows(partial)
-            return self
-        count = lax.axis_size(DP)
-        rows, cols = partial.shape[0] // count, partial.shape[1]
-        mine, theirs = parted(partial.reshape(count // 2, 2, rows, cols), "core", 1)
-        self.kept, self.sent = mine.reshape(-1, cols), theirs.reshape(-1, cols)
-        return self
-
-    def across_core(self):
-        if self.pairs:
-            self.moving = swapped(self.sent, "core")
-
-    def across(self, stage):
-        if not self.pairs:
-            return
-        if stage == 0:
-            whole = (2, 2, -1) + self.kept.shape[1:]
-            kept, got = self.kept.reshape(whole), self.moving.reshape(whole)
-            dim = DP.index(self.axes[0])
-        else:
-            kept, got, dim = self.kept, self.moving, 0
-        pieces = zip(parted(kept, self.axes[stage], dim), parted(got, self.axes[stage], dim))
-        keep, send = [(a.astype(jnp.float32) + b.astype(jnp.float32)).astype(jnp.bfloat16) for a, b in pieces]
-        self.kept, self.moving = keep, swapped(send, self.axes[stage])
-
-    def total(self):
-        if not self.pairs:
-            return self.moving
-        return (self.kept.astype(jnp.float32) + self.moving.astype(jnp.float32)).astype(jnp.bfloat16)
+def paired():
+    return lax.axis_size("outer") == 2
 
 
 def reduce_rows(partial):
     return lax.psum_scatter(partial, DP, scatter_dimension=0, tiled=True)
+
+
+def outer_scatter(partial, count):
+    return lax.psum_scatter(partial, "outer", scatter_dimension=0, tiled=True)
+
+
+class Flow:
+    def __init__(self, kept, got, axes):
+        self.axes = list(axes) if paired() else ["outer", "mid"]
+        lead = (lax.axis_size("outer"), 2, -1) + kept.shape[1:]
+        self.kept = kept.reshape(lead)
+        self.moving = None if got is None else got.reshape(lead)
+
+    def across(self):
+        axis = self.axes.pop(0)
+        low = jnp.bfloat16
+        if lax.axis_size(axis) != 2:
+            whole = self.kept if self.moving is None else added(self.kept, self.moving).astype(low)
+            self.kept = lax.psum_scatter(whole, axis, scatter_dimension=0, tiled=False)
+            self.moving = None
+            return
+        dim = 1 if axis == "mid" and self.axes else 0
+        rank = lax.axis_index(axis)
+        if self.moving is None:
+            keep, send = parts_of(self.kept, rank, dim)
+        else:
+            keep, send = [added(a, b).astype(low) for a, b in zip(
+                parts_of(self.kept, rank, dim), parts_of(self.moving, rank, dim))]
+        self.kept, self.moving = keep, swapped(send, axis)
+
+    def total(self):
+        if self.moving is None:
+            return self.kept
+        return added(self.kept, self.moving).astype(jnp.bfloat16)
+
+
+def core_halves(former, latter):
+    rows = former.shape[1] // lax.axis_size(DP)
+    halves = parts_of(former.reshape(former.shape[0], -1, 2, rows), lax.axis_index("core"), 2)
+    return [dot_tn(h.reshape(former.shape[0], -1), latter).astype(jnp.bfloat16) for h in halves]
+
+
+def shard_total(summed):
+    rank = half_rank()
+    keep, send = parts_of(summed.reshape(2, -1, summed.shape[-1]), rank)
+    got = lax.ppermute(send, "tensor", [(i, i ^ 2) for i in range(4)])
+    return relocated(added(keep, got).astype(jnp.bfloat16)).astype(jnp.float32)
 
 
 def body(
@@ -419,43 +461,56 @@
     up_bias,
 ):
     low = jnp.bfloat16
-    tensor_count = lax.axis_size("tensor")
-    tensor_rank = lax.axis_index("tensor")
-    width = D // tensor_count
+    count = lax.axis_size("tensor")
+    width = D // count
     scale = HD ** (-0.5)
-    start = tensor_rank * width
-    rows = inputs[0]
-    ids = block_ids[0]
+    quarter = quarter_rank()
+    start = quarter * width
+    core = lax.axis_index("core")
 
     in_low = in_weight.astype(low)
     shards = in_low.shape[1]
-    hidden_self = lax.all_gather(rows, "tensor", axis=0, tiled=True)
-    head_pack = jnp.concatenate([in_low[0], in_low[1], in_low[2], in_low[4], in_low[5]], axis=1)
-    head_pack = gather_over(head_pack, ("core", "mid", "outer")).reshape(D, 5 * width)
-    w_self = head_pack[:, : 3 * width]
-    w_cross = head_pack[:, 3 * width :]
+    rows = relocated(inputs[0])
+    qkv_all = gather_shards(jnp.concatenate([in_low[0], in_low[1], in_low[2]], axis=1))
+    hidden_self = gather_quarters(rows)
+
+    def own_shard(stacked):
+        mine = lax.dynamic_index_in_dim(stacked, quarter, 0, keepdims=False)
+        theirs = lax.dynamic_index_in_dim(stacked, quarter ^ 2, 0, keepdims=False)
+        return ordered(mine, swapped(theirs, "core"), core)
+
+    w_self = gather_axis(gather_axis(own_shard(qkv_all), "mid"), "outer").reshape(D, 3 * width)
+    unit_pack = jnp.concatenate([up_weight.astype(low), down_weight.astype(low).T], axis=1)
+    unit_pack = lax.all_gather(unit_pack, ("tensor",) + DP, axis=0, tiled=True).reshape(count, D, -1)
     out_turned = jnp.swapaxes(out_weight.astype(low), 1, 2)
-    mid_pack = jnp.concatenate([in_low[3], out_turned[0], out_turned[1]], axis=1)
-    encoder, mid_pack, hidden_self = tied(encoder_out[0], mid_pack, hidden_self)
-    mid_pack = gather_over(gather_tokens(mid_pack).reshape(tensor_count, shards, 3 * width), ("core", "mid", "outer"))
-    mid_pack = mid_pack.reshape(D // shards, tensor_count, shards, 3, width)
-    wq_cross, wo_self, wo_cross = (
-        jnp.swapaxes(mid_pack[:, :, :, n], 1, 2).reshape(D, D) for n in range(3))
-    unit_pack = jnp.concatenate([up_weight.astype(low), down_weight.astype(low).T], axis=1)
-    unit_pack = lax.all_gather(unit_pack, ("tensor",) + DP, axis=0, tiled=True).reshape(tensor_count, D, -1)
-    encoder_full = gather_tokens(encoder)
-
+    mid_all = jnp.concatenate([in_low[4], in_low[5], in_low[3], out_turned[0], out_turned[1]], axis=1)
+    encoder, mid_all, hidden_self = tied(encoder_out[0], mid_all, hidden_self)
+    mid_all = gather_shards(mid_all)
+    encoder = relocated(encoder)
+    kv_mine = own_shard(mid_all[:, :, : 2 * width])
+    full = jnp.transpose(mid_all[:, :, 2 * width :].reshape(count, shards, 3, width), (1, 2, 0, 3))
+    pack = jnp.concatenate([kv_mine[0], kv_mine[1], full.reshape(shards, 3 * D)], axis=1)
+    pack = gather_axis(gather_axis(pack, "mid"), "outer")
+    encoder_full = gather_quarters(encoder)
+
+    ids = block_ids[0]
+    ids = jnp.where(core == half_rank(), ids, swapped(ids, "core"))
     head_bias = lax.dynamic_slice_in_dim(vectors[0:4], start, width, 1)
     counts_self = jnp.sum((ids[None, :] <= ids[:, None]).astype(jnp.int32), axis=1)
-    counts_cross = jnp.full((ids.shape[0] // 2,), encoder_full.shape[0] // KB, jnp.int32)
+    counts_cross = jnp.full((ids.shape[0] // 2,), 4 * encoder.shape[0] // KB, jnp.int32)
 
     q_self = ((dot_tt(w_self[:, :width], hidden_self) + head_bias[0][:, None]) * scale).astype(low)
     k_self = dot_nn(hidden_self, w_self[:, width : 2 * width]).astype(low)
     v_self = (dot_nn(hidden_self, w_self[:, 2 * width :]) + head_bias[1]).astype(low)
     mine_self, lse_self = attend(counts_self, q_self, k_self, v_self)
+    mixed_self = heads_to_tokens(mine_self)
+    mine_self, pack, encoder_full = tied(mine_self, pack, encoder_full)
+    upstream = relocated(out_grad[0])
+    w_cross = jnp.stack([pack[..., : 2 * width], pack[..., 2 * width : 4 * width]], axis=2).reshape(D, 2 * width)
+    projections = gather_axis(pack[..., 4 * width :], "core", 2).reshape(D, 3 * D)
+    wq_cross, wo_self, wo_cross = (projections[:, n * D : (n + 1) * D] for n in range(3))
     k_cross = dot_nn(encoder_full, w_cross[:, :width]).astype(low)
     v_cross = (dot_nn(encoder_full, w_cross[:, width:]) + head_bias[3]).astype(low)
-    mixed_self = heads_to_tokens(mine_self)
     summed_one = rows.astype(jnp.float32) + (dot_tt(mixed_self, wo_self) + vectors[4])
     normed_one = layer_norm(summed_one, norm_gains[0], vectors[7])
     hidden_cross = normed_one.astype(low)
@@ -469,93 +524,92 @@
     summed_three = normed_two + (unit_out + vectors[6])
     layer_out = layer_norm(summed_three, norm_gains[2], vectors[9]).astype(low)
 
-    grad_three, gain_three, shift_three = layer_norm_back(out_grad[0].astype(jnp.float32), summed_three, norm_gains[2])
+    grad_three, gain_three, shift_three = layer_norm_back(upstream.astype(jnp.float32), summed_three, norm_gains[2])
     branch_three = grad_three.astype(low)
     bias_down = jnp.sum(branch_three.astype(jnp.float32), axis=0)
     grad_before, unit_bias, unit_back = units_back(branch_three, unit_pack, slope)
     grad_two, gain_two, shift_two = layer_norm_back(grad_three + unit_back, summed_two, norm_gains[1])
     branch_two = grad_two.astype(low)
     bias_cross_out = jnp.sum(branch_two.astype(jnp.float32), axis=0)
-    down = Flow(branch_three, active, ("mid", "outer"))
-    up = Flow(hidden_units, grad_before, ("outer", "mid"))
     grad_mixed_cross = tokens_to_heads(dot_tt(wo_cross, branch_two).astype(low))
-    out_grad_cross = dot_tt(branch_two, mixed_cross).astype(low)
-    if down.pairs:
-        grad_mixed_cross, out_grad_cross, down.kept, down.sent, up.kept, up.sent = tied(
-            grad_mixed_cross, out_grad_cross, down.kept, down.sent, up.kept, up.sent)
-    down.across_core()
-    up.across_core()
+    down_kept, down_sent = core_halves(branch_three, active)
+    up_kept, up_sent = core_halves(hidden_units, grad_before)
+    grad_mixed_cross, down_kept, down_sent, up_kept, up_sent = tied(
+        grad_mixed_cross, down_kept, down_sent, up_kept, up_sent)
+    down_got, up_got = swapped(down_sent, "core"), swapped(up_sent, "core")
+    layer_out = relocated(layer_out)
     dq_mine, dkv_cross = attend_back(
         counts_cross, q_cross, grad_mixed_cross, mine_cross, lse_cross, k_cross, v_cross, bq=512)
-    dq_mine, dkv_cross, down.moving, up.moving = tied(dq_mine, dkv_cross, down.moving, up.moving)
-    encoder_part = lax.psum_scatter(
-        dot_tt(dkv_cross, w_cross).astype(low), "tensor", scatter_dimension=0, tiled=True)
-    kv_grad = dot_tt(encoder_full, dkv_cross).astype(low)
+    dq_mine, dkv_cross, down_got, up_got, layer_out = tied(dq_mine, dkv_cross, down_got, up_got, layer_out)
     dq_cross = heads_to_tokens(dq_mine)
+    down = Flow(down_kept, down_got, ("mid", "outer"))
+    up = Flow(up_kept, up_got, ("outer", "mid"))
+    down.across()
+    up.across()
+    encoder_part = dot_tt(dkv_cross, w_cross).astype(low)
+    kv_flow = Flow(dot_tt(encoder_full, dkv_cross).astype(low), None, ("mid", "outer"))
+    out_grad_cross = dot_tt(branch_two, mixed_cross).astype(low)
     bias_query_cross = jnp.sum(dq_cross.astype(jnp.float32), axis=1)
     bias_value_cross = jnp.sum(dkv_cross[width:].astype(jnp.float32), axis=1)
-    down.across(0)
-    up.across(0)
-    query_grad_cross = dot_tt(hidden_cross, dq_cross).astype(low)
-    cross_grads = reduce_rows(jnp.concatenate([query_grad_cross, out_grad_cross, kv_grad], axis=1))
     grad_one_in = grad_two + dot_tt(dq_cross, wq_cross)
     grad_one, gain_one, shift_one = layer_norm_back(grad_one_in, summed_one, norm_gains[0])
     branch_one = grad_one.astype(low)
     bias_self_out = jnp.sum(branch_one.astype(jnp.float32), axis=0)
     grad_mixed_self = tokens_to_heads(dot_tt(wo_self, branch_one).astype(low))
+    query_grad_cross = dot_tt(hidden_cross, dq_cross).astype(low)
     out_grad_self = dot_tt(branch_one, mixed_self).astype(low)
-    grad_mixed_self, down.moving, up.moving, out_grad_self, encoder_part = tied(
-        grad_mixed_self, down.moving, up.moving, out_grad_self, encoder_part)
-    down.across(1)
-    up.across(1)
+    square_grads = reduce_rows(jnp.concatenate([query_grad_cross, out_grad_self, out_grad_cross], axis=1))
+    grad_mixed_self, down.moving, up.moving, query_grad_cross, out_grad_self, encoder_part = tied(
+        grad_mixed_self, down.moving, up.moving, query_grad_cross, out_grad_self, encoder_part)
+    down.across()
+    up.across()
+    kv_flow.across()
+    encoder_sum = scatter_quarters(encoder_part)
     dq_self, dkv_self = attend_back(
         counts_self, q_self, grad_mixed_self, mine_self, lse_self, k_self, v_self)
-    dq_self, dkv_self, down.moving, up.moving, cross_grads = tied(
-        dq_self, dkv_self, down.moving, up.moving, cross_grads)
+    dq_self, dkv_self, down.moving, up.moving, kv_flow.moving, encoder_sum = tied(
+        dq_self, dkv_self, down.moving, up.moving, kv_flow.moving, encoder_sum)
     dqkv = jnp.concatenate([dq_self, dkv_self], axis=0)
     input_part = dot_tt(dqkv, w_self).astype(low)
     input_part, dqkv = tied(input_part, dqkv)
-    input_grad = grad_one + lax.psum_scatter(
-        input_part, "tensor", scatter_dimension=0, tiled=True).astype(jnp.float32)
-    self_flow = Flow.of(
-        jnp.concatenate([out_grad_self, dot_tt(hidden_self, dqkv).astype(low)], axis=1), ("mid", "outer"))
-    self_flow.across_core()
-    self_flow.across(0)
-    self_flow.across(1)
-    self_grads = self_flow.total()
+    input_sum = grad_one + scatter_quarters(input_part)
+    input_grad = relocated(input_sum.astype(low)).astype(jnp.float32)
+    self_flow = Flow(dot_tt(hidden_self, dqkv).astype(low), None, ("outer", "mid"))
+    self_flow.across()
+    kv_flow.across()
+    self_flow.across()
+    head_grads = shard_total(jnp.concatenate([
+        t.reshape(-1, t.shape[-1]) for t in (self_flow.total(), kv_flow.total())], axis=1))
+    encoder_grad = relocated(encoder_sum.astype(low)).astype(jnp.float32)
     bias_query_self = jnp.sum(dq_self.astype(jnp.float32), axis=1)
     bias_value_self = jnp.sum(dkv_self[width:].astype(jnp.float32), axis=1)
 
-    encoder_grad = encoder_part.astype(jnp.float32)
-    query_shard = reduce_columns(cross_grads[:, :D])
-    out_shard = jnp.stack([reduce_columns(self_grads[:, :D]).T, reduce_columns(cross_grads[:, D : 2 * D]).T])
-    kv_shard = cross_grads[:, 2 * D :].astype(jnp.float32)
-    self_shard = self_grads[:, D:].astype(jnp.float32)
-    up_shard = reduce_columns(up.total())
-    down_shard = reduce_columns(down.total()).T
-    in_shard = jnp.stack([
-        self_shard[:, :width], self_shard[:, width : 2 * width], self_shard[:, 2 * width :],
-        query_shard, kv_shard[:, :width], kv_shard[:, width:]])
+    unit_sums = column_sums(interleaved([t.reshape(shards, -1) for t in (up.total(), down.total())]))
+    units_here = unit_sums.shape[1] // 2
+    square_sums = column_sums(interleaved([square_grads[:, n * D : (n + 1) * D] for n in range(3)]))
+    head = [head_grads[:, n * width : (n + 1) * width] for n in range(5)]
+    in_shard = jnp.stack([head[0], head[1], head[2], square_sums[:, :width], head[3], head[4]])
+    out_shard = jnp.stack([square_sums[:, width : 2 * width].T, square_sums[:, 2 * width :].T])
 
     def embed(part):
         return lax.dynamic_update_slice_in_dim(jnp.zeros((D,), jnp.float32), part, start, 0)
 
-    vector_grad = jnp.stack([
+    small = jnp.stack([
         embed(bias_query_self), embed(bias_value_self), bias_query_cross, embed(bias_value_cross),
-        bias_self_out, bias_cross_out, bias_down, shift_one, shift_two, shift_three])
-    gain_grad = jnp.stack([gain_one, gain_two, gain_three])
-    vector_total, gain_total, unit_total = lax.psum((vector_grad, gain_grad, unit_bias[0]), EVERY)
+        bias_self_out, bias_cross_out, bias_down, shift_one, shift_two, shift_three,
+        gain_one, gain_two, gain_three])
+    small = summed_everywhere(jnp.concatenate([small, unit_bias.reshape(-1, D)], axis=0))
     return (
         layer_out[None],
         input_grad[None],
         encoder_grad[None],
         in_shard,
         out_shard,
-        up_shard,
-        down_shard,
-        vector_total,
-        gain_total,
-        unit_total,
+        unit_sums[:, :units_here],
+        unit_sums[:, units_here:].T,
+        small[:10],
+        small[10:13],
+        small[13:].reshape(-1),
     )
 
 

time: 650 us -> 590 us (0.908)
  blocking collectives: 47.8 us -> 0 us
  waiting for transfers between devices: 202 us -> 156 us
  starting transfers between devices: 103 us -> 131 us
  other arithmetic: 43.5 us -> 56.1 us
  local copies, waits for them, and re-layouts: 76.4 us -> 65.6 us
    all_gather x1 -> x0, waiting for transfers between devices: 48.7 us -> none  [body(): hidden_self = lax.all_gather(rows, 'tensor', axis=0, tiled=True)]
    psum x1 -> x0, blocking collectives: 47.8 us -> none  [body(): lax.psum((vector_grad, gain_grad, unit_bias[0]), EVERY)]
    ppermute x39 -> x48, starting transfers between devices: 80.9 us -> 114 us  [the longest x6 37.7 us: gather_shards(): lax.ppermute(x, 'tensor', [(i, (i + s) % count) for i in range(count)])]
    ppermute x39 -> x48, waiting for transfers between devices: 101 us -> 120 us  [the longest x26 54.2 us: group_swapped(): lax.ppermute(x, COLUMN, [(place_of(s, q), place_of(s, q ^ delta)) for s i...]
    reduce_scatter x3 -> x0, waiting for transfers between devices: 13.6 us -> none  [the longest x1 13.6 us: reduce_rows(): return lax.psum_scatter(partial, DP, scatter_dimension=0, tiled=True)]
    reshape x4 -> x9, local copies, waits for them, and re-layouts: 13.8 us -> 3.73 us  [the longest x5 2.2 us: interleaved(): p.reshape(rows, count, -1)]
    unnamed x169 -> x184, local copies, waits for them, and re-layouts: 17.6 us -> 27.4 us
    transpose x4 -> x2, local copies, waits for them, and re-layouts: 9.48 us -> 1.84 us  [the longest x1 0.99 us: body(): jnp.transpose(mid_all[:, :, 2 * width:].reshape(count, shards, 3, width),...]
  transfers between devices with their start and end apart: 59 -> 71, of which waited for: 24 -> 28; matrix products, arithmetic and copies ran while one was open for 19% -> 21% of each run, Pallas kernels for 13% -> 17%
where the time goes in v3:
time: 590 us; the launch traced here: 582 us
  waiting for transfers between devices  156 us (26%)
  starting transfers between devices  131 us (22%)
  Pallas kernels  106 us (18%)
  local copies, waits for them, and re-layouts  65.6 us (11%)
  other arithmetic  56.1 us (10%)
  matrix products  51.1 us (9%)
  between operations  16.3 us (3%)
    ppermute x26, waiting for transfers between devices, group_swapped(): lax.ppermute(x, COLUMN, [(place_of(s, q), place_of(s, q ^ delta)) for s i...  54.2 us
    pallas_call x2, Pallas kernels, attend_back(): pl.pallas_call(functools.partial(attend_back_kernel, heads=heads, blocks=...  47.1 us
    pallas_call x2, Pallas kernels, attend(): pl.pallas_call(functools.partial(attend_kernel, heads=heads, blocks=block...  40 us
    ppermute x6, starting transfers between devices, gather_shards(): lax.ppermute(x, 'tensor', [(i, (i + s) % count) for i in range(count)])  37.7 us
    ppermute x21, waiting for transfers between devices, swapped(): return lax.ppermute(x, axis, [(0, 1), (1, 0)])  36.3 us
    dot_general x14, matrix products, dot_tt(): lax.dot_general(former, latter, (((0,), (1,)), ((), ())), preferred_eleme...  35.4 us
    ppermute x6, waiting for transfers between devices, gather_shards(): lax.ppermute(x, 'tensor', [(i, (i + s) % count) for i in range(count)])  31.6 us
    ppermute x26, starting transfers between devices, group_swapped(): lax.ppermute(x, COLUMN, [(place_of(s, q), place_of(s, q ^ delta)) for s i...  28.6 us
  transfers between devices with their start and end apart: 71, of which 28 were waited for; matrix products, arithmetic and copies ran while one was open for 21% of the time, Pallas kernels for 17%

profile of v3, /device:TPU:0, one launch (start us, length us, event | category | flops | bytes accessed | tf_op | source)
XLA Modules:
  0.0 581.8 jit_solution(11983505686514174529)
XLA Ops:
  11.0 3.1 collective-permute-start.8
  15.2 30.9 %collective-permute-start.2 = (bf16[96,576]{1,0:T(8,128)(2,1)S(1)}, bf16[96,576]{1,0:T(8,128)(2,1)S(1)}, u32[]{:S(2)}, u32[]{:S(2)}) collective-permute-start(bf16[96,576]{1,0:T(8,128)(2,1)S(1)} %get-tuple-element.176), channel_id=1, source_target_pairs={{0,2},{1,3},{2,0},{3,1},{4,6},{5,7},{6,4},{7,5},{8,10},{9,11},{10,... | collective-permute-start | bytes 331784 | tf_op jit(solution)/shard_map/ppermute | solution.py:354
  46.0 2.4 collective-permute-start.3
  48.5 23.9 %collective-permute-done.1 = bf16[96,576]{1,0:T(8,128)(2,1)S(1)} collective-permute-done((bf16[96,576]{1,0:T(8,128)(2,1)S(1)}, bf16[96,576]{1,0:T(8,128)(2,1)S(1)}, u32[]{:S(2)}, u32[]{:S(2)}) %collective-permute-start.1) | collective-permute-done | bytes 110624 | tf_op jit(solution)/shard_map/ppermute | solution.py:354
  75.2 4.4 collective-permute-done.4
  85.2 10.1 %collective-permute-done.5 = bf16[2,96,576]{2,1,0:T(8,128)(2,1)} collective-permute-done((bf16[2,96,576]{2,1,0:T(8,128)(2,1)S(1)}, bf16[2,96,576]{2,1,0:T(8,128)(2,1)}, u32[]{:S(2)}, u32[]{:S(2)}) %collective-permute-start.5) | collective-permute-done | bytes 221216 | tf_op jit(solution)/shard_map/ppermute | solution.py:288
  98.8 10.2 %collective-permute-done.6 = bf16[2,2,96,576]{3,2,1,0:T(8,128)(2,1)S(1)} collective-permute-done((bf16[2,2,96,576]{3,2,1,0:T(8,128)(2,1)S(1)}, bf16[2,2,96,576]{3,2,1,0:T(8,128)(2,1)S(1)}, u32[]{:S(2)}, u32[]{:S(2)}) %collective-permute-start.6) | collective-permute-done | bytes 442400 | tf_op jit(solution)/shard_map/ppermute | solution.py:288
  116.3 2.0 fusion.v_ref
  120.0 6.1 %collective-permute-done.11 = bf16[96,960]{1,0:T(8,128)(2,1)S(1)} collective-permute-done((bf16[96,960]{1,0:T(8,128)(2,1)S(1)}, bf16[96,960]{1,0:T(8,128)(2,1)S(1)}, u32[]{:S(2)}, u32[]{:S(2)}) %collective-permute-start.11) | collective-permute-done | bytes 184352 | tf_op jit(solution)/shard_map/ppermute | solution.py:354
  129.5 8.9 %collective-permute-start.17 = (bf16[256,768]{1,0:T(8,128)(2,1)S(1)}, bf16[256,768]{1,0:T(8,128)(2,1)S(1)}, u32[]{:S(2)}, u32[]{:S(2)}) collective-permute-start(bf16[256,768]{1,0:T(8,128)(2,1)S(1)} %collective-permute-done.16), channel_id=1, source_target_pairs={{0,1},{1,0},{4,5},{5,4},{2,3},{3,2},{6,7},{7,6},{8,9},{9,8},{12,13... | collective-permute-start | bytes 1179656 | tf_op jit(solution)/shard_map/ppermute | solution.py:276
  140.1 3.3 fusion.2.q_ref
  143.4 4.1 collective-permute-done.17
  148.8 5.2 collective-permute-done.14
  155.8 26.5 %attend.2 = (bf16[192,2048]{1,0:T(8,128)(2,1)S(1)}, f32[8,2048]{1,0:T(8,128)S(1)}) custom-call(s32[8]{0:T(128)S(1)} %convert_reduce_fusion.8.counts_ref, bf16[192,2048]{1,0:T(8,128)(2,1)S(1)} %fusion.2.q_ref, bf16[2048,192]{1,0:T(8,128)(2,1)S(1)} %convolution_convert_fusion.5.k_ref, bf16[2048,192]{1,0:T(8,128)(2,1)S(1)} %copy-done.13), custom_call_target="tpu_custom_call" | custom-call | flops 12884901888 | bytes 3145728 | tf_op jit(solution)/shard_map/attend/pallas_call | solution.py:62
  189.7 4.6 collective-permute-done.21
  194.3 2.3 collective-permute-done.22
  197.5 2.6 bitcast_select_fusion
  206.1 5.7 collective-permute-done.24
  211.8 2.4 collective-permute-done.25
  214.3 13.4 %attend.3 = (bf16[192,2048]{1,0:T(8,128)(2,1)S(1)}, f32[8,2048]{1,0:T(8,128)S(1)}) custom-call(s32[4]{0:T(128)S(1)} %broadcast_11_counts_ref.2.counts_ref, bf16[192,2048]{1,0:T(8,128)(2,1)S(1)} %constant_dynamic-update-slice_fusion.12.q_ref, bf16[1024,192]{1,0:T(8,128)(2,1)S(1)} %convolution_convert_fusion.14.k_ref, bf16[1024,192]{1,0:T(8,128)(2,1)S(1)} %fusion.16.v_ref), custom_call_target="tpu_custom_call" | custom-call | flops 6442450944 | bytes 3145728 | tf_op jit(solution)/shard_map/attend/pallas_call | solution.py:62
  229.6 7.5 %collective-permute-start.29 = (bf16[512,768]{1,0:T(8,128)(2,1)}, bf16[512,768]{1,0:T(8,128)(2,1)}, u32[]{:S(2)}, u32[]{:S(2)}) collective-permute-start(bf16[512,768]{1,0:T(8,128)(2,1)} %bitcast.46), channel_id=1, source_target_pairs={{0,0},{1,1},{2,4},{3,5},{4,2},{5,3},{6,6},{7,7},{8,8},{9,9},{10,12... | collective-permute-start | bytes 2359304 | tf_op jit(solution)/shard_map/ppermute | solution.py:272
  238.1 8.2 %collective-permute-done.28 = bf16[192,512]{1,0:T(8,128)(2,1)S(1)} collective-permute-done((bf16[192,512]{1,0:T(8,128)(2,1)}, bf16[192,512]{1,0:T(8,128)(2,1)S(1)}, u32[]{:S(2)}, u32[]{:S(2)}) %collective-permute-start.28) | collective-permute-done | bytes 196640 | tf_op jit(solution)/shard_map/ppermute | solution.py:276
  246.3 3.2 fusion.67
  252.3 2.1 constant_dynamic-slice_fusion.11
  254.3 10.3 %units.1 = (bf16[512,3072]{1,0:T(8,128)(2,1)S(1)}, bf16[512,3072]{1,0:T(8,128)(2,1)S(1)}, f32[512,768]{1,0:T(8,128)S(1)}) custom-call(bf16[512,768]{1,0:T(8,128)(2,1)S(1)} %fusion.15.x_ref, bf16[4,768,1536]{2,1,0:T(8,128)(2,1)} %bitcast.273, bf16[4,768,1536]{2,1,0:T(8,128)(2,1)} %bitcast.274, f32[1,3072]{1,0:T(1,128)S(1)} %bitcast.272), custom_call_target="tpu_custom_call" | custom-call | tf_op jit(solution)/shard_map/units/pallas_call | solution.py:206
  268.3 3.0 fusion.9
  276.1 8.8 %units_back.1 = (bf16[512,3072]{1,0:T(8,128)(2,1)S(1)}, f32[1,3072]{1,0:T(1,128)S(1)}, f32[512,768]{1,0:T(8,128)S(1)}) custom-call(bf16[512,768]{1,0:T(8,128)(2,1)S(1)} %get-tuple-element.167.g_ref, bf16[4,768,1536]{2,1,0:T(8,128)(2,1)} %bitcast.275, bf16[4,768,1536]{2,1,0:T(8,128)(2,1)} %bitcast.276, bf16[512,3072]{1,0:T(8,128)(2,1)S(1)} %copy-done.1), custom_call_target="tpu_custom_call" | custom-call | tf_op jit(solution)/shard_map/units_back/pallas_call | solution.py:247
  284.9 2.8 convolution_convert_fusion
  287.7 2.8 convolution_convert_fusion.1
  291.9 2.5 multiply_reduce_fusion
  295.0 2.7 convolution_convert_fusion.12
  298.7 2.3 collective-permute-start.31
  301.1 2.8 convolution_convert_fusion.2
  303.9 2.8 convolution_convert_fusion.3
  306.8 6.8 %collective-permute-done.32 = bf16[192,512]{1,0:T(8,128)(2,1)S(1)} collective-permute-done((bf16[192,512]{1,0:T(8,128)(2,1)S(1)}, bf16[192,512]{1,0:T(8,128)(2,1)S(1)}, u32[]{:S(2)}, u32[]{:S(2)}) %collective-permute-start.32) | collective-permute-done | bytes 196640 | tf_op jit(solution)/shard_map/ppermute | solution.py:276
  314.2 7.4 %collective-permute-start.35 = (bf16[512,768]{1,0:T(8,128)(2,1)}, bf16[512,768]{1,0:T(8,128)(2,1)}, u32[]{:S(2)}, u32[]{:S(2)}) collective-permute-start(bf16[512,768]{1,0:T(8,128)(2,1)} %get-tuple-element.181), channel_id=1, source_target_pairs={{0,0},{1,1},{2,4},{3,5},{4,2},{5,3},{6,6},{7,7},{8,8},{9,9},{10,12... | collective-permute-start | bytes 2359304 | tf_op jit(solution)/shard_map/ppermute | solution.py:272
  322.9 3.6 convolution_convert_fusion.7
  326.6 19.2 %attend_back.2 = (bf16[192,2048]{1,0:T(8,128)(2,1)S(1)}, bf16[384,1024]{1,0:T(8,128)(2,1)S(1)}) custom-call(s32[4]{0:T(128)S(1)} %broadcast_11_counts_ref.2.counts_ref, bf16[192,2048]{1,0:T(8,128)(2,1)S(1)} %constant_dynamic-update-slice_fusion.12.q_ref, bf16[192,2048]{1,0:T(8,128)(2,1)S(1)} %constant_dynamic-update-slice_fusion.6.g_ref, ...), custom_call_target="tpu_custom_call" | custom-call | flops 16106127360 | bytes 6291456 | tf_op jit(solution)/shard_map/attend_back/pallas_call | solution.py:123
  345.8 2.2 convolution_convert_fusion.6
  349.8 2.7 fusion.17
  352.5 2.7 add_convert_fusion.1
  358.0 4.0 add_convert_fusion
  370.4 3.5 multiply_reduce_fusion.1
  376.0 2.1 convolution_convert_fusion.11
  380.2 2.1 pad_maximum_fusion
  385.7 4.4 collective-permute-done.41
  394.2 5.8 copy.99
  405.6 27.9 %attend_back.3 = (bf16[192,2048]{1,0:T(8,128)(2,1)S(1)}, bf16[384,2048]{1,0:T(8,128)(2,1)}) custom-call(s32[8]{0:T(128)S(1)} %convert_reduce_fusion.8.counts_ref, bf16[192,2048]{1,0:T(8,128)(2,1)S(1)} %copy-done.6, bf16[192,2048]{1,0:T(8,128)(2,1)S(1)} %constant_dynamic-update-slice_fusion.g_ref, bf16[192,2048]{1,0:T(8,128)(2,1)S(1)} %get-tuple-element.78.o_ref, ...), custom_call_target="tpu_custom_call" | custom-call | flops 32212254720 | bytes 6291456 | tf_op jit(solution)/shard_map/attend_back/pallas_call | solution.py:123
  433.5 2.0 fusion.32
  444.7 2.9 constant_dynamic-update-slice_fusion.18
  447.6 6.2 %convolution_convert_fusion.4 = bf16[2048,768]{1,0:T(8,128)(2,1)} fusion(bf16[576,2048]{1,0:T(8,128)(2,1)} %constant_dynamic-update-slice_fusion.18, bf16[768,576]{1,0:T(8,128)(2,1)S(1)} %copy-done.49), kind=kOutput, calls=%fused_computation.6 | convolution fusion | flops 1813512192 | bytes 6389760 | tf_op jit(solution)/shard_map/dot_general | solution.py:155
  453.8 3.0 convolution_convert_fusion.10
  471.2 2.4 collective-permute-start.68
  475.4 2.6 collective-permute-done.55
  477.9 3.0 collective-permute-start.62
  488.6 8.9 %collective-permute-done.62 = bf16[96,1536]{1,0:T(8,128)(2,1)} collective-permute-done((bf16[96,1536]{1,0:T(8,128)(2,1)}, bf16[96,1536]{1,0:T(8,128)(2,1)}, u32[]{:S(2)}, u32[]{:S(2)}) %collective-permute-start.62) | collective-permute-done | bytes 294944 | tf_op jit(solution)/shard_map/ppermute | solution.py:368
  500.1 10.5 %collective-permute-start.56 = (bf16[96,960]{1,0:T(8,128)(2,1)S(1)}, bf16[96,960]{1,0:T(8,128)(2,1)S(1)}, u32[]{:S(2)}, u32[]{:S(2)}) collective-permute-start(bf16[96,960]{1,0:T(8,128)(2,1)S(1)} %dynamic-slice_bitcast_fusion.4), channel_id=1, source_target_pairs={{0,2},{1,3},{2,0},{3,1},{4,6},{5,7},{6,4},{7,5},{8,10},{9,11},{10,... | collective-permute-start | bytes 552968 | tf_op jit(solution)/shard_map/ppermute | solution.py:446
  512.0 3.0 collective-permute-start.50
  515.9 4.7 collective-permute-done.56
  523.0 12.3 %collective-permute-done.50 = bf16[512,768]{1,0:T(8,128)(2,1)S(1)} collective-permute-done((bf16[512,768]{1,0:T(8,128)(2,1)S(1)}, bf16[512,768]{1,0:T(8,128)(2,1)S(1)}, u32[]{:S(2)}, u32[]{:S(2)}) %collective-permute-start.50) | collective-permute-done | bytes 786464 | tf_op jit(solution)/shard_map/ppermute | solution.py:276
  542.3 6.7 %collective-permute-start.59 = (bf16[96,576]{1,0:T(8,128)(2,1)S(1)}, bf16[96,576]{1,0:T(8,128)(2,1)S(1)}, u32[]{:S(2)}, u32[]{:S(2)}) collective-permute-start(bf16[96,576]{1,0:T(8,128)(2,1)S(1)} %get-tuple-element.219), channel_id=1, source_target_pairs={{0,2},{1,3},{2,0},{3,1},{4,6},{5,7},{6,4},{7,5},{8,10},{9,11},{10,... | collective-permute-start | bytes 331784 | tf_op jit(solution)/shard_map/ppermute | solution.py:368
  550.7 8.4 %collective-permute-done.58 = bf16[96,576]{1,0:T(8,128)(2,1)S(1)} collective-permute-done((bf16[96,576]{1,0:T(8,128)(2,1)S(1)}, bf16[96,576]{1,0:T(8,128)(2,1)S(1)}, u32[]{:S(2)}, u32[]{:S(2)}) %collective-permute-start.58) | collective-permute-done | bytes 110624 | tf_op jit(solution)/shard_map/ppermute | solution.py:368
  559.1 10.4 %collective-permute-done.59 = bf16[96,576]{1,0:T(8,128)(2,1)S(1)} collective-permute-done((bf16[96,576]{1,0:T(8,128)(2,1)S(1)}, bf16[96,576]{1,0:T(8,128)(2,1)S(1)}, u32[]{:S(2)}, u32[]{:S(2)}) %collective-permute-start.59) | collective-permute-done | bytes 110624 | tf_op jit(solution)/shard_map/ppermute | solution.py:368
  572.6 2.1 copy.149
  (485 shorter events, 148.0 us)
Async XLA Ops:
  7.2 247.1 %all-gather.2.cloned.1.call-start = ((), (), s32[]{:S(2)}) async-start(), calls=%async_computation.1 | async-start | bytes 9732096 | tf_op jit(solution)/shard_map/all_gather | solution.py:484
  10.1 528.9 %reduce-scatter.4.cloned.1.call-start = ((), (), s32[]{:S(2)}) async-start(), calls=%async_computation.2 | async-start | bytes 3981312
  11.0 62.2 %collective-permute-start.8 = (bf16[512,768]{1,0:T(8,128)(2,1)S(1)}, bf16[512,768]{1,0:T(8,128)(2,1)S(1)}, u32[]{:S(2)}, u32[]{:S(2)}) collective-permute-start(bf16[512,768]{1,0:T(8,128)(2,1)S(1)} %collective-permute-done.7), channel_id=1, source_target_pairs={{0,1},{1,0},{4,5},{5,4},{2,3},{3,2},{6,7},{7,6},{8,9},{9,8},{12,13... | collective-permute-start | bytes 2359304 | tf_op jit(solution)/shard_map/ppermute | solution.py:276
  15.0 57.5 %collective-permute-start.1 = (bf16[96,576]{1,0:T(8,128)(2,1)S(1)}, bf16[96,576]{1,0:T(8,128)(2,1)S(1)}, u32[]{:S(2)}, u32[]{:S(2)}) collective-permute-start(bf16[96,576]{1,0:T(8,128)(2,1)S(1)} %get-tuple-element.176), channel_id=1, source_target_pairs={{0,1},{1,2},{2,3},{3,0},{4,5},{5,6},{6,7},{7,4},{8,9},{9,10},{10,1... | collective-permute-start | bytes 331784 | tf_op jit(solution)/shard_map/ppermute | solution.py:354
  15.2 57.3 %collective-permute-start.2 = (bf16[96,576]{1,0:T(8,128)(2,1)S(1)}, bf16[96,576]{1,0:T(8,128)(2,1)S(1)}, u32[]{:S(2)}, u32[]{:S(2)}) collective-permute-start(bf16[96,576]{1,0:T(8,128)(2,1)S(1)} %get-tuple-element.176), channel_id=1, source_target_pairs={{0,2},{1,3},{2,0},{3,1},{4,6},{5,7},{6,4},{7,5},{8,10},{9,11},{10,... | collective-permute-start | bytes 331784 | tf_op jit(solution)/shard_map/ppermute | solution.py:354
  46.0 27.6 %collective-permute-start.3 = (bf16[96,576]{1,0:T(8,128)(2,1)S(1)}, bf16[96,576]{1,0:T(8,128)(2,1)S(1)}, u32[]{:S(2)}, u32[]{:S(2)}) collective-permute-start(bf16[96,576]{1,0:T(8,128)(2,1)S(1)} %get-tuple-element.176), channel_id=1, source_target_pairs={{0,3},{1,0},{2,1},{3,2},{4,7},{5,4},{6,5},{7,6},{8,11},{9,8},{10,9... | collective-permute-start | bytes 331784 | tf_op jit(solution)/shard_map/ppermute | solution.py:354
  48.5 50.1 %collective-permute-start = (s32[8]{0:T(128)S(1)}, s32[8]{0:T(128)}, u32[]{:S(2)}, u32[]{:S(2)}) collective-permute-start(s32[8]{0:T(128)S(1)} %bitcast.317), channel_id=1, source_target_pairs={{0,4},{4,0},{1,5},{5,1},{2,6},{6,2},{3,7},{7,3},{8,12},{12,8},{9,1... | collective-permute-start | bytes 104 | tf_op jit(solution)/shard_map/ppermute | solution.py:288
  73.5 35.7 %collective-permute-start.9 = (bf16[2,512,768]{2,1,0:T(8,128)(2,1)S(1)}, bf16[2,512,768]{2,1,0:T(8,128)(2,1)S(1)}, u32[]{:S(2)}, u32[]{:S(2)}) collective-permute-start(bf16[2,512,768]{2,1,0:T(8,128)(2,1)S(1)} %broadcast_select_fusion.1), channel_id=1, source_target_pairs={{0,4},{1,5},{4,0},{5,1},{2,6},{3,7},{6,2},{7,3},{8,12},{9,13},{12,... | collective-permute-start | bytes 4718600 | tf_op jit(solution)/shard_map/ppermute | solution.py:276
  74.4 5.2 collective-permute-start.4
  81.3 14.0 %collective-permute-start.5 = (bf16[2,96,576]{2,1,0:T(8,128)(2,1)S(1)}, bf16[2,96,576]{2,1,0:T(8,128)(2,1)}, u32[]{:S(2)}, u32[]{:S(2)}) collective-permute-start(bf16[2,96,576]{2,1,0:T(8,128)(2,1)S(1)} %broadcast_select_fusion.5), channel_id=1, source_target_pairs={{0,8},{8,0},{1,9},{9,1},{2,10},{10,2},{3,11},{11,3},{4,12},{12,4},... | collective-permute-start | bytes 663560 | tf_op jit(solution)/shard_map/ppermute | solution.py:288
  96.4 12.6 %collective-permute-start.6 = (bf16[2,2,96,576]{3,2,1,0:T(8,128)(2,1)S(1)}, bf16[2,2,96,576]{3,2,1,0:T(8,128)(2,1)S(1)}, u32[]{:S(2)}, u32[]{:S(2)}) collective-permute-start(bf16[2,2,96,576]{3,2,1,0:T(8,128)(2,1)S(1)} %broadcast_select_fusion.4), channel_id=1, source_target_pairs={{0,16},{16,0},{1,17},{17,1},{2,18},{18,2},{3,19},{19,3},{4,20},{20... | collective-permute-start | bytes 1327112 | tf_op jit(solution)/shard_map/ppermute | solution.py:288
  110.4 9.6 %collective-permute-start.10 = (bf16[96,960]{1,0:T(8,128)(2,1)S(1)}, bf16[96,960]{1,0:T(8,128)(2,1)S(1)}, u32[]{:S(2)}, u32[]{:S(2)}) collective-permute-start(bf16[96,960]{1,0:T(8,128)(2,1)S(1)} %copy-done.50), channel_id=1, source_target_pairs={{0,1},{1,2},{2,3},{3,0},{4,5},{5,6},{6,7},{7,4},{8,9},{9,10},{10,1... | collective-permute-start | bytes 552968 | tf_op jit(solution)/shard_map/ppermute | solution.py:354
  112.3 13.9 %collective-permute-start.11 = (bf16[96,960]{1,0:T(8,128)(2,1)S(1)}, bf16[96,960]{1,0:T(8,128)(2,1)S(1)}, u32[]{:S(2)}, u32[]{:S(2)}) collective-permute-start(bf16[96,960]{1,0:T(8,128)(2,1)S(1)} %copy-done.50), channel_id=1, source_target_pairs={{0,2},{1,3},{2,0},{3,1},{4,6},{5,7},{6,4},{7,5},{8,10},{9,11},{10,... | collective-permute-start | bytes 552968 | tf_op jit(solution)/shard_map/ppermute | solution.py:354
  113.5 12.6 %collective-permute-start.12 = (bf16[96,960]{1,0:T(8,128)(2,1)S(1)}, bf16[96,960]{1,0:T(8,128)(2,1)S(1)}, u32[]{:S(2)}, u32[]{:S(2)}) collective-permute-start(bf16[96,960]{1,0:T(8,128)(2,1)S(1)} %copy-done.50), channel_id=1, source_target_pairs={{0,3},{1,0},{2,1},{3,2},{4,7},{5,4},{6,5},{7,6},{8,11},{9,8},{10,9... | collective-permute-start | bytes 552968 | tf_op jit(solution)/shard_map/ppermute | solution.py:354
  114.6 14.9 %collective-permute-start.16 = (bf16[256,768]{1,0:T(8,128)(2,1)}, bf16[256,768]{1,0:T(8,128)(2,1)S(1)}, u32[]{:S(2)}, u32[]{:S(2)}) collective-permute-start(bf16[256,768]{1,0:T(8,128)(2,1)} %bitcast.12), channel_id=1, source_target_pairs={{0,0},{1,1},{2,4},{3,5},{4,2},{5,3},{6,6},{7,7},{8,8},{9,9},{10,12... | collective-permute-start | bytes 1179656 | tf_op jit(solution)/shard_map/ppermute | solution.py:272
  129.5 17.9 %collective-permute-start.17 = (bf16[256,768]{1,0:T(8,128)(2,1)S(1)}, bf16[256,768]{1,0:T(8,128)(2,1)S(1)}, u32[]{:S(2)}, u32[]{:S(2)}) collective-permute-start(bf16[256,768]{1,0:T(8,128)(2,1)S(1)} %collective-permute-done.16), channel_id=1, source_target_pairs={{0,1},{1,0},{4,5},{5,4},{2,3},{3,2},{6,7},{7,6},{8,9},{9,8},{12,13... | collective-permute-start | bytes 1179656 | tf_op jit(solution)/shard_map/ppermute | solution.py:276
  138.5 15.5 %collective-permute-start.14 = (bf16[96,3072]{1,0:T(8,128)(2,1)S(1)}, bf16[96,3072]{1,0:T(8,128)(2,1)S(1)}, u32[]{:S(2)}, u32[]{:S(2)}) collective-permute-start(bf16[96,3072]{1,0:T(8,128)(2,1)S(1)} %pad_maximum_fusion.2), channel_id=1, source_target_pairs={{0,8},{8,0},{1,9},{9,1},{2,10},{10,2},{3,11},{11,3},{4,12},{12,4},... | collective-permute-start | bytes 1769480 | tf_op jit(solution)/shard_map/ppermute | solution.py:288
  147.6 34.7 %collective-permute-start.18 = (bf16[2,256,768]{2,1,0:T(8,128)(2,1)S(1)}, bf16[2,256,768]{2,1,0:T(8,128)(2,1)S(1)}, u32[]{:S(2)}, u32[]{:S(2)}) collective-permute-start(bf16[2,256,768]{2,1,0:T(8,128)(2,1)S(1)} %broadcast_select_fusion.3), channel_id=1, source_target_pairs={{0,4},{1,5},{4,0},{5,1},{2,6},{3,7},{6,2},{7,3},{8,12},{9,13},{12,... | collective-permute-start | bytes 2359304 | tf_op jit(solution)/shard_map/ppermute | solution.py:276
  154.2 29.6 %collective-permute-start.15 = (bf16[2,96,3072]{2,1,0:T(8,128)(2,1)S(1)}, bf16[2,96,3072]{2,1,0:T(8,128)(2,1)S(1)}, u32[]{:S(2)}, u32[]{:S(2)}) collective-permute-start(bf16[2,96,3072]{2,1,0:T(8,128)(2,1)S(1)} %broadcast_select_fusion.2), channel_id=1, source_target_pairs={{0,16},{16,0},{1,17},{17,1},{2,18},{18,2},{3,19},{19,3},{4,20},{20... | collective-permute-start | bytes 3538952 | tf_op jit(solution)/shard_map/ppermute | solution.py:288
  185.5 12.1 %collective-permute-start.19 = (bf16[2,2,96,2304]{3,2,1,0:T(8,128)(2,1)}, bf16[2,2,96,2304]{3,2,1,0:T(8,128)(2,1)}, u32[]{:S(2)}, u32[]{:S(2)}) collective-permute-start(bf16[2,2,96,2304]{3,2,1,0:T(8,128)(2,1)} %slice.186), channel_id=1, source_target_pairs={{0,4},{4,0},{1,5},{5,1},{2,6},{6,2},{3,7},{7,3},{8,12},{12,8},{9,1... | collective-permute-start | bytes 5308424 | tf_op jit(solution)/shard_map/ppermute | solution.py:288
  186.4 7.8 %collective-permute-start.21 = (bf16[192,512]{1,0:T(8,128)(2,1)S(1)}, bf16[192,512]{1,0:T(8,128)(2,1)S(1)}, u32[]{:S(2)}, u32[]{:S(2)}) collective-permute-start(bf16[192,512]{1,0:T(8,128)(2,1)S(1)} %get-tuple-element.210), channel_id=1, source_target_pairs={{0,1},{1,0},{4,5},{5,4},{2,3},{3,2},{6,7},{7,6},{8,9},{9,8},{12,13... | collective-permute-start | bytes 589832 | tf_op jit(solution)/shard_map/ppermute | solution.py:276
  186.6 10.0 %collective-permute-start.22 = (bf16[192,512]{1,0:T(8,128)(2,1)S(1)}, bf16[192,512]{1,0:T(8,128)(2,1)S(1)}, u32[]{:S(2)}, u32[]{:S(2)}) collective-permute-start(bf16[192,512]{1,0:T(8,128)(2,1)S(1)} %get-tuple-element.209), channel_id=1, source_target_pairs={{0,5},{1,4},{4,1},{5,0},{2,7},{3,6},{6,3},{7,2},{8,13},{9,12},{12,... | collective-permute-start | bytes 589832 | tf_op jit(solution)/shard_map/ppermute | solution.py:276
  204.0 7.8 %collective-permute-start.24 = (bf16[192,512]{1,0:T(8,128)(2,1)S(1)}, bf16[192,512]{1,0:T(8,128)(2,1)S(1)}, u32[]{:S(2)}, u32[]{:S(2)}) collective-permute-start(bf16[192,512]{1,0:T(8,128)(2,1)S(1)} %get-tuple-element.206), channel_id=1, source_target_pairs={{0,1},{1,0},{4,5},{5,4},{2,3},{3,2},{6,7},{7,6},{8,9},{9,8},{12,13... | collective-permute-start | bytes 589832 | tf_op jit(solution)/shard_map/ppermute | solution.py:276
  204.9 9.3 %collective-permute-start.25 = (bf16[192,512]{1,0:T(8,128)(2,1)S(1)}, bf16[192,512]{1,0:T(8,128)(2,1)S(1)}, u32[]{:S(2)}, u32[]{:S(2)}) collective-permute-start(bf16[192,512]{1,0:T(8,128)(2,1)S(1)} %get-tuple-element.205), channel_id=1, source_target_pairs={{0,5},{1,4},{4,1},{5,0},{2,7},{3,6},{6,3},{7,2},{8,13},{9,12},{12,... | collective-permute-start | bytes 589832 | tf_op jit(solution)/shard_map/ppermute | solution.py:276
  228.6 8.5 %collective-permute-start.26 = (bf16[192,512]{1,0:T(8,128)(2,1)}, bf16[192,512]{1,0:T(8,128)(2,1)}, u32[]{:S(2)}, u32[]{:S(2)}) collective-permute-start(bf16[192,512]{1,0:T(8,128)(2,1)} %get-tuple-element.203), channel_id=1, source_target_pairs={{0,4},{1,5},{4,0},{5,1},{2,6},{3,7},{6,2},{7,3},{8,12},{9,13},{12,... | collective-permute-start | bytes 589832 | tf_op jit(solution)/shard_map/ppermute | solution.py:276
  229.3 8.8 %collective-permute-start.27 = (bf16[192,512]{1,0:T(8,128)(2,1)}, bf16[192,512]{1,0:T(8,128)(2,1)S(1)}, u32[]{:S(2)}, u32[]{:S(2)}) collective-permute-start(bf16[192,512]{1,0:T(8,128)(2,1)} %get-tuple-element.202), channel_id=1, source_target_pairs={{0,1},{1,0},{4,5},{5,4},{2,3},{3,2},{6,7},{7,6},{8,9},{9,8},{12,13... | collective-permute-start | bytes 589832 | tf_op jit(solution)/shard_map/ppermute | solution.py:276
  229.6 38.7 %collective-permute-start.29 = (bf16[512,768]{1,0:T(8,128)(2,1)}, bf16[512,768]{1,0:T(8,128)(2,1)}, u32[]{:S(2)}, u32[]{:S(2)}) collective-permute-start(bf16[512,768]{1,0:T(8,128)(2,1)} %bitcast.46), channel_id=1, source_target_pairs={{0,0},{1,1},{2,4},{3,5},{4,2},{5,3},{6,6},{7,7},{8,8},{9,9},{10,12... | collective-permute-start | bytes 2359304 | tf_op jit(solution)/shard_map/ppermute | solution.py:272
  237.1 9.2 %collective-permute-start.28 = (bf16[192,512]{1,0:T(8,128)(2,1)}, bf16[192,512]{1,0:T(8,128)(2,1)S(1)}, u32[]{:S(2)}, u32[]{:S(2)}) collective-permute-start(bf16[192,512]{1,0:T(8,128)(2,1)} %get-tuple-element.201), channel_id=1, source_target_pairs={{0,5},{1,4},{4,1},{5,0},{2,7},{3,6},{6,3},{7,2},{8,13},{9,12},{12,... | collective-permute-start | bytes 589832 | tf_op jit(solution)/shard_map/ppermute | solution.py:276
  297.9 8.9 %collective-permute-start.30 = (bf16[192,512]{1,0:T(8,128)(2,1)S(1)}, bf16[192,512]{1,0:T(8,128)(2,1)S(1)}, u32[]{:S(2)}, u32[]{:S(2)}) collective-permute-start(bf16[192,512]{1,0:T(8,128)(2,1)S(1)} %get-tuple-element.199), channel_id=1, source_target_pairs={{0,4},{1,5},{4,0},{5,1},{2,6},{3,7},{6,2},{7,3},{8,12},{9,13},{12,... | collective-permute-start | bytes 589832 | tf_op jit(solution)/shard_map/ppermute | solution.py:276
  298.7 8.1 %collective-permute-start.31 = (bf16[192,512]{1,0:T(8,128)(2,1)S(1)}, bf16[192,512]{1,0:T(8,128)(2,1)S(1)}, u32[]{:S(2)}, u32[]{:S(2)}) collective-permute-start(bf16[192,512]{1,0:T(8,128)(2,1)S(1)} %get-tuple-element.198), channel_id=1, source_target_pairs={{0,1},{1,0},{4,5},{5,4},{2,3},{3,2},{6,7},{7,6},{8,9},{9,8},{12,13... | collective-permute-start | bytes 589832 | tf_op jit(solution)/shard_map/ppermute | solution.py:276
  306.7 6.9 %collective-permute-start.32 = (bf16[192,512]{1,0:T(8,128)(2,1)S(1)}, bf16[192,512]{1,0:T(8,128)(2,1)S(1)}, u32[]{:S(2)}, u32[]{:S(2)}) collective-permute-start(bf16[192,512]{1,0:T(8,128)(2,1)S(1)} %get-tuple-element.197), channel_id=1, source_target_pairs={{0,5},{1,4},{4,1},{5,0},{2,7},{3,6},{6,3},{7,2},{8,13},{9,12},{12,... | collective-permute-start | bytes 589832 | tf_op jit(solution)/shard_map/ppermute | solution.py:276
  313.6 32.2 %collective-permute-start.33 = (bf16[384,3072]{1,0:T(8,128)(2,1)}, bf16[384,3072]{1,0:T(8,128)(2,1)}, u32[]{:S(2)}, u32[]{:S(2)}) collective-permute-start(bf16[384,3072]{1,0:T(8,128)(2,1)} %convolution_convert_fusion.2), channel_id=1, source_target_pairs={{0,4},{4,0},{1,5},{5,1},{2,6},{6,2},{3,7},{7,3},{8,12},{12,8},{9,1... | collective-permute-start | bytes 7077896 | tf_op jit(solution)/shard_map/ppermute | solution.py:288
  313.9 31.9 %collective-permute-start.34 = (bf16[384,3072]{1,0:T(8,128)(2,1)}, bf16[384,3072]{1,0:T(8,128)(2,1)}, u32[]{:S(2)}, u32[]{:S(2)}) collective-permute-start(bf16[384,3072]{1,0:T(8,128)(2,1)} %convolution_convert_fusion), channel_id=1, source_target_pairs={{0,4},{4,0},{1,5},{5,1},{2,6},{6,2},{3,7},{7,3},{8,12},{12,8},{9,1... | collective-permute-start | bytes 7077896 | tf_op jit(solution)/shard_map/ppermute | solution.py:288
  314.2 31.6 %collective-permute-start.35 = (bf16[512,768]{1,0:T(8,128)(2,1)}, bf16[512,768]{1,0:T(8,128)(2,1)}, u32[]{:S(2)}, u32[]{:S(2)}) collective-permute-start(bf16[512,768]{1,0:T(8,128)(2,1)} %get-tuple-element.181), channel_id=1, source_target_pairs={{0,0},{1,1},{2,4},{3,5},{4,2},{5,3},{6,6},{7,7},{8,8},{9,9},{10,12... | collective-permute-start | bytes 2359304 | tf_op jit(solution)/shard_map/ppermute | solution.py:272
  356.1 9.7 %collective-permute-start.36 = (bf16[192,512]{1,0:T(8,128)(2,1)}, bf16[192,512]{1,0:T(8,128)(2,1)}, u32[]{:S(2)}, u32[]{:S(2)}) collective-permute-start(bf16[192,512]{1,0:T(8,128)(2,1)} %get-tuple-element.191), channel_id=1, source_target_pairs={{0,4},{1,5},{4,0},{5,1},{2,6},{3,7},{6,2},{7,3},{8,12},{9,13},{12,... | collective-permute-start | bytes 589832 | tf_op jit(solution)/shard_map/ppermute | solution.py:276
  356.1 12.3 %collective-permute-start.37 = (bf16[192,512]{1,0:T(8,128)(2,1)}, bf16[192,512]{1,0:T(8,128)(2,1)}, u32[]{:S(2)}, u32[]{:S(2)}) collective-permute-start(bf16[192,512]{1,0:T(8,128)(2,1)} %get-tuple-element.190), channel_id=1, source_target_pairs={{0,1},{1,0},{4,5},{5,4},{2,3},{3,2},{6,7},{7,6},{8,9},{9,8},{12,13... | collective-permute-start | bytes 589832 | tf_op jit(solution)/shard_map/ppermute | solution.py:276
  356.1 13.3 %collective-permute-start.38 = (bf16[192,512]{1,0:T(8,128)(2,1)}, bf16[192,512]{1,0:T(8,128)(2,1)}, u32[]{:S(2)}, u32[]{:S(2)}) collective-permute-start(bf16[192,512]{1,0:T(8,128)(2,1)} %get-tuple-element.189), channel_id=1, source_target_pairs={{0,5},{1,4},{4,1},{5,0},{2,7},{3,6},{6,3},{7,2},{8,13},{9,12},{12,... | collective-permute-start | bytes 589832 | tf_op jit(solution)/shard_map/ppermute | solution.py:276
  362.0 28.5 %collective-permute-start.43 = (bf16[2,96,3072]{2,1,0:T(8,128)(2,1)}, bf16[2,96,3072]{2,1,0:T(8,128)(2,1)}, u32[]{:S(2)}, u32[]{:S(2)}) collective-permute-start(bf16[2,96,3072]{2,1,0:T(8,128)(2,1)} %get-tuple-element.178), channel_id=1, source_target_pairs={{0,16},{16,0},{1,17},{17,1},{2,18},{18,2},{3,19},{19,3},{4,20},{20... | collective-permute-start | bytes 3538952 | tf_op jit(solution)/shard_map/ppermute | solution.py:288
  363.3 29.2 %collective-permute-start.42 = (bf16[2,96,3072]{2,1,0:T(8,128)(2,1)}, bf16[2,96,3072]{2,1,0:T(8,128)(2,1)}, u32[]{:S(2)}, u32[]{:S(2)}) collective-permute-start(bf16[2,96,3072]{2,1,0:T(8,128)(2,1)} %fusion.17), channel_id=1, source_target_pairs={{0,8},{8,0},{1,9},{9,1},{2,10},{10,2},{3,11},{11,3},{4,12},{12,4},... | collective-permute-start | bytes 3538952 | tf_op jit(solution)/shard_map/ppermute | solution.py:288
  365.9 69.7 %collective-permute-start.46 = (bf16[2,192,384]{2,1,0:T(8,128)(2,1)S(1)}, bf16[2,192,384]{2,1,0:T(8,128)(2,1)}, u32[]{:S(2)}, u32[]{:S(2)}) collective-permute-start(bf16[2,192,384]{2,1,0:T(8,128)(2,1)S(1)} %dynamic-slice_bitcast_fusion.3), channel_id=1, source_target_pairs={{0,8},{8,0},{1,9},{9,1},{2,10},{10,2},{3,11},{11,3},{4,12},{12,4},... | collective-permute-start | bytes 884744 | tf_op jit(solution)/shard_map/ppermute | solution.py:288
  378.3 4.7 collective-permute-start.39
  378.4 7.3 %collective-permute-start.40 = (bf16[192,512]{1,0:T(8,128)(2,1)S(1)}, bf16[192,512]{1,0:T(8,128)(2,1)S(1)}, u32[]{:S(2)}, u32[]{:S(2)}) collective-permute-start(bf16[192,512]{1,0:T(8,128)(2,1)S(1)} %get-tuple-element.186), channel_id=1, source_target_pairs={{0,1},{1,0},{4,5},{5,4},{2,3},{3,2},{6,7},{7,6},{8,9},{9,8},{12,13... | collective-permute-start | bytes 589832 | tf_op jit(solution)/shard_map/ppermute | solution.py:276
  382.9 7.2 %collective-permute-start.41 = (bf16[192,512]{1,0:T(8,128)(2,1)S(1)}, bf16[192,512]{1,0:T(8,128)(2,1)S(1)}, u32[]{:S(2)}, u32[]{:S(2)}) collective-permute-start(bf16[192,512]{1,0:T(8,128)(2,1)S(1)} %get-tuple-element.185), channel_id=1, source_target_pairs={{0,5},{1,4},{4,1},{5,0},{2,7},{3,6},{6,3},{7,2},{8,13},{9,12},{12,... | collective-permute-start | bytes 589832 | tf_op jit(solution)/shard_map/ppermute | solution.py:276
  393.4 10.6 %collective-permute-start.47 = (bf16[2,256,768]{2,1,0:T(8,128)(2,1)}, bf16[2,256,768]{2,1,0:T(8,128)(2,1)}, u32[]{:S(2)}, u32[]{:S(2)}) collective-permute-start(bf16[2,256,768]{2,1,0:T(8,128)(2,1)} %dynamic-slice_bitcast_fusion.1), channel_id=1, source_target_pairs={{0,4},{1,5},{4,0},{5,1},{2,6},{3,7},{6,2},{7,3},{8,12},{9,13},{12,... | collective-permute-start | bytes 2359304 | tf_op jit(solution)/shard_map/ppermute | solution.py:276
  401.5 34.0 %collective-permute-start.45 = (bf16[96,3072]{1,0:T(8,128)(2,1)S(1)}, bf16[96,3072]{1,0:T(8,128)(2,1)S(1)}, u32[]{:S(2)}, u32[]{:S(2)}) collective-permute-start(bf16[96,3072]{1,0:T(8,128)(2,1)S(1)} %fusion.34), channel_id=1, source_target_pairs={{0,8},{8,0},{1,9},{9,1},{2,10},{10,2},{3,11},{11,3},{4,12},{12,4},... | collective-permute-start | bytes 1769480 | tf_op jit(solution)/shard_map/ppermute | solution.py:288
  403.5 32.0 %collective-permute-start.44 = (bf16[96,3072]{1,0:T(8,128)(2,1)S(1)}, bf16[96,3072]{1,0:T(8,128)(2,1)S(1)}, u32[]{:S(2)}, u32[]{:S(2)}) collective-permute-start(bf16[96,3072]{1,0:T(8,128)(2,1)S(1)} %fusion.33), channel_id=1, source_target_pairs={{0,16},{16,0},{1,17},{17,1},{2,18},{18,2},{3,19},{19,3},{4,20},{20... | collective-permute-start | bytes 1769480 | tf_op jit(solution)/shard_map/ppermute | solution.py:288
  405.2 28.2 %collective-permute-start.48 = (bf16[256,768]{1,0:T(8,128)(2,1)S(1)}, bf16[256,768]{1,0:T(8,128)(2,1)S(1)}, u32[]{:S(2)}, u32[]{:S(2)}) collective-permute-start(bf16[256,768]{1,0:T(8,128)(2,1)S(1)} %fusion.31), channel_id=1, source_target_pairs={{0,1},{1,0},{4,5},{5,4},{2,3},{3,2},{6,7},{7,6},{8,9},{9,8},{12,13... | collective-permute-start | bytes 1179656 | tf_op jit(solution)/shard_map/ppermute | solution.py:276
  438.7 21.3 %collective-permute-start.64 = (f32[17,768]{1,0:T(8,128)S(1)}, f32[17,768]{1,0:T(8,128)S(1)}, u32[]{:S(2)}, u32[]{:S(2)}) collective-permute-start(f32[17,768]{1,0:T(8,128)S(1)} %concatenate.39), channel_id=1, source_target_pairs={{0,16},{16,0},{1,17},{17,1},{2,18},{18,2},{3,19},{19,3},{4,20},{20... | collective-permute-start | bytes 156680 | tf_op jit(solution)/shard_map/ppermute | solution.py:288
  461.9 23.0 %collective-permute-start.53 = (bf16[2,192,576]{2,1,0:T(8,128)(2,1)}, bf16[2,192,576]{2,1,0:T(8,128)(2,1)}, u32[]{:S(2)}, u32[]{:S(2)}) collective-permute-start(bf16[2,192,576]{2,1,0:T(8,128)(2,1)} %dynamic-slice_bitcast_fusion.2), channel_id=1, source_target_pairs={{0,16},{16,0},{1,17},{17,1},{2,18},{18,2},{3,19},{19,3},{4,20},{20... | collective-permute-start | bytes 1327112 | tf_op jit(solution)/shard_map/ppermute | solution.py:288
  465.4 12.5 %collective-permute-start.55 = (bf16[192,384]{1,0:T(8,128)(2,1)S(1)}, bf16[192,384]{1,0:T(8,128)(2,1)S(1)}, u32[]{:S(2)}, u32[]{:S(2)}) collective-permute-start(bf16[192,384]{1,0:T(8,128)(2,1)S(1)} %fusion.45), channel_id=1, source_target_pairs={{0,16},{16,0},{1,17},{17,1},{2,18},{18,2},{3,19},{19,3},{4,20},{20... | collective-permute-start | bytes 442376 | tf_op jit(solution)/shard_map/ppermute | solution.py:288
  466.5 4.7 collective-permute-start.67
  469.8 40.8 %collective-permute-start.49 = (bf16[2,512,768]{2,1,0:T(8,128)(2,1)}, bf16[2,512,768]{2,1,0:T(8,128)(2,1)}, u32[]{:S(2)}, u32[]{:S(2)}) collective-permute-start(bf16[2,512,768]{2,1,0:T(8,128)(2,1)} %dynamic-slice_bitcast_fusion), channel_id=1, source_target_pairs={{0,4},{1,5},{4,0},{5,1},{2,6},{3,7},{6,2},{7,3},{8,12},{9,13},{12,... | collective-permute-start | bytes 4718600 | tf_op jit(solution)/shard_map/ppermute | solution.py:276
  471.2 9.7 %collective-permute-start.68 = (f32[17,768]{1,0:T(8,128)S(1)}, f32[17,768]{1,0:T(8,128)S(1)}, u32[]{:S(2)}, u32[]{:S(2)}) collective-permute-start(f32[17,768]{1,0:T(8,128)S(1)} %add.668), channel_id=1, source_target_pairs={{0,2},{1,3},{2,0},{3,1},{4,6},{5,7},{6,4},{7,5},{8,10},{9,11},{10,... | collective-permute-start | bytes 156680 | tf_op jit(solution)/shard_map/ppermute | solution.py:387
  474.5 13.0 %collective-permute-start.61 = (bf16[96,1536]{1,0:T(8,128)(2,1)}, bf16[96,1536]{1,0:T(8,128)(2,1)}, u32[]{:S(2)}, u32[]{:S(2)}) collective-permute-start(bf16[96,1536]{1,0:T(8,128)(2,1)} %get-tuple-element.182), channel_id=1, source_target_pairs={{0,1},{1,2},{2,3},{3,0},{4,5},{5,6},{6,7},{7,4},{8,9},{9,10},{10,1... | collective-permute-start | bytes 884744 | tf_op jit(solution)/shard_map/ppermute | solution.py:368
  477.9 19.6 %collective-permute-start.62 = (bf16[96,1536]{1,0:T(8,128)(2,1)}, bf16[96,1536]{1,0:T(8,128)(2,1)}, u32[]{:S(2)}, u32[]{:S(2)}) collective-permute-start(bf16[96,1536]{1,0:T(8,128)(2,1)} %get-tuple-element.184), channel_id=1, source_target_pairs={{0,2},{1,3},{2,0},{3,1},{4,6},{5,7},{6,4},{7,5},{8,10},{9,11},{10,... | collective-permute-start | bytes 884744 | tf_op jit(solution)/shard_map/ppermute | solution.py:368
  480.9 16.6 %collective-permute-start.63 = (bf16[96,1536]{1,0:T(8,128)(2,1)}, bf16[96,1536]{1,0:T(8,128)(2,1)}, u32[]{:S(2)}, u32[]{:S(2)}) collective-permute-start(bf16[96,1536]{1,0:T(8,128)(2,1)} %get-tuple-element.183), channel_id=1, source_target_pairs={{0,3},{1,0},{2,1},{3,2},{4,7},{5,4},{6,5},{7,6},{8,11},{9,8},{10,9... | collective-permute-start | bytes 884744 | tf_op jit(solution)/shard_map/ppermute | solution.py:368
  484.9 36.5 %collective-permute-start.52 = (bf16[256,768]{1,0:T(8,128)(2,1)}, bf16[256,768]{1,0:T(8,128)(2,1)S(1)}, u32[]{:S(2)}, u32[]{:S(2)}) collective-permute-start(bf16[256,768]{1,0:T(8,128)(2,1)} %fusion.32), channel_id=1, source_target_pairs={{0,0},{1,1},{2,4},{3,5},{4,2},{5,3},{6,6},{7,7},{8,8},{9,9},{10,12... | collective-permute-start | bytes 1179656 | tf_op jit(solution)/shard_map/ppermute | solution.py:272
  487.5 11.4 %collective-permute-start.54 = (bf16[192,576]{1,0:T(8,128)(2,1)S(1)}, bf16[192,576]{1,0:T(8,128)(2,1)S(1)}, u32[]{:S(2)}, u32[]{:S(2)}) collective-permute-start(bf16[192,576]{1,0:T(8,128)(2,1)S(1)} %fusion.37), channel_id=1, source_target_pairs={{0,8},{8,0},{1,9},{9,1},{2,10},{10,2},{3,11},{11,3},{4,12},{12,4},... | collective-permute-start | bytes 663560 | tf_op jit(solution)/shard_map/ppermute | solution.py:288
  500.1 20.5 %collective-permute-start.56 = (bf16[96,960]{1,0:T(8,128)(2,1)S(1)}, bf16[96,960]{1,0:T(8,128)(2,1)S(1)}, u32[]{:S(2)}, u32[]{:S(2)}) collective-permute-start(bf16[96,960]{1,0:T(8,128)(2,1)S(1)} %dynamic-slice_bitcast_fusion.4), channel_id=1, source_target_pairs={{0,2},{1,3},{2,0},{3,1},{4,6},{5,7},{6,4},{7,5},{8,10},{9,11},{10,... | collective-permute-start | bytes 552968 | tf_op jit(solution)/shard_map/ppermute | solution.py:446
  512.0 23.3 %collective-permute-start.50 = (bf16[512,768]{1,0:T(8,128)(2,1)S(1)}, bf16[512,768]{1,0:T(8,128)(2,1)S(1)}, u32[]{:S(2)}, u32[]{:S(2)}) collective-permute-start(bf16[512,768]{1,0:T(8,128)(2,1)S(1)} %fusion.10), channel_id=1, source_target_pairs={{0,1},{1,0},{4,5},{5,4},{2,3},{3,2},{6,7},{7,6},{8,9},{9,8},{12,13... | collective-permute-start | bytes 2359304 | tf_op jit(solution)/shard_map/ppermute | solution.py:276
  536.9 12.6 %collective-permute-start.51 = (bf16[512,768]{1,0:T(8,128)(2,1)S(1)}, bf16[512,768]{1,0:T(8,128)(2,1)S(1)}, u32[]{:S(2)}, u32[]{:S(2)}) collective-permute-start(bf16[512,768]{1,0:T(8,128)(2,1)S(1)} %fusion.13), channel_id=1, source_target_pairs={{0,0},{1,1},{2,4},{3,5},{4,2},{5,3},{6,6},{7,7},{8,8},{9,9},{10,12... | collective-permute-start | bytes 2359304 | tf_op jit(solution)/shard_map/ppermute | solution.py:272
  542.1 17.0 %collective-permute-start.58 = (bf16[96,576]{1,0:T(8,128)(2,1)S(1)}, bf16[96,576]{1,0:T(8,128)(2,1)S(1)}, u32[]{:S(2)}, u32[]{:S(2)}) collective-permute-start(bf16[96,576]{1,0:T(8,128)(2,1)S(1)} %get-tuple-element.217), channel_id=1, source_target_pairs={{0,1},{1,2},{2,3},{3,0},{4,5},{5,6},{6,7},{7,4},{8,9},{9,10},{10,1... | collective-permute-start | bytes 331784 | tf_op jit(solution)/shard_map/ppermute | solution.py:368
  542.3 27.2 %collective-permute-start.59 = (bf16[96,576]{1,0:T(8,128)(2,1)S(1)}, bf16[96,576]{1,0:T(8,128)(2,1)S(1)}, u32[]{:S(2)}, u32[]{:S(2)}) collective-permute-start(bf16[96,576]{1,0:T(8,128)(2,1)S(1)} %get-tuple-element.219), channel_id=1, source_target_pairs={{0,2},{1,3},{2,0},{3,1},{4,6},{5,7},{6,4},{7,5},{8,10},{9,11},{10,... | collective-permute-start | bytes 331784 | tf_op jit(solution)/shard_map/ppermute | solution.py:368
  549.0 20.5 %collective-permute-start.60 = (bf16[96,576]{1,0:T(8,128)(2,1)S(1)}, bf16[96,576]{1,0:T(8,128)(2,1)S(1)}, u32[]{:S(2)}, u32[]{:S(2)}) collective-permute-start(bf16[96,576]{1,0:T(8,128)(2,1)S(1)} %get-tuple-element.218), channel_id=1, source_target_pairs={{0,3},{1,0},{2,1},{3,2},{4,7},{5,4},{6,5},{7,6},{8,11},{9,8},{10,9... | collective-permute-start | bytes 331784 | tf_op jit(solution)/shard_map/ppermute | solution.py:368
  (93 other events, 750.9 us)
Sparse Core Ops, SparseCore 0:
  11.5 100.5 all-gather.1
  400.1 48.1 reduce-scatter.3
